TPU v7x, 256 devices: a whole 4x4x8 slice. The times are simulated.
256 devices in a mesh: tm: 32 (over z, y), space: 8 (over x, core).
Axes of the slice: x: 4, y: 4, z: 8, core: 2. Of those that a mesh axis runs over, the one named last changes fastest.
Arguments:
- density: bfloat16 [8192, 256, 128], P('tm', 'space'), may hold values from -6 to 6
- active: int32 [8192], P('tm'), may hold values from 1 to 256
- neighbours: int32 [256, 8], P('space'), may hold values from 0 to 255, as said below
- near_blocks: bfloat16 [2, 256, 8, 128, 128], P(None, 'space'), may hold values from -0.125 to 0.125
- to_moments: bfloat16 [64, 256, 128], P(None, 'space'), may hold values from -0.03125 to 0.03125
- from_moments: bfloat16 [64, 256, 128], P(None, 'space'), may hold values from -0.75 to 0.75
- decay_rates: float32 [64], replicated, may hold values from 2.4414063e-05 to 0.05, as said below
- lengths: float32 [8192], P('tm'), may hold values from 0.5 to 4096, as said below
Outputs:
- potential: bfloat16 [8192, 256, 128], P('tm', 'space')
Inputs may be any that keep to these rules, and one draw needn't show every extreme that they name: `neighbours`: every entry of row c lies within 8 of c; each row names c - 8 and c + 8, clipped to the clusters that exist. `decay_rates`: positive rates. Positive lengths.
All inputs are finite; a program needn't handle non-finite values.
Results may differ from a plain program's by a relative error of at most 0.0085.
Values may be sent and summed in bfloat16 or wider, within the bound.
No kernel may reach another device: no remote copies, remote signals or barrier semaphores. Data moves between devices by JAX's collectives and lax.ppermute only.
A program may use at most 128 MiB of HBM per device.

v0:
```python
import jax
import jax.numpy as jnp
from jax import lax
from jax.sharding import PartitionSpec as P

REACH = 8


def shifted(block, axis, distance):
    devices = range(lax.axis_size(axis))
    route = [(i - distance, i) for i in devices if i - distance in devices]
    return lax.ppermute(block, axis, route)


def extended_2(block, sides, width):
    for axis, dim in sides:
        count = lax.axis_size(axis)
        forward = [(i, i + 1) for i in range(count - 1)]
        backward = [(target, source) for source, target in forward]
        low = lax.ppermute(
            lax.slice_in_dim(block, block.shape[dim] - width, None, axis=dim), axis, forward
        )
        high = lax.ppermute(lax.slice_in_dim(block, 0, width, axis=dim), axis, backward)
        block = jnp.concatenate([low, block, high], axis=dim)
    return block


def cut_along(x, dim, peers):
    before, after = (x.shape[:dim], x.shape[dim + 1 :])
    return jnp.moveaxis(x.reshape(*before, peers, -1, *after), dim, 0)


def sum_at_owner(x, axis, dim):
    blocks = cut_along(x, dim, lax.axis_size(axis))
    arrived = lax.all_to_all(blocks, axis, split_axis=0, concat_axis=0, tiled=True)
    return arrived.astype(jnp.float32).sum(axis=0)


def copy_for_each(x, axis):
    copies = jnp.broadcast_to(x, (lax.axis_size(axis), *x.shape))
    return lax.all_to_all(copies, axis, split_axis=0, concat_axis=0, tiled=True)


def gathered_once(x, axis):
    leaves = jax.tree.leaves(x)
    turns = sorted(range(len(leaves)), key=lambda k: -leaves[k].size)
    width = (1, *leaves[turns[0]].shape)[-1]
    lines = [
        jnp.pad(leaves[k].reshape(-1), (0, -leaves[k].size % width)).reshape(-1, width)
        for k in turns
    ]
    both, at, found = (copy_for_each(jnp.concatenate(lines), axis), 0, {})
    for k, line in zip(turns, lines):
        section = both[:, at : at + len(line)].reshape(len(both), -1)
        found[k] = section[:, : leaves[k].size].reshape(-1, *leaves[k].shape)
        at += len(line)
    numbers = iter(range(len(leaves)))
    return jax.tree.map(lambda _: found[next(numbers)], x)


def joined_by_halves(pieces, combine):
    while len(jax.tree.leaves(pieces)[0]) > 1:
        pieces = jax.vmap(combine)(
            *(jax.tree.map(lambda part: part[side::2], pieces) for side in (0, 1))
        )
    return jax.tree.map(lambda part: part[0], pieces)


def carried_in(x, axis, combine, identity):
    peers, place = (lax.axis_size(axis), lax.axis_index(axis))
    passed = jnp.arange(peers) < place

    def kept(part, zero, own):
        part = jnp.where(
            passed.reshape(-1, *(1 for _ in own.shape)), part, jnp.asarray(zero, own.dtype)
        )
        return part

    pieces = gathered_once(x, axis)
    return joined_by_halves(jax.tree.map(kept, pieces, identity, x), combine)


def laid_out(blocks, dim):
    shape = list(blocks.shape[1:])
    shape[dim] *= blocks.shape[0]
    return jnp.moveaxis(blocks, 0, dim).reshape(shape)


def gathered_copies(x, axis, dim):
    blocks = copy_for_each(x, axis)
    return laid_out(blocks, dim)


def combine(earlier, later):
    return (earlier[0] * later[0], later[0] * earlier[1] + later[1])


def slab_terms(rates, moments, lengths):
    steps_here = lengths.shape[0]
    inclusive = jnp.cumsum(lengths)
    exclusive = inclusive - lengths
    spread = jnp.maximum(exclusive[:, None] - inclusive[None, :], 0.0)
    positions = jnp.arange(steps_here, dtype=jnp.int32)
    before_mask = positions[None, :] < positions[:, None]
    weights = jnp.where(
        before_mask[None, :, :], jnp.exp(-rates[:, None, None] * spread[None, :, :]), 0.0
    )
    local_far = jnp.einsum("mts,sm->tm", weights, moments, precision=lax.Precision.HIGHEST)
    total_decay = jnp.exp(-rates * inclusive[-1])
    end_weights = jnp.exp(-rates[None, :] * (inclusive[-1] - inclusive)[:, None])
    end_state = jnp.sum(end_weights * moments, axis=0)
    return (local_far, end_state, total_decay, exclusive)


def local(density, active, neighbours, near_blocks, to_moments, from_moments, decay_rates, lengths):
    steps_here, clusters_here, unknowns = density.shape
    blocks_each = neighbours.shape[1]
    space_index = lax.axis_index("space")
    first_cluster = space_index * clusters_here
    global_ids = first_cluster + jnp.arange(clusters_here, dtype=jnp.int32)
    live_mask = (global_ids[None, :] < active[:, None]).astype(jnp.bfloat16)
    masked = density * live_mask[:, :, None]
    last_row = shifted(masked[-1:], "tm", 1)
    extended = jnp.concatenate([last_row, masked], 0)
    window = extended_2(extended, (("space", 1),), REACH)
    cluster_major = jnp.transpose(window, (1, 0, 2))
    local_index = (neighbours - (first_cluster - REACH)).reshape(-1)
    picked = jnp.take(cluster_major, local_index, axis=0).reshape(
        clusters_here, blocks_each, steps_here + 1, unknowns
    )
    both_lags = jnp.einsum(
        "cjte,lcjef->ctlf", picked, near_blocks, preferred_element_type=jnp.float32
    )
    near_term = both_lags[:, 1:, 0, :] + both_lags[:, :-1, 1, :]
    near_term = jnp.transpose(near_term, (1, 0, 2))
    terms = decay_rates.shape[0]
    share_width = terms // lax.axis_size("space")
    flat = masked.reshape(steps_here, clusters_here * unknowns)
    partial_moments = lax.dot_general(
        flat,
        to_moments.reshape(terms, clusters_here * unknowns),
        (((1,), (1,)), ((), ())),
        preferred_element_type=jnp.float32,
    )
    moments = sum_at_owner(partial_moments.astype(jnp.bfloat16), "space", 1)
    rates_here = lax.dynamic_slice_in_dim(decay_rates, space_index * share_width, share_width)
    local_far, end_state, total_decay, exclusive = slab_terms(rates_here, moments, lengths)
    prefix = carried_in(
        (total_decay, end_state),
        "tm",
        combine,
        (jnp.ones_like(total_decay), jnp.zeros_like(end_state)),
    )
    arriving = prefix[1]
    far_coeff = jnp.exp(-rates_here[None, :] * exclusive[:, None]) * arriving[None, :] + local_far
    scaled = (far_coeff * jnp.sqrt(2.0 * rates_here)[None, :]).astype(jnp.bfloat16)
    scaled = gathered_copies(scaled, "space", 1)
    far_term = jnp.dot(
        scaled,
        from_moments.reshape(terms, clusters_here * unknowns),
        preferred_element_type=jnp.float32,
    )
    far_term = far_term.reshape(steps_here, clusters_here, unknowns)
    return (live_mask.astype(jnp.float32)[:, :, None] * (near_term + far_term)).astype(jnp.bfloat16)


def solution(mesh):
    placed = (
        P("tm", "space", None),
        P("tm"),
        P("space", None),
        P(None, "space", None, None, None),
        P(None, "space", None),
        P(None, "space", None),
        P(),
        P("tm"),
    )
    return jax.shard_map(
        local, mesh=mesh, in_specs=placed, out_specs=P("tm", "space", None), check_vma=False
    )
```

profile of v0, /device:TPU:1, one launch (start us, length us, event | category | flops | bytes accessed | tf_op | source)
XLA Modules:
  0.0 98.5 jit_solution(3452070897583500147)
XLA Ops:
  0.0 1.4 %fusion.32 = (f32[256,32]{0,1:T(8,128)}, bf16[256,32]{0,1:T(8,128)(2,1)S(1)}) fusion(s32[256]{0:T(256)} %param.9, s32[32]{0:T(128)S(1)} %iota_add_fusion), kind=kLoop, calls=%fused_computation.52 | loop fusion | flops 24576 | bytes 50304 | tf_op jit(solution)/shard_map/convert_element_type | solution.py:164
  1.4 3.3 %copy_multiply_fusion = bf16[256,32,128]{2,0,1:T(8,128)(2,1)S(1)} fusion(bf16[256,32,128]{2,1,0:T(8,128)(2,1)} %param.8, bf16[256,32]{0,1:T(8,128)(2,1)S(1)} %get-tuple-element.22), kind=kLoop, calls=%fused_computation.14 | loop fusion | flops 1048576 | bytes 4210688 | tf_op jit(solution)/shard_map/mul | solution.py:122
  4.7 4.0 %collective-permute-start = (bf16[1,32,128]{2,0,1:T(2,128)(2,1)S(1)}, bf16[1,32,128]{2,0,1:T(2,128)(2,1)S(1)}, u32[]{:S(2)}, u32[]{:S(2)}) collective-permute-start(bf16[1,32,128]{2,0,1:T(2,128)(2,1)S(1)} %slice.123), channel_id=1, source_target_pairs={{0,8},{8,16},{16,24},{24,32},{32,40},{40,48},{48,56},{56,64},{64,7... | collective-permute-start | bytes 24584 | tf_op jit(solution)/shard_map/ppermute | solution.py:12
  8.8 1.4 %fusion.20 = bf16[8,256,8]{1,2,0:T(8,128)(2,1)} fusion(bf16[256,32,128]{2,0,1:T(8,128)(2,1)S(1)} %copy_multiply_fusion, bf16[64,32,128]{2,1,0:T(8,128)(2,1)S(1)} %copy-done), kind=kOutput, calls=%fused_computation.21 | convolution fusion | flops 134234112 | bytes 2654208 | tf_op jit(solution)/shard_map/dot_general | solution.py:139
  10.2 5.3 %all-to-all-start = ((bf16[8,256,8]{1,2,0:T(8,128)(2,1)}), bf16[8,256,8]{1,2,0:T(8,128)(2,1)S(1)}, u32[]{:S(2)}, u32[]{:S(2)}) async-start(bf16[8,256,8]{1,2,0:T(8,128)(2,1)} %fusion.20), calls=%async_computation | async-start | bytes 65536 | tf_op jit(solution)/shard_map/all_to_all | solution.py:35
  15.5 0.5 iota_compare_fusion.1
  16.0 0.3 reduce-window.9
  16.6 0.6 slice.99
  17.2 0.6 broadcast_subtract_fusion.1
  18.2 1.3 %exponential_bitcast_fusion = (f32[1,8]{1,0:T(1,128)}, f32[8]{0:T(128)S(1)}, f32[8]{0:T(128)}) fusion(f32[]{:T(128)} %bitcast.11, f32[64]{0:T(128)S(1)} %copy-done.5, s32[]{:T(128)S(6)} %select_n.39), kind=kLoop, calls=%fused_computation.60 | loop fusion | flops 24 | bytes 136 | tf_op jit(solution)/shard_map/reshape | solution.py:49
  19.5 0.7 copy.23
  20.1 0.3 pad_maximum_fusion.1
  20.5 0.9 copy.26
  21.4 1.9 %collective-permute-start.2 = (bf16[257,8,128]{2,1,0:T(8,128)(2,1)}, bf16[257,8,128]{2,1,0:T(8,128)(2,1)}, u32[]{:S(2)}, u32[]{:S(2)}) collective-permute-start(bf16[257,8,128]{2,1,0:T(8,128)(2,1)} %copy.26), channel_id=1, source_target_pairs={{1,0},{2,1},{3,2},{4,3},{5,4},{6,5},{7,6},{9,8},{10,9},{11,10},{12... | collective-permute-start | bytes 1579016 | tf_op jit(solution)/shard_map/ppermute | solution.py:23
  23.3 3.6 %collective-permute-start.1 = (bf16[257,8,128]{2,1,0:T(8,128)(2,1)S(1)}, bf16[257,8,128]{2,1,0:T(8,128)(2,1)}, u32[]{:S(2)}, u32[]{:S(2)}) collective-permute-start(bf16[257,8,128]{2,1,0:T(8,128)(2,1)S(1)} %copy.25), channel_id=1, source_target_pairs={{0,1},{1,2},{2,3},{3,4},{4,5},{5,6},{6,7},{8,9},{9,10},{10,11},{11... | collective-permute-start | bytes 1579016 | tf_op jit(solution)/shard_map/ppermute | solution.py:20
  27.0 0.2 multiply_reduce_fusion
  27.2 0.6 pad_maximum_fusion.2
  27.8 0.6 broadcast_in_dim.65
  28.4 10.9 %all-to-all-start.1 = ((f32[32,2,8]{2,1,0:T(2,128)}), f32[32,2,8]{2,1,0:T(2,128)S(1)}, u32[]{:S(2)}, u32[]{:S(2)}) async-start(f32[32,2,8]{2,1,0:T(2,128)} %broadcast_in_dim.65), calls=%async_computation.1 | async-start | bytes 65536 | tf_op jit(solution)/shard_map/all_to_all | solution.py:41
  39.3 2.0 %fusion.15 = f32[8,1,256]{2,1,0:T(1,128)S(1)} fusion(f32[256,256]{1,0:T(8,128)S(1)} %subtract_maximum_fusion, f32[8]{0:T(128)S(1)} %get-tuple-element.6, pred[256,256]{1,0:T(8,128)(4,1)S(1)} %iota_compare_fusion, f32[256,8,1]{0,1,2:T(8,128)S(1)} %bitcast.81), kind=kOutput, calls=%fused_computation.15 | convolution fusion | flops 7340032 | bytes 344096 | tf_op jit(solution)/shard_map/mts,sm->tm/dot_general | solution.py:108
  41.4 6.8 %all-to-all-done.1 = f32[32,2,8]{2,1,0:T(2,128)S(1)} async-done(((f32[32,2,8]{2,1,0:T(2,128)}), f32[32,2,8]{2,1,0:T(2,128)S(1)}, u32[]{:S(2)}, u32[]{:S(2)}) %all-to-all-start.1) | async-done | bytes 2080 | tf_op jit(solution)/shard_map/all_to_all | solution.py:41
  48.2 0.7 broadcast_select_fusion.1
  49.3 0.7 fusion.30
  50.0 0.6 broadcast_in_dim.70
  50.6 5.3 %all-to-all-start.2 = ((bf16[8,256,8]{1,2,0:T(8,128)(2,1)}), bf16[8,256,8]{1,2,0:T(8,128)(2,1)S(1)}, u32[]{:S(2)}, u32[]{:S(2)}) async-start(bf16[8,256,8]{1,2,0:T(8,128)(2,1)} %broadcast_in_dim.70), calls=%async_computation.2 | async-start | bytes 65536 | tf_op jit(solution)/shard_map/all_to_all | solution.py:41
  55.9 1.1 %copy.28 = bf16[257,8,128]{2,0,1:T(8,128)(2,1)S(1)} copy(bf16[257,8,128]{2,1,0:T(8,128)(2,1)} %collective-permute-done.2) | data formatting | bytes 1052672 | tf_op jit(solution)/shard_map/ppermute | solution.py:23
  57.0 1.1 %copy.27 = bf16[257,8,128]{2,0,1:T(8,128)(2,1)S(1)} copy(bf16[257,8,128]{2,1,0:T(8,128)(2,1)} %collective-permute-done.1) | data formatting | bytes 1052672 | tf_op jit(solution)/shard_map/ppermute | solution.py:20
  58.2 4.2 %maximum_bitcast_fusion = bf16[48,257,128]{2,1,0:T(8,128)(2,1)} fusion(bf16[257,8,128]{2,0,1:T(8,128)(2,1)S(1)} %copy.28, bf16[256,32,128]{2,0,1:T(8,128)(2,1)S(1)} %copy_multiply_fusion, bf16[1,32,128]{2,0,1:T(2,128)(2,1)S(1)} %collective-permute-done, bf16[257,8,128]{2,0,1:T(8,128)(2,1)S(1)} %copy.27), kind=kLoop, calls=%fused_computation.13 | loop fusion | flops 12632064 | bytes 6316032 | tf_op jit(solution)/shard_map/transpose | solution.py:126
  62.3 12.1 %gather_fusion = bf16[256,257,128]{2,1,0:T(8,128)(2,1)} fusion(bf16[48,257,128]{2,1,0:T(8,128)(2,1)} %maximum_bitcast_fusion, s32[1024]{0:T(1024)S(1)} %pad_clamp_fusion), kind=kCustom, calls=%fused_computation | custom fusion | bytes 33686528 | tf_op jit(solution)/shard_map/jit(_take)/gather | solution.py:128
  74.5 16.8 %fusion.10 = f32[32,257,2,128]{3,1,2,0:T(8,128)} fusion(bf16[2,32,8,128,128]{4,3,2,1,0:T(8,128)(2,1)} %param.11, bf16[32,8,257,128]{3,2,1,0:T(8,128)(2,1)} %bitcast.78, pred[32,8]{1,0:T(8,128)(4,1)S(1)} %copy-done.2), kind=kOutput, calls=%fused_computation.12 | convolution fusion | flops 4320165888 | bytes 42041600 | tf_op jit(solution)/shard_map/cjte,lcjef->ctlf/dot_general | solution.py:131
  91.3 4.6 %fusion.9 = bf16[256,32,128]{2,0,1:T(8,128)(2,1)S(1)} fusion(f32[32,257,2,128]{3,1,2,0:T(8,128)} %fusion.10, f32[256,32]{0,1:T(8,128)S(1)} %copy-done.1, bf16[8,256,8]{1,2,0:T(8,128)(2,1)S(1)} %all-to-all-done.2, bf16[8,8,32,128]{3,2,1,0:T(8,128)(2,1)} %bitcast.85), kind=kOutput, calls=%fused_computation.11 | convolution fusion | flops 138412032 | bytes 11075584 | tf_op jit(solution)/shard_map/dot_general | solution.py:158
  95.8 2.7 %copy.34 = bf16[256,32,128]{2,1,0:T(8,128)(2,1)} copy(bf16[256,32,128]{2,0,1:T(8,128)(2,1)S(1)} %fusion.9) | data formatting | bytes 4194304 | tf_op jit(solution)/shard_map/convert_element_type | solution.py:164
  (54 shorter events, 1.1 us)
Async XLA Ops:
  0.0 8.8 %copy-start = (bf16[64,32,128]{2,1,0:T(8,128)(2,1)S(1)}, bf16[64,32,128]{2,1,0:T(8,128)(2,1)}, u32[]{:S(2)}) copy-start(bf16[64,32,128]{2,1,0:T(8,128)(2,1)} %param.12) | copy-start | bytes 1572868
  1.4 14.6 %copy-start.4 = (f32[256]{0:T(256)S(1)}, f32[256]{0:T(256)}, u32[]{:S(2)}) copy-start(f32[256]{0:T(256)} %param.15) | copy-start | bytes 3076
  1.4 16.4 %copy-start.3 = (s32[32,8]{0,1:T(8,128)S(1)}, s32[32,8]{0,1:T(8,128)}, u32[]{:S(2)}) copy-start(s32[32,8]{0,1:T(8,128)} %param.10) | copy-start | bytes 3076
  1.4 16.8 %copy-start.5 = (f32[64]{0:T(128)S(1)}, f32[64]{0:T(128)}, u32[]{:S(2)}) copy-start(f32[64]{0:T(128)} %param.14) | copy-start | bytes 772
  4.7 15.4 %collective-permute-start = (bf16[1,32,128]{2,0,1:T(2,128)(2,1)S(1)}, bf16[1,32,128]{2,0,1:T(2,128)(2,1)S(1)}, u32[]{:S(2)}, u32[]{:S(2)}) collective-permute-start(bf16[1,32,128]{2,0,1:T(2,128)(2,1)S(1)} %slice.123), channel_id=1, source_target_pairs={{0,8},{8,16},{16,24},{24,32},{32,40},{40,48},{48,56},{56,64},{64,7... | collective-permute-start | bytes 24584 | tf_op jit(solution)/shard_map/ppermute | solution.py:12
  10.2 16.8 %all-to-all-start = ((bf16[8,256,8]{1,2,0:T(8,128)(2,1)}), bf16[8,256,8]{1,2,0:T(8,128)(2,1)S(1)}, u32[]{:S(2)}, u32[]{:S(2)}) async-start(bf16[8,256,8]{1,2,0:T(8,128)(2,1)} %fusion.20), calls=%async_computation | async-start | bytes 65536 | tf_op jit(solution)/shard_map/all_to_all | solution.py:35
  21.4 34.5 %collective-permute-start.2 = (bf16[257,8,128]{2,1,0:T(8,128)(2,1)}, bf16[257,8,128]{2,1,0:T(8,128)(2,1)}, u32[]{:S(2)}, u32[]{:S(2)}) collective-permute-start(bf16[257,8,128]{2,1,0:T(8,128)(2,1)} %copy.26), channel_id=1, source_target_pairs={{1,0},{2,1},{3,2},{4,3},{5,4},{6,5},{7,6},{9,8},{10,9},{11,10},{12... | collective-permute-start | bytes 1579016 | tf_op jit(solution)/shard_map/ppermute | solution.py:23
  23.3 33.7 %collective-permute-start.1 = (bf16[257,8,128]{2,1,0:T(8,128)(2,1)S(1)}, bf16[257,8,128]{2,1,0:T(8,128)(2,1)}, u32[]{:S(2)}, u32[]{:S(2)}) collective-permute-start(bf16[257,8,128]{2,1,0:T(8,128)(2,1)S(1)} %copy.25), channel_id=1, source_target_pairs={{0,1},{1,2},{2,3},{3,4},{4,5},{5,6},{6,7},{8,9},{9,10},{10,11},{11... | collective-permute-start | bytes 1579016 | tf_op jit(solution)/shard_map/ppermute | solution.py:20
  28.4 19.8 %all-to-all-start.1 = ((f32[32,2,8]{2,1,0:T(2,128)}), f32[32,2,8]{2,1,0:T(2,128)S(1)}, u32[]{:S(2)}, u32[]{:S(2)}) async-start(f32[32,2,8]{2,1,0:T(2,128)} %broadcast_in_dim.65), calls=%async_computation.1 | async-start | bytes 65536 | tf_op jit(solution)/shard_map/all_to_all | solution.py:41
  50.6 40.7 %all-to-all-start.2 = ((bf16[8,256,8]{1,2,0:T(8,128)(2,1)}), bf16[8,256,8]{1,2,0:T(8,128)(2,1)S(1)}, u32[]{:S(2)}, u32[]{:S(2)}) async-start(bf16[8,256,8]{1,2,0:T(8,128)(2,1)} %broadcast_in_dim.70), calls=%async_computation.2 | async-start | bytes 65536 | tf_op jit(solution)/shard_map/all_to_all | solution.py:41
  62.3 12.1 %copy-start.2 = (pred[32,8]{1,0:T(8,128)(4,1)S(1)}, pred[32,8]{1,0:T(8,128)(4,1)}, u32[]{:S(2)}) copy-start(pred[32,8]{1,0:T(8,128)(4,1)} %copy.23) | copy-start | bytes 772
  74.5 16.8 %copy-start.1 = (f32[256,32]{0,1:T(8,128)S(1)}, f32[256,32]{0,1:T(8,128)}, u32[]{:S(2)}) copy-start(f32[256,32]{0,1:T(8,128)} %get-tuple-element.21) | copy-start | bytes 98308
where the time goes:
time: 99.1 us; the launch traced here: 98.5 us
  starting transfers between devices  31.1 us (31%)
  matrix products  24.7 us (25%)
  local copies, waits for them, and re-layouts  21.2 us (21%)
  other arithmetic  14.5 us (15%)
  waiting for transfers between devices  6.84 us (7%)
    dot_general x1, matrix products, local(): jnp.einsum('cjte,lcjef->ctlf', picked, near_blocks, preferred_element_typ...  16.8 us
    all_to_all x2, starting transfers between devices, copy_for_each(): return lax.all_to_all(copies, axis, split_axis=0, concat_axis=0, tiled=True)  16.2 us
    gather x1, local copies, waits for them, and re-layouts, local(): jnp.take(cluster_major, local_index, axis=0)  12.1 us
    all_to_all x2, waiting for transfers between devices, copy_for_each(): return lax.all_to_all(copies, axis, split_axis=0, concat_axis=0, tiled=True)  6.83 us
    all_to_all x1, starting transfers between devices, sum_at_owner(): lax.all_to_all(blocks, axis, split_axis=0, concat_axis=0, tiled=True)  5.25 us
    dot_general x1, matrix products, local(): jnp.dot(scaled, from_moments.reshape(terms, clusters_here * unknowns), pr...  4.57 us
    transpose x1, other arithmetic, local(): cluster_major = jnp.transpose(window, (1, 0, 2))  4.17 us
    ppermute x1, starting transfers between devices, shifted(): return lax.ppermute(block, axis, route)  4.03 us
  transfers between devices with their start and end apart: 6, of which 1 were waited for; matrix products, arithmetic and copies ran while one was open for 49% of the time, Pallas kernels for 0%

commit v1 on v0

v1 whole, which is shorter than its diff:
```python
import functools

import jax
import jax.numpy as jnp
from jax import lax
from jax.experimental import pallas as pl
from jax.experimental.pallas import tpu as pltpu
from jax.sharding import PartitionSpec as P

REACH = 8
F32 = jnp.float32
BF16 = jnp.bfloat16


def column(row, lanes):
    return jnp.transpose(jnp.broadcast_to(row, (lanes, row.shape[1])))


def shifted_down(v, steps, fill):
    rows = v.shape[0]
    if steps < 8:
        moved = pltpu.roll(v, steps, 0)
        at = lax.broadcasted_iota(jnp.int32, v.shape, 0)
        return jnp.where(at < steps, jnp.full_like(v, fill), moved)
    return jnp.concatenate([jnp.full((steps, v.shape[1]), fill, v.dtype), v[: rows - steps]], 0)


def doubled(row):
    return jnp.concatenate([row, row], axis=1)


def prep_kernel(
    steps,
    density,
    active,
    to_moments,
    rates,
    lengths,
    low,
    mid,
    high,
    far,
    decay,
    ends,
    flat,
    flat_map,
    live,
):
    step = pl.program_id(0)
    last = pl.num_programs(0) - 1
    chunk, clusters, unknowns = density.shape
    terms = to_moments.shape[0]
    first = lax.axis_index("space") * clusters

    @pl.when(step == 0)
    def _():
        live[...] = column(active[...], unknowns)

    flat[...] = density[...].astype(F32).reshape(chunk * clusters, unknowns)
    here = pl.ds(pl.multiple_of(step * chunk, chunk), chunk)
    alive = live[here, :]

    def place(c):
        if c < REACH:
            return low, c
        if c < clusters - REACH:
            return mid, c - REACH
        return high, c - (clusters - REACH)

    for c in range(clusters):
        x = flat[pl.ds(c, chunk, stride=clusters), :]
        x = jnp.where(alive > first + c, x, 0.0).astype(BF16)
        ref, at = place(c)
        ref[at, here, :] = x

    @pl.when(step == last)
    def _():
        flat_map[...] = to_moments[...].astype(F32).reshape(terms * clusters, unknowns)
        total = jnp.zeros((steps, 2 * terms), F32)
        for c in range(0, clusters, 2):
            a, i = place(c)
            b, j = place(c + 1)
            x = jnp.concatenate([a[i], b[j]], axis=1)
            w = jnp.concatenate(
                [
                    flat_map[pl.ds(c, terms, stride=clusters), :].astype(BF16),
                    flat_map[pl.ds(c + 1, terms, stride=clusters), :].astype(BF16),
                ],
                axis=1,
            )
            w = jnp.concatenate([w, w], axis=0)
            total = total + lax.dot_general(
                x, w, (((1,), (1,)), ((), ())), preferred_element_type=F32
            )
        d = jnp.exp(-doubled(rates[...]) * column(lengths[...], 2 * terms))
        s = 1
        while s < steps:
            before = shifted_down(total, s, 0.0)
            factor = shifted_down(d, s, 1.0)
            total = total + d * before
            d = d * factor
            s *= 2
        far[...] = shifted_down(total, 1, 0.0)
        decay[...] = shifted_down(d, 1, 1.0)
        lane = lax.broadcasted_iota(jnp.int32, (1, 2 * terms), 1)
        line = jnp.where(lane < terms, total[steps - 1 :], d[steps - 1 :])
        for k in range(ends.shape[0]):
            ends[k] = line


def prep(density, active, to_moments, rates, lengths, slabs):
    steps, clusters, unknowns = density.shape
    terms = to_moments.shape[0]
    chunk = 64
    whole = lambda *shape: pl.BlockSpec(shape, lambda i: (0,) * len(shape))

    return pl.pallas_call(
        functools.partial(prep_kernel, steps),
        grid=(steps // chunk,),
        in_specs=[
            pl.BlockSpec((chunk, clusters, unknowns), lambda i: (i, 0, 0)),
            whole(1, steps),
            whole(terms, clusters, unknowns),
            whole(1, terms),
            whole(1, steps),
        ],
        out_specs=[
            whole(REACH, steps, unknowns),
            whole(clusters - 2 * REACH, steps, unknowns),
            whole(REACH, steps, unknowns),
            whole(steps, 2 * terms),
            whole(steps, 2 * terms),
            whole(slabs, 1, 2 * terms),
        ],
        out_shape=[
            jax.ShapeDtypeStruct((REACH, steps, unknowns), BF16),
            jax.ShapeDtypeStruct((clusters - 2 * REACH, steps, unknowns), BF16),
            jax.ShapeDtypeStruct((REACH, steps, unknowns), BF16),
            jax.ShapeDtypeStruct((steps, 2 * terms), F32),
            jax.ShapeDtypeStruct((steps, 2 * terms), F32),
            jax.ShapeDtypeStruct((slabs, 1, 2 * terms), F32),
        ],
        scratch_shapes=[
            pltpu.VMEM((chunk * clusters, unknowns), F32),
            pltpu.VMEM((terms * clusters, unknowns), F32),
            pltpu.VMEM((steps, unknowns), jnp.int32),
        ],
        compiler_params=pltpu.CompilerParams(vmem_limit_bytes=24 << 20),
        name="prep",
    )(density, active, to_moments, rates, lengths)


def arrive_kernel(ends, far, decay, out):
    me = lax.axis_index("tm")
    slabs = ends.shape[0]
    steps, lanes = far.shape
    half = lanes // 2
    lane = lax.broadcasted_iota(jnp.int32, (1, lanes), 1)
    state = jnp.zeros((1, lanes), F32)
    for k in range(slabs):
        v = ends[k]
        other = pltpu.roll(v, half, 1)
        end = jnp.where(lane < half, v, other)
        factor = jnp.where(lane < half, other, v)
        state = jnp.where(k < me, factor * state + end, state)
    x = far[...] + decay[...] * state
    wide = lax.broadcasted_iota(jnp.int32, (steps // 2, lanes), 1)
    packed = jnp.where(wide < half, x[: steps // 2], x[steps // 2 :]).astype(BF16)
    for k in range(out.shape[0]):
        out[k] = packed


def arrive(ends, far, decay, peers):
    steps, lanes = far.shape
    return pl.pallas_call(
        arrive_kernel,
        out_shape=jax.ShapeDtypeStruct((peers, steps // 2, lanes), BF16),
        name="arrive",
    )(ends, far, decay)


def near_kernel(offset, split, group, neighbours, *refs):
    sources = refs[: len(offset)]
    blocks, near, carry, window, sems = refs[len(offset) :]
    step = pl.program_id(0)

    @pl.when(step == 0)
    def _():
        copies = [
            pltpu.make_async_copy(src, window.at[pl.ds(at, src.shape[0])], sems.at[k])
            for k, (src, at) in enumerate(zip(sources, offset))
        ]
        for copy in copies:
            copy.start()
        for copy in copies:
            copy.wait()

    lags, _, nb, unknowns, _ = blocks.shape
    clusters = neighbours.shape[0]
    base = lax.axis_index("space") * clusters - REACH
    for g in range(group):
        here = step * group + g
        cluster = split(here)
        x = jnp.concatenate(
            [window[neighbours[cluster, j] - base] for j in range(nb)], axis=1
        )
        w = jnp.concatenate(
            [blocks[lag, g].reshape(nb * unknowns, unknowns) for lag in range(lags)], axis=1
        )
        both = jnp.dot(x, w, preferred_element_type=F32)
        now, later = both[:, :unknowns], both[:, unknowns:]
        near[g] = now + shifted_down(later, 1, 0.0)
        carry[g] = later[later.shape[0] - 1 :]


def near_field(neighbours, sources, offset, blocks, split, block_of, count, group):
    steps, unknowns = sources[0].shape[1:]
    lags, clusters, nb = blocks.shape[:3]

    return pl.pallas_call(
        functools.partial(near_kernel, offset, split, group),
        grid_spec=pltpu.PrefetchScalarGridSpec(
            num_scalar_prefetch=1,
            grid=(count // group,),
            in_specs=[pl.BlockSpec(memory_space=pl.ANY)] * len(sources)
            + [
                pl.BlockSpec(
                    (lags, group, nb, unknowns, unknowns),
                    lambda i, _: (0, block_of(i), 0, 0, 0),
                )
            ],
            out_specs=[
                pl.BlockSpec((group, steps, unknowns), lambda i, _: (i, 0, 0)),
                pl.BlockSpec((group, 1, unknowns), lambda i, _: (i, 0, 0)),
            ],
            scratch_shapes=[
                pltpu.VMEM((clusters + 2 * REACH, steps, unknowns), BF16),
                pltpu.SemaphoreType.DMA((len(sources),)),
            ],
        ),
        out_shape=[
            jax.ShapeDtypeStruct((count, steps, unknowns), F32),
            jax.ShapeDtypeStruct((count, 1, unknowns), F32),
        ],
        compiler_params=pltpu.CompilerParams(vmem_limit_bytes=24 << 20),
        name="near",
    )(neighbours, *sources, blocks)


def final_kernel(
    inner,
    outer,
    carry_in,
    carry_out,
    parts,
    from_moments,
    rates,
    active,
    out,
    flat,
    live,
    flat_map,
    maps,
    scaled,
):
    step = pl.program_id(0)
    chunk, clusters, unknowns = out.shape
    terms = from_moments.shape[0]
    steps = active.shape[1]
    first = lax.axis_index("space") * clusters

    @pl.when(step == 0)
    def _():
        live[...] = column(active[...], unknowns)
        flat_map[...] = from_moments[...].astype(F32).reshape(terms * clusters, unknowns)
        for c in range(clusters):
            w = flat_map[pl.ds(c, terms, stride=clusters), :].astype(BF16)
            maps[c // 2, :, pl.ds((c % 2) * unknowns, unknowns)] = jnp.concatenate([w, w], axis=0)
        total = parts[0].astype(F32)
        for k in range(1, parts.shape[0]):
            total = total + parts[k].astype(F32)
        scaled[...] = total * jnp.sqrt(2.0 * doubled(rates[...]))

    here = pl.ds(pl.multiple_of(step * chunk, chunk), chunk)
    alive = live[here, :]
    per_half = steps // 2 // chunk
    half = step // per_half
    mine = scaled[pl.ds(pl.multiple_of(lax.rem(step, per_half) * chunk, chunk), chunk), :]
    lane = lax.broadcasted_iota(jnp.int32, mine.shape, 1)
    mine = jnp.where(lane // terms == half, mine, 0.0).astype(BF16)
    row = lax.broadcasted_iota(jnp.int32, (chunk, unknowns), 0)
    starts = jnp.logical_and(row == 0, step == 0)
    for p in range(clusters // 2):
        both = jnp.dot(mine, maps[p], preferred_element_type=F32)
        for q in range(2):
            c = 2 * p + q
            if c < REACH:
                near, at, carry = outer, c, carry_out
            elif c < clusters - REACH:
                near, at, carry = inner, c - REACH, carry_in
            else:
                near, at, carry = outer, c - (clusters - 2 * REACH), carry_out
            x = both[:, q * unknowns : (q + 1) * unknowns] + near[at]
            x = x + jnp.where(starts, jnp.broadcast_to(carry[at], x.shape), 0.0)
            x = jnp.where(alive > first + c, x, 0.0)
            flat[pl.ds(c, chunk, stride=clusters), :] = x
    out[...] = flat[...].reshape(chunk, clusters, unknowns).astype(BF16)


def final(inner, outer, carry_in, carry_out, parts, from_moments, rates, active):
    count, steps, unknowns = inner.shape
    terms, clusters = from_moments.shape[:2]
    chunk = 64
    whole = lambda *shape: pl.BlockSpec(shape, lambda i: (0,) * len(shape))
    return pl.pallas_call(
        final_kernel,
        grid=(steps // chunk,),
        in_specs=[
            pl.BlockSpec((count, chunk, unknowns), lambda i: (0, i, 0)),
            pl.BlockSpec((outer.shape[0], chunk, unknowns), lambda i: (0, i, 0)),
            whole(*carry_in.shape),
            whole(*carry_out.shape),
            whole(*parts.shape),
            whole(*from_moments.shape),
            whole(1, terms),
            whole(1, steps),
        ],
        out_specs=pl.BlockSpec((chunk, clusters, unknowns), lambda i: (i, 0, 0)),
        out_shape=jax.ShapeDtypeStruct((steps, clusters, unknowns), BF16),
        scratch_shapes=[
            pltpu.VMEM((chunk * clusters, unknowns), F32),
            pltpu.VMEM((steps, unknowns), jnp.int32),
            pltpu.VMEM((terms * clusters, unknowns), F32),
            pltpu.VMEM((clusters // 2, 2 * terms, 2 * unknowns), BF16),
            pltpu.VMEM((steps // 2, 2 * terms), F32),
        ],
        compiler_params=pltpu.CompilerParams(vmem_limit_bytes=24 << 20),
        name="final",
    )(inner, outer, carry_in, carry_out, parts, from_moments, rates, active)


def exchanged(x, axis):
    return lax.all_to_all(x, axis, split_axis=0, concat_axis=0, tiled=True)


def passed_on(x, axis, distance):
    count = lax.axis_size(axis)
    route = [(i, i + distance) for i in range(count) if 0 <= i + distance < count]
    return lax.ppermute(x, axis, route)


def local(density, active, neighbours, near_blocks, to_moments, from_moments, decay_rates, lengths):
    steps, clusters, unknowns = density.shape
    slabs, peers = lax.axis_size("tm"), lax.axis_size("space")
    active = active.reshape(1, steps)
    lengths = lengths.reshape(1, steps)
    rates = decay_rates.reshape(1, -1)
    low, mid, high, far, decay, ends = prep(density, active, to_moments, rates, lengths, slabs)
    ends = exchanged(ends, "tm")
    from_below = passed_on(high, "space", 1)
    from_above = passed_on(low, "space", -1)
    inner_count = clusters - 2 * REACH
    group = 2
    inner, carry_in = near_field(
        neighbours,
        (low, mid, high),
        (REACH, 2 * REACH, clusters),
        near_blocks,
        lambda i: i + REACH,
        lambda i: i + REACH // group,
        inner_count,
        group,
    )
    parts = exchanged(arrive(ends, far, decay, peers), "space")
    half = REACH // group
    outer, carry_out = near_field(
        neighbours,
        (from_below, low, mid, high, from_above),
        (0, REACH, 2 * REACH, clusters, clusters + REACH),
        near_blocks,
        lambda i: jnp.where(i < REACH, i, i + inner_count),
        lambda i: jnp.where(i < half, i, i + inner_count // group),
        2 * REACH,
        group,
    )
    carry = passed_on(jnp.concatenate([carry_in, carry_out], axis=0), "tm", 1)
    return final(
        inner,
        outer,
        carry[:inner_count],
        carry[inner_count:],
        parts,
        from_moments,
        rates,
        active,
    )


def solution(mesh):
    placed = (
        P("tm", "space", None),
        P("tm"),
        P("space", None),
        P(None, "space", None, None, None),
        P(None, "space", None),
        P(None, "space", None),
        P(),
        P("tm"),
    )
    return jax.shard_map(
        local, mesh=mesh, in_specs=placed, out_specs=P("tm", "space", None), check_vma=False
    )
```

time: 99.1 us -> 73.9 us (0.75)
  matrix products: 24.7 us -> 0 us
  Pallas kernels: 0 us -> 23.4 us
  other arithmetic: 14.5 us -> 0.02 us
  starting transfers between devices: 31.1 us -> 25.3 us
  local copies, waits for them, and re-layouts: 21.2 us -> 18 us
    dot_general x4 -> x0, matrix products: 24.7 us -> none  [the longest x1 16.8 us: local(): jnp.einsum('cjte,lcjef->ctlf', picked, near_blocks, preferred_element_typ...]
    pallas_call x0 -> x5, Pallas kernels: none -> 23.4 us  [the longest x2 10.5 us: near_field(): pl.pallas_call(functools.partial(near_kernel, offset, split, group), grid...]
    unnamed x12 -> x35, local copies, waits for them, and re-layouts: 0.02 us -> 18 us
    gather x1 -> x0, local copies, waits for them, and re-layouts: 12.1 us -> none  [local(): jnp.take(cluster_major, local_index, axis=0)]
    all_to_all x3 -> x2, starting transfers between devices: 21.5 us -> 15.1 us  [exchanged(): return lax.all_to_all(x, axis, split_axis=0, concat_axis=0, tiled=True)]
    transpose x1 -> x0, other arithmetic: 4.17 us -> none  [local(): cluster_major = jnp.transpose(window, (1, 0, 2))]
    mul x6 -> x0, other arithmetic: 3.32 us -> none  [the longest x1 3.28 us: local(): masked = density * live_mask[:, :, None]]
    convert_element_type x1 -> x0, local copies, waits for them, and re-layouts: 2.67 us -> none  [local(): (live_mask.astype(jnp.float32)[:, :, None] * (near_term + far_term)).asty...]
  transfers between devices with their start and end apart: 6 -> 5, of which waited for: 1 -> 1; matrix products, arithmetic and copies ran while one was open for 49% -> 0% of each run, Pallas kernels for 0% -> 17%
where the time goes in v1:
time: 73.9 us; the launch traced here: 73.3 us
  starting transfers between devices  25.3 us (34%)
  Pallas kernels  23.4 us (32%)
  local copies, waits for them, and re-layouts  18 us (24%)
  waiting for transfers between devices  6.51 us (9%)
    unnamed x35, local copies, waits for them, and re-layouts  18 us
    all_to_all x2, starting transfers between devices, exchanged(): return lax.all_to_all(x, axis, split_axis=0, concat_axis=0, tiled=True)  15.1 us
    pallas_call x2, Pallas kernels, near_field(): pl.pallas_call(functools.partial(near_kernel, offset, split, group), grid...  10.5 us
    ppermute x3, starting transfers between devices, passed_on(): return lax.ppermute(x, axis, route)  10.2 us
    all_to_all x2, waiting for transfers between devices, exchanged(): return lax.all_to_all(x, axis, split_axis=0, concat_axis=0, tiled=True)  6.5 us
    pallas_call x1, Pallas kernels, final(): pl.pallas_call(final_kernel, grid=(steps // chunk,), in_specs=[pl.BlockSp...  5.52 us
    pallas_call x1, Pallas kernels, prep(): pl.pallas_call(functools.partial(prep_kernel, steps), grid=(steps // chun...  5.51 us
    pallas_call x1, Pallas kernels, arrive(): pl.pallas_call(arrive_kernel, out_shape=jax.ShapeDtypeStruct((peers, step...  1.86 us
  transfers between devices with their start and end apart: 5, of which 1 were waited for; matrix products, arithmetic and copies ran while one was open for 0% of the time, Pallas kernels for 17%

profile of v1, /device:TPU:1, one launch (start us, length us, event | category | flops | bytes accessed | tf_op | source)
XLA Modules:
  0.0 73.3 jit_solution(4836912026517954057)
XLA Ops:
  0.0 1.6 %copy-done.1 = bf16[256,32,128]{2,1,0:T(8,128)(2,1)S(1)} copy-done((bf16[256,32,128]{2,1,0:T(8,128)(2,1)S(1)}, bf16[256,32,128]{2,1,0:T(8,128)(2,1)}, u32[]{:S(2)}) %copy-start.1) | copy-done | bytes 2097176
  1.6 1.0 %copy-done.6 = bf16[64,32,128]{2,1,0:T(8,128)(2,1)S(1)} copy-done((bf16[64,32,128]{2,1,0:T(8,128)(2,1)S(1)}, bf16[64,32,128]{2,1,0:T(8,128)(2,1)}, u32[]{:S(2)}) %copy-start.6) | copy-done | bytes 524312
  2.7 0.7 copy-done.10
  3.3 0.7 copy-done.12
  4.0 0.7 copy-done.14
  4.7 5.5 %prep.1 = (bf16[8,256,128]{2,1,0:T(8,128)(2,1)S(1)}, bf16[16,256,128]{2,1,0:T(8,128)(2,1)S(1)}, bf16[8,256,128]{2,1,0:T(8,128)(2,1)S(1)}, f32[256,128]{1,0:T(8,1...) custom-call(bf16[256,32,128]{2,1,0:T(8,128)(2,1)S(1)} %copy-done.1, s32[1,256]{1,0:T(1,128)S(1)} %bitcast.3, ...), custom_call_target="tpu_custom_call" | custom-call | tf_op jit(solution)/shard_map/prep/pallas_call | solution.py:117
  10.2 0.7 copy-done.8
  10.8 0.7 copy-done.9
  11.5 5.1 %collective-permute-start.1 = (bf16[8,256,128]{2,1,0:T(8,128)(2,1)S(1)}, bf16[8,256,128]{2,1,0:T(8,128)(2,1)S(1)}, u32[]{:S(2)}, u32[]{:S(2)}) collective-permute-start(bf16[8,256,128]{2,1,0:T(8,128)(2,1)S(1)} %get-tuple-element.15.refs_0_.refs_1_), channel_id=1, source_target_pairs={{1,0},{2,1},{3,2},{4,3},{5,4},{6,5},{7,6},{9,8},{10,9},{11,10},{12... | collective-permute-start | bytes 1572872 | tf_op jit(solution)/shard_map/ppermute | solution.py:349
  16.6 1.9 %collective-permute-start = (bf16[8,256,128]{2,1,0:T(8,128)(2,1)S(1)}, bf16[8,256,128]{2,1,0:T(8,128)(2,1)S(1)}, u32[]{:S(2)}, u32[]{:S(2)}) collective-permute-start(bf16[8,256,128]{2,1,0:T(8,128)(2,1)S(1)} %get-tuple-element.17.refs_2_.refs_3_), channel_id=1, source_target_pairs={{0,1},{1,2},{2,3},{3,4},{4,5},{5,6},{6,7},{8,9},{9,10},{10,11},{11... | collective-permute-start | bytes 1572872 | tf_op jit(solution)/shard_map/ppermute | solution.py:349
  18.6 10.6 %all-to-all-start = ((f32[32,1,128]{2,1,0:T(1,128)}), f32[32,1,128]{2,1,0:T(1,128)S(1)}, u32[]{:S(2)}, u32[]{:S(2)}) async-start(f32[32,1,128]{2,1,0:T(1,128)} %get-tuple-element.22), calls=%async_computation | async-start | bytes 32768 | tf_op jit(solution)/shard_map/all_to_all | solution.py:343
  29.1 0.1 copy.9.neighbours
  29.2 5.8 %copy-done = bf16[2,32,8,128,128]{4,3,2,1,0:T(8,128)(2,1)S(1)} copy-done((bf16[2,32,8,128,128]{4,3,2,1,0:T(8,128)(2,1)S(1)}, bf16[2,32,8,128,128]{4,3,2,1,0:T(8,128)(2,1)}, u32[]{:S(2)}) %copy-start) | copy-done | bytes 16777240
  35.0 5.2 %near.2 = (f32[16,256,128]{2,1,0:T(8,128)S(1)}, f32[16,1,128]{2,1,0:T(1,128)S(1)}) custom-call(s32[32,8]{1,0:T(8,128)S(1)} %copy.9.neighbours, bf16[8,256,128]{2,1,0:T(8,128)(2,1)S(1)} %get-tuple-element.15.refs_0_.refs_1_, bf16[16,256,128]{2,1,0:T(8,128)(2,1)S(1)} %get-tuple-element.16.refs_1_.refs_2_, ...), custom_call_target="tpu_custom_call" | custom-call | tf_op jit(solution)/shard_map/near/pallas_call | solution.py:220
  40.2 0.0 copy-start.2
  40.2 0.0 copy-start.11
  40.2 0.0 copy-start.13
  40.2 0.0 collective-permute-done.1.refs_4_
  40.2 0.0 collective-permute-done.refs_0_
  40.3 5.3 %near.3 = (f32[16,256,128]{2,1,0:T(8,128)S(1)}, f32[16,1,128]{2,1,0:T(1,128)S(1)}) custom-call(s32[32,8]{1,0:T(8,128)S(1)} %copy.9.neighbours, bf16[8,256,128]{2,1,0:T(8,128)(2,1)S(1)} %collective-permute-done.refs_0_, bf16[8,256,128]{2,1,0:T(8,128)(2,1)S(1)} %get-tuple-element.15.refs_0_.refs_1_, ...), custom_call_target="tpu_custom_call" | custom-call | tf_op jit(solution)/shard_map/near/pallas_call | solution.py:220
  45.6 1.3 %copy-done.4 = f32[16,256,128]{2,1,0:T(8,128)} copy-done((f32[16,256,128]{2,1,0:T(8,128)}, f32[16,256,128]{2,1,0:T(8,128)S(1)}, u32[]{:S(2)}) %copy-start.4) | copy-done | bytes 2097176
  46.9 3.1 %collective-permute-start.2 = (f32[32,1,128]{2,1,0:T(1,128)S(1)}, f32[32,1,128]{2,1,0:T(1,128)S(1)}, u32[]{:S(2)}, u32[]{:S(2)}) collective-permute-start(f32[32,1,128]{2,1,0:T(1,128)S(1)} %pad_maximum_fusion), channel_id=1, source_target_pairs={{0,8},{8,16},{16,24},{24,32},{32,40},{40,48},{48,56},{56,64},{64,7... | collective-permute-start | bytes 49160 | tf_op jit(solution)/shard_map/ppermute | solution.py:349
  50.1 0.0 all-to-all-done.ends
  50.1 0.6 copy-done.15
  50.7 1.9 %arrive.1 = bf16[8,128,128]{2,1,0:T(8,128)(2,1)} custom-call(f32[32,1,128]{2,1,0:T(1,128)} %copy-done.15, f32[256,128]{1,0:T(8,128)} %copy-done.8, f32[256,128]{1,0:T(8,128)} %copy-done.9), custom_call_target="tpu_custom_call" | custom-call | tf_op jit(solution)/shard_map/arrive/pallas_call | solution.py:175
  52.5 4.5 %all-to-all-start.1 = ((bf16[8,128,128]{2,1,0:T(8,128)(2,1)}), bf16[8,128,128]{2,1,0:T(8,128)(2,1)S(1)}, u32[]{:S(2)}, u32[]{:S(2)}) async-start(bf16[8,128,128]{2,1,0:T(8,128)(2,1)} %arrive.1), calls=%async_computation.1 | async-start | bytes 524288 | tf_op jit(solution)/shard_map/all_to_all | solution.py:343
  57.1 0.0 collective-permute-done.2
  57.1 6.5 %all-to-all-done.1.parts = bf16[8,128,128]{2,1,0:T(8,128)(2,1)S(1)} async-done(((bf16[8,128,128]{2,1,0:T(8,128)(2,1)}), bf16[8,128,128]{2,1,0:T(8,128)(2,1)S(1)}, u32[]{:S(2)}, u32[]{:S(2)}) %all-to-all-start.1) | async-done | bytes 262176 | tf_op jit(solution)/shard_map/all_to_all | solution.py:343
  63.6 1.6 %copy-done.3 = f32[16,256,128]{2,1,0:T(8,128)S(1)} copy-done((f32[16,256,128]{2,1,0:T(8,128)S(1)}, f32[16,256,128]{2,1,0:T(8,128)}, u32[]{:S(2)}) %copy-start.3) | copy-done | bytes 2097176
  65.2 1.6 %copy-done.5 = f32[16,256,128]{2,1,0:T(8,128)S(1)} copy-done((f32[16,256,128]{2,1,0:T(8,128)S(1)}, f32[16,256,128]{2,1,0:T(8,128)}, u32[]{:S(2)}) %copy-start.5) | copy-done | bytes 2097176
  66.8 1.0 %copy-done.7 = bf16[64,32,128]{2,1,0:T(8,128)(2,1)S(1)} copy-done((bf16[64,32,128]{2,1,0:T(8,128)(2,1)S(1)}, bf16[64,32,128]{2,1,0:T(8,128)(2,1)}, u32[]{:S(2)}) %copy-start.7) | copy-done | bytes 524312
  67.8 5.5 %final.1 = bf16[256,32,128]{2,1,0:T(8,128)(2,1)} custom-call(f32[16,256,128]{2,1,0:T(8,128)S(1)} %copy-done.3, f32[16,256,128]{2,1,0:T(8,128)S(1)} %copy-done.5, f32[16,1,128]{2,1,0:T(1,128)S(1)} %get-tuple-element.26.carry_in, f32[16,1,128]{2,1,0:T(1,128)S(1)} %get-tuple-element.25.carry_out, bf16[8,128,128]{2,1,0:T(8,128)(2,1)S(1)} %all-to-all-done.1.parts, ...), custom_call_target="tpu_custom_call" | custom-call | tf_op jit(solution)/shard_map/final/pallas_call | solution.py:315
  (20 shorter events, 0.1 us)
Async XLA Ops:
  0.0 29.1 %copy-start.16 = (s32[32,8]{0,1:T(8,128)S(1)}, s32[32,8]{0,1:T(8,128)}, u32[]{:S(2)}) copy-start(s32[32,8]{0,1:T(8,128)} %param.10) | copy-start | bytes 3076
  0.0 1.6 %copy-start.1 = (bf16[256,32,128]{2,1,0:T(8,128)(2,1)S(1)}, bf16[256,32,128]{2,1,0:T(8,128)(2,1)}, u32[]{:S(2)}) copy-start(bf16[256,32,128]{2,1,0:T(8,128)(2,1)} %density.1) | copy-start | bytes 6291460
  1.6 1.0 %copy-start.6 = (bf16[64,32,128]{2,1,0:T(8,128)(2,1)S(1)}, bf16[64,32,128]{2,1,0:T(8,128)(2,1)}, u32[]{:S(2)}) copy-start(bf16[64,32,128]{2,1,0:T(8,128)(2,1)} %to_moments.1) | copy-start | bytes 1572868
  2.6 0.7 copy-start.10
  3.3 0.7 copy-start.12
  4.0 0.7 copy-start.14
  10.2 0.7 copy-start.8
  10.8 0.7 copy-start.9
  11.5 28.8 %collective-permute-start.1 = (bf16[8,256,128]{2,1,0:T(8,128)(2,1)S(1)}, bf16[8,256,128]{2,1,0:T(8,128)(2,1)S(1)}, u32[]{:S(2)}, u32[]{:S(2)}) collective-permute-start(bf16[8,256,128]{2,1,0:T(8,128)(2,1)S(1)} %get-tuple-element.15.refs_0_.refs_1_), channel_id=1, source_target_pairs={{1,0},{2,1},{3,2},{4,3},{5,4},{6,5},{7,6},{9,8},{10,9},{11,10},{12... | collective-permute-start | bytes 1572872 | tf_op jit(solution)/shard_map/ppermute | solution.py:349
  16.6 23.6 %collective-permute-start = (bf16[8,256,128]{2,1,0:T(8,128)(2,1)S(1)}, bf16[8,256,128]{2,1,0:T(8,128)(2,1)S(1)}, u32[]{:S(2)}, u32[]{:S(2)}) collective-permute-start(bf16[8,256,128]{2,1,0:T(8,128)(2,1)S(1)} %get-tuple-element.17.refs_2_.refs_3_), channel_id=1, source_target_pairs={{0,1},{1,2},{2,3},{3,4},{4,5},{5,6},{6,7},{8,9},{9,10},{10,11},{11... | collective-permute-start | bytes 1572872 | tf_op jit(solution)/shard_map/ppermute | solution.py:349
  18.6 31.5 %all-to-all-start = ((f32[32,1,128]{2,1,0:T(1,128)}), f32[32,1,128]{2,1,0:T(1,128)S(1)}, u32[]{:S(2)}, u32[]{:S(2)}) async-start(f32[32,1,128]{2,1,0:T(1,128)} %get-tuple-element.22), calls=%async_computation | async-start | bytes 32768 | tf_op jit(solution)/shard_map/all_to_all | solution.py:343
  29.2 5.8 %copy-start = (bf16[2,32,8,128,128]{4,3,2,1,0:T(8,128)(2,1)S(1)}, bf16[2,32,8,128,128]{4,3,2,1,0:T(8,128)(2,1)}, u32[]{:S(2)}) copy-start(bf16[2,32,8,128,128]{4,3,2,1,0:T(8,128)(2,1)} %refs_5_.1) | copy-start | bytes 50331652
  40.2 5.4 %copy-start.2 = (f32[16,256,128]{2,1,0:T(8,128)}, f32[16,256,128]{2,1,0:T(8,128)S(1)}, u32[]{:S(2)}) copy-start(f32[16,256,128]{2,1,0:T(8,128)S(1)} %get-tuple-element.18.inner) | copy-start | bytes 6291460
  40.2 23.4 %copy-start.11 = (s32[256]{0:T(256)S(1)}, s32[256]{0:T(256)}, u32[]{:S(2)}) copy-start(s32[256]{0:T(256)} %param.9) | copy-start | bytes 3076
  40.2 23.4 %copy-start.13 = (f32[64]{0:T(128)S(1)}, f32[64]{0:T(128)}, u32[]{:S(2)}) copy-start(f32[64]{0:T(128)} %param.14) | copy-start | bytes 772
  45.6 1.3 %copy-start.4 = (f32[16,256,128]{2,1,0:T(8,128)}, f32[16,256,128]{2,1,0:T(8,128)S(1)}, u32[]{:S(2)}) copy-start(f32[16,256,128]{2,1,0:T(8,128)S(1)} %get-tuple-element.19.outer) | copy-start | bytes 6291460
  46.9 10.2 %collective-permute-start.2 = (f32[32,1,128]{2,1,0:T(1,128)S(1)}, f32[32,1,128]{2,1,0:T(1,128)S(1)}, u32[]{:S(2)}, u32[]{:S(2)}) collective-permute-start(f32[32,1,128]{2,1,0:T(1,128)S(1)} %pad_maximum_fusion), channel_id=1, source_target_pairs={{0,8},{8,16},{16,24},{24,32},{32,40},{40,48},{48,56},{56,64},{64,7... | collective-permute-start | bytes 49160 | tf_op jit(solution)/shard_map/ppermute | solution.py:349
  50.1 0.6 copy-start.15
  52.5 11.0 %all-to-all-start.1 = ((bf16[8,128,128]{2,1,0:T(8,128)(2,1)}), bf16[8,128,128]{2,1,0:T(8,128)(2,1)S(1)}, u32[]{:S(2)}, u32[]{:S(2)}) async-start(bf16[8,128,128]{2,1,0:T(8,128)(2,1)} %arrive.1), calls=%async_computation.1 | async-start | bytes 524288 | tf_op jit(solution)/shard_map/all_to_all | solution.py:343
  63.6 1.6 %copy-start.3 = (f32[16,256,128]{2,1,0:T(8,128)S(1)}, f32[16,256,128]{2,1,0:T(8,128)}, u32[]{:S(2)}) copy-start(f32[16,256,128]{2,1,0:T(8,128)} %copy-done.2) | copy-start | bytes 6291460
  65.2 1.6 %copy-start.5 = (f32[16,256,128]{2,1,0:T(8,128)S(1)}, f32[16,256,128]{2,1,0:T(8,128)}, u32[]{:S(2)}) copy-start(f32[16,256,128]{2,1,0:T(8,128)} %copy-done.4) | copy-start | bytes 6291460
  66.8 1.0 %copy-start.7 = (bf16[64,32,128]{2,1,0:T(8,128)(2,1)S(1)}, bf16[64,32,128]{2,1,0:T(8,128)(2,1)}, u32[]{:S(2)}) copy-start(bf16[64,32,128]{2,1,0:T(8,128)(2,1)} %from_moments.1) | copy-start | bytes 1572868

commit v2 on v0

v2 whole, which is shorter than its diff:
```python
import functools

import jax
import jax.numpy as jnp
from jax import lax
from jax.experimental import pallas as pl
from jax.experimental.pallas import tpu as pltpu
from jax.sharding import PartitionSpec as P

REACH = 8
F32 = jnp.float32
BF16 = jnp.bfloat16
HBM = pl.BlockSpec(memory_space=pltpu.HBM)
VMEM = pl.BlockSpec(memory_space=pltpu.VMEM)
SMEM = pl.BlockSpec(memory_space=pltpu.SMEM)


def in_hbm(x):
    return pltpu.with_memory_space_constraint(x, pltpu.HBM)


def in_vmem(x):
    return pltpu.with_memory_space_constraint(x, pltpu.VMEM)


def column(row, lanes):
    return jnp.transpose(jnp.broadcast_to(row, (lanes, row.shape[1])))


def shifted_down(v, steps, fill):
    rows = v.shape[0]
    if steps < 8:
        moved = pltpu.roll(v, steps, 0)
        at = lax.broadcasted_iota(jnp.int32, v.shape, 0)
        return jnp.where(at < steps, jnp.full_like(v, fill), moved)
    return jnp.concatenate([jnp.full((steps, v.shape[1]), fill, v.dtype), v[: rows - steps]], 0)


def doubled(row):
    return jnp.concatenate([row, row], axis=1)


def is_even():
    return lax.rem(lax.axis_index("space"), 2) == 0


def prep_kernel(
    density,
    active,
    to_moments,
    rates,
    lengths,
    window,
    pair,
    other,
    far,
    decay,
    ends,
    live,
    dense,
    maps,
    active_row,
    rates_row,
    lengths_row,
    flat,
    sems,
):
    steps, clusters, unknowns = density.shape
    terms = to_moments.shape[0]
    pieces = 4
    size = steps // pieces
    chunk = 32
    pitch = clusters + 1
    first = lax.axis_index("space") * clusters

    def copy(src, dst, k):
        return pltpu.make_async_copy(src, dst, sems.at[k])

    small = [
        copy(active, active_row, 0),
        copy(lengths, lengths_row, 1),
        copy(rates, rates_row, 2),
    ]
    parts = [
        copy(density.at[pl.ds(k * size, size)], dense.at[pl.ds(k * size, size)], 4 + k)
        for k in range(pieces)
    ]
    weights = copy(to_moments, maps, 3)
    for c in small + parts + [weights]:
        c.start()
    for c in small:
        c.wait()
    live[...] = column(active_row[...], unknowns)

    for k in range(pieces):
        parts[k].wait()

        def spread(i, _):
            start = pl.multiple_of(k * size + i * chunk, chunk)
            here = pl.ds(start, chunk)
            x = dense[here].astype(F32)
            for t in range(chunk):
                flat[pl.ds(t * pitch, clusters), :] = x[t]
            alive = live[here, :]
            for c in range(clusters):
                y = flat[pl.ds(c, chunk, stride=pitch), :]
                y = jnp.where(alive > first + c, y, 0.0)
                window[REACH + c, here, :] = y.astype(BF16)
            return 0

        lax.fori_loop(0, size // chunk, spread, 0)

    even = is_even()
    above = clusters
    sides = [
        copy(window.at[pl.ds(jnp.where(even, above, REACH), REACH)], pair, 8),
        copy(window.at[pl.ds(jnp.where(even, REACH, above), REACH)], other, 9),
    ]
    for c in sides:
        c.start()

    weights.wait()
    w = jnp.transpose(maps[...], (1, 0, 2))
    total = jnp.zeros((steps, 2 * terms), F32)
    for c in range(0, clusters, 2):
        x = jnp.concatenate([window[REACH + c], window[REACH + c + 1]], axis=1)
        y = jnp.concatenate([w[c], w[c + 1]], axis=1)
        y = jnp.concatenate([y, y], axis=0)
        total = total + lax.dot_general(
            x, y, (((1,), (1,)), ((), ())), preferred_element_type=F32
        )
    d = jnp.exp(-doubled(rates_row[...]) * column(lengths_row[...], 2 * terms))
    s = 1
    while s < steps:
        before = shifted_down(total, s, 0.0)
        factor = shifted_down(d, s, 1.0)
        total = total + d * before
        d = d * factor
        s *= 2
    lane = lax.broadcasted_iota(jnp.int32, (1, 2 * terms), 1)
    line = jnp.where(lane < terms, total[steps - 1 :], d[steps - 1 :])
    for k in range(ends.shape[0]):
        ends[k] = line
    scale = jnp.sqrt(2.0 * doubled(rates_row[...]))
    far[...] = shifted_down(total, 1, 0.0) * scale
    decay[...] = shifted_down(d, 1, 1.0) * scale
    for c in sides:
        c.wait()


def prep(density, active, to_moments, rates, lengths, slabs):
    steps, clusters, unknowns = density.shape
    terms = to_moments.shape[0]
    lanes = 2 * terms
    side = pltpu.HBM((REACH, steps, unknowns), BF16)
    return pl.pallas_call(
        prep_kernel,
        in_specs=[HBM] * 5,
        out_specs=[VMEM, HBM, HBM] + [VMEM] * 4,
        out_shape=[
            jax.ShapeDtypeStruct((clusters + 2 * REACH, steps, unknowns), BF16),
            side,
            side,
            jax.ShapeDtypeStruct((steps, lanes), F32),
            jax.ShapeDtypeStruct((steps, lanes), F32),
            jax.ShapeDtypeStruct((slabs, 1, lanes), F32),
            jax.ShapeDtypeStruct((steps, unknowns), jnp.int32),
        ],
        scratch_shapes=[
            pltpu.VMEM(density.shape, BF16),
            pltpu.VMEM(to_moments.shape, BF16),
            pltpu.VMEM(active.shape, jnp.int32),
            pltpu.VMEM(rates.shape, F32),
            pltpu.VMEM(lengths.shape, F32),
            pltpu.VMEM((32 * (clusters + 1) + 7, unknowns), F32),
            pltpu.SemaphoreType.DMA((10,)),
        ],
        compiler_params=pltpu.CompilerParams(vmem_limit_bytes=10 << 20),
        name="prep",
    )(*map(in_hbm, (density, active, to_moments, rates, lengths)))


def arrive_kernel(ends, far, decay, out):
    me = lax.axis_index("tm")
    slabs = ends.shape[0]
    steps, lanes = far.shape
    half = lanes // 2
    lane = lax.broadcasted_iota(jnp.int32, (1, lanes), 1)
    state = jnp.zeros((1, lanes), F32)
    for k in range(slabs):
        v = ends[k]
        swapped = pltpu.roll(v, half, 1)
        end = jnp.where(lane < half, v, swapped)
        factor = jnp.where(lane < half, swapped, v)
        state = jnp.where(k < me, factor * state + end, state)
    x = far[...] + decay[...] * state
    wide = lax.broadcasted_iota(jnp.int32, (steps // 2, lanes), 1)
    out[...] = jnp.where(wide < half, x[: steps // 2], x[steps // 2 :])


def arrive(ends, far, decay):
    steps, lanes = far.shape
    return pl.pallas_call(
        arrive_kernel,
        in_specs=[VMEM] * 3,
        out_specs=VMEM,
        out_shape=jax.ShapeDtypeStruct((steps // 2, lanes), F32),
        compiler_params=pltpu.CompilerParams(vmem_limit_bytes=4 << 20),
        name="arrive",
    )(ends, far, decay)


def pair_kernel(a, b, out):
    out[...] = (a[...] + b[...]).astype(BF16)


def pair_sum(a, b):
    return pl.pallas_call(
        pair_kernel,
        in_specs=[VMEM] * 2,
        out_specs=VMEM,
        out_shape=jax.ShapeDtypeStruct(a.shape, BF16),
        compiler_params=pltpu.CompilerParams(vmem_limit_bytes=4 << 20),
        name="pair_sum",
    )(a, b)


def near_fetches(blocks, held, sems, order):
    return [
        [
            pltpu.make_async_copy(blocks.at[lag, c], held.at[lag, i], sems.at[lag, i])
            for lag in range(blocks.shape[0])
        ]
        for i, c in enumerate(order)
    ]


def near_of(neighbours, window, held, fetches, i, cluster):
    lags, _, nb, unknowns, _ = held.shape
    base = lax.axis_index("space") * neighbours.shape[1] - REACH
    for fetch in fetches[i]:
        fetch.wait()
    x = jnp.concatenate([window[neighbours[j, cluster] - base] for j in range(nb)], axis=1)
    w = jnp.concatenate(
        [held[lag, i].reshape(nb * unknowns, unknowns) for lag in range(lags)], axis=1
    )
    both = jnp.dot(x, w, preferred_element_type=F32)
    now, later = both[:, :unknowns], both[:, unknowns:]
    last = pltpu.roll(later[later.shape[0] - 8 :], 1, 0)
    return now + shifted_down(later, 1, 0.0), last


def inner_kernel(order, neighbours, window, blocks, near, held, found, sems, out_sems):
    steps = window.shape[1]
    fetches = near_fetches(blocks, held, sems, order)
    for some in fetches:
        for fetch in some:
            fetch.start()
    stores = []
    for i, cluster in enumerate(order):
        x, last = near_of(neighbours, window, held, fetches, i, cluster)
        found[i, :steps, :] = x
        found[i, steps:, :] = last
        stores.append(pltpu.make_async_copy(found.at[i], near.at[i], out_sems.at[i]))
        stores[-1].start()
    for store in stores:
        store.wait()


def inner_near(neighbours, window, blocks):
    steps, unknowns = window.shape[1:]
    lags, clusters, nb = blocks.shape[:3]
    order = tuple(range(REACH, clusters - REACH))
    count = len(order)
    return pl.pallas_call(
        functools.partial(inner_kernel, order),
        in_specs=[SMEM, VMEM, HBM],
        out_specs=HBM,
        out_shape=pltpu.HBM((count, steps + 8, unknowns), F32),
        scratch_shapes=[
            pltpu.VMEM((lags, count, nb, unknowns, unknowns), BF16),
            pltpu.VMEM((count, steps + 8, unknowns), F32),
            pltpu.SemaphoreType.DMA((lags, count)),
            pltpu.SemaphoreType.DMA((count,)),
        ],
        compiler_params=pltpu.CompilerParams(vmem_limit_bytes=16 << 20),
        name="inner",
    )(neighbours, window, in_hbm(blocks))


def outer_kernel(
    order,
    neighbours,
    window_in,
    from_pair,
    from_other,
    blocks,
    inner,
    from_moments,
    near,
    carry,
    maps,
    window,
    held,
    rows,
    sems,
    side_sems,
):
    del window_in
    steps = window.shape[1]
    even = is_even()
    above = window.shape[0] - REACH

    def copy(src, dst, k):
        return pltpu.make_async_copy(src, dst, side_sems.at[k])

    sides = [
        copy(from_pair, window.at[pl.ds(jnp.where(even, above, 0), REACH)], 0),
        copy(from_other, window.at[pl.ds(jnp.where(even, 0, above), REACH)], 1),
    ]
    inner_copy = copy(inner, near.at[pl.ds(REACH, inner.shape[0])], 2)
    rows_copy = copy(from_moments, rows, 3)
    fetches = near_fetches(blocks, held, sems, order)
    for c in sides:
        c.start()
    for some in fetches:
        for fetch in some:
            fetch.start()
    inner_copy.start()
    rows_copy.start()
    for c in sides:
        c.wait()
    for i, cluster in enumerate(order):
        x, last = near_of(neighbours, window, held, fetches, i, cluster)
        near[cluster, :steps, :] = x
        carry[cluster] = last[:1]
    inner_copy.wait()
    for i in range(inner.shape[0]):
        carry[REACH + i] = near[REACH + i, steps : steps + 1, :]
    rows_copy.wait()
    w = jnp.transpose(rows[...], (1, 0, 2))
    for p in range(maps.shape[0]):
        x = jnp.concatenate([w[2 * p], w[2 * p + 1]], axis=1)
        maps[p] = jnp.concatenate([x, x], axis=0)


def outer_near(neighbours, window, from_pair, from_other, blocks, inner, from_moments):
    steps, unknowns = window.shape[1:]
    lags, clusters, nb = blocks.shape[:3]
    terms = from_moments.shape[0]
    order = tuple(range(REACH)) + tuple(range(clusters - REACH, clusters))
    count = len(order)
    return pl.pallas_call(
        functools.partial(outer_kernel, order),
        in_specs=[SMEM, VMEM] + [HBM] * 5,
        out_specs=[VMEM] * 4,
        out_shape=[
            jax.ShapeDtypeStruct((clusters, steps + 8, unknowns), F32),
            jax.ShapeDtypeStruct((clusters, 1, unknowns), F32),
            jax.ShapeDtypeStruct((clusters // 2, 2 * terms, 2 * unknowns), BF16),
            jax.ShapeDtypeStruct(window.shape, BF16),
        ],
        scratch_shapes=[
            pltpu.VMEM((lags, count, nb, unknowns, unknowns), BF16),
            pltpu.VMEM(from_moments.shape, BF16),
            pltpu.SemaphoreType.DMA((lags, count)),
            pltpu.SemaphoreType.DMA((4,)),
        ],
        input_output_aliases={1: 3},
        compiler_params=pltpu.CompilerParams(vmem_limit_bytes=14 << 20),
        name="outer",
    )(
        neighbours,
        window,
        in_hbm(from_pair),
        in_hbm(from_other),
        in_hbm(blocks),
        in_hbm(inner),
        in_hbm(from_moments),
    )


def final_kernel(near, carry, *refs):
    parts = refs[:4]
    maps, live, out, major, done, sems = refs[4:]
    steps, clusters, unknowns = out.shape
    terms = maps.shape[1] // 2
    first = lax.axis_index("space") * clusters
    total = parts[0][...].astype(F32)
    for part in parts[1:]:
        total = total + part[...].astype(F32)
    lane = lax.broadcasted_iota(jnp.int32, total.shape, 1)
    size = steps // 2
    chunk = 32
    row = lax.broadcasted_iota(jnp.int32, (8, unknowns), 0)
    copies = []
    for half in range(2):
        mine = jnp.where(lane // terms == half, total, 0.0).astype(BF16)
        here = pl.ds(half * size, size)
        alive = live[here, :]
        for p in range(clusters // 2):
            both = jnp.dot(mine, maps[p], preferred_element_type=F32)
            for q in range(2):
                c = 2 * p + q
                x = both[:, q * unknowns : (q + 1) * unknowns] + near[c, here, :]
                if half == 0:
                    head = jnp.where(row == 0, jnp.broadcast_to(carry[c], row.shape), 0.0)
                    x = jnp.concatenate([x[:8] + head, x[8:]], axis=0)
                major[c] = jnp.where(alive > first + c, x, 0.0).astype(BF16)
        for i in range(size // chunk):
            at = half * size + i * chunk
            done[pl.ds(at, chunk)] = jnp.transpose(major[:, pl.ds(i * chunk, chunk), :], (1, 0, 2))
            copies.append(
                pltpu.make_async_copy(
                    done.at[pl.ds(at, chunk)], out.at[pl.ds(at, chunk)], sems.at[at // chunk]
                )
            )
            copies[-1].start()
    for copy in copies:
        copy.wait()


def final(near, carry, parts, maps, live):
    steps, unknowns = live.shape
    clusters = near.shape[0]
    return pl.pallas_call(
        final_kernel,
        in_specs=[VMEM] * (4 + len(parts)),
        out_specs=HBM,
        out_shape=jax.ShapeDtypeStruct((steps, clusters, unknowns), BF16),
        scratch_shapes=[
            pltpu.VMEM((clusters, steps // 2, unknowns), BF16),
            pltpu.VMEM((steps, clusters, unknowns), BF16),
            pltpu.SemaphoreType.DMA((steps // 32,)),
        ],
        compiler_params=pltpu.CompilerParams(vmem_limit_bytes=10 << 20),
        name="final",
    )(near, carry, *parts, maps, live)


def exchanged(x, axis):
    return lax.all_to_all(x, axis, split_axis=0, concat_axis=0, tiled=True)


def swapped_from(x, axis, start):
    count = lax.axis_size(axis)
    route = []
    for i in range(start, count - 1, 2):
        route += [(i, i + 1), (i + 1, i)]
    return lax.ppermute(x, axis, route)


def from_chip(x, axis, distance):
    count = lax.axis_size(axis)
    return lax.ppermute(x, axis, [(i, (i + 2 * distance) % count) for i in range(count)])


def passed_on(x, axis):
    count = lax.axis_size(axis)
    return lax.ppermute(x, axis, [(i, i + 1) for i in range(count - 1)])


def local(density, active, neighbours, near_blocks, to_moments, from_moments, decay_rates, lengths):
    steps = density.shape[0]
    slabs, chips = lax.axis_size("tm"), lax.axis_size("space") // 2
    window, pair, other, far, decay, ends, live = prep(
        density,
        active.reshape(1, steps),
        to_moments,
        decay_rates.reshape(1, -1),
        lengths.reshape(1, steps),
        slabs,
    )
    ends = exchanged(ends, "tm")
    from_pair = swapped_from(pair, "space", 0)
    from_other = swapped_from(other, "space", 1)
    neighbours = neighbours.T
    inner = inner_near(neighbours, window, near_blocks)
    ends, inner = lax.optimization_barrier((ends, inner))
    mine = arrive(ends, far, decay)
    mine = pair_sum(mine, swapped_from(mine, "space", 0))
    parts = [mine] + [from_chip(mine, "space", d) for d in range(1, chips)]
    inner, mine = lax.optimization_barrier((inner, mine))
    near, carry, maps, _ = outer_near(
        neighbours, window, from_pair, from_other, near_blocks, inner, from_moments
    )
    carry = passed_on(carry, "tm")
    return final(near, carry, parts, maps, live)


def solution(mesh):
    placed = (
        P("tm", "space", None),
        P("tm"),
        P("space", None),
        P(None, "space", None, None, None),
        P(None, "space", None),
        P(None, "space", None),
        P(),
        P("tm"),
    )
    return jax.shard_map(
        local, mesh=mesh, in_specs=placed, out_specs=P("tm", "space", None), check_vma=False
    )
```

time: 99.1 us -> 57.9 us (0.58)
  the two profiles are of different devices: /device:TPU:1 before, /device:TPU:32 now
where the time goes in v2:
time: 57.9 us; the launch traced here: 57.6 us
  Pallas kernels  26.7 us (46%)
  starting transfers between devices  23.5 us (41%)
  waiting for transfers between devices  5.25 us (9%)
  local copies, waits for them, and re-layouts  1.96 us (3%)
    pallas_call x1, Pallas kernels, outer_near(): pl.pallas_call(functools.partial(outer_kernel, order), in_specs=[SMEM, VM...  11.6 us
    all_to_all x1, starting transfers between devices, exchanged(): return lax.all_to_all(x, axis, split_axis=0, concat_axis=0, tiled=True)  11.4 us
    pallas_call x1, Pallas kernels, inner_near(): pl.pallas_call(functools.partial(inner_kernel, order), in_specs=[SMEM, VM...  9.5 us
    ppermute x3, starting transfers between devices, from_chip(): lax.ppermute(x, axis, [(i, (i + 2 * distance) % count) for i in range(cou...  5.71 us
    ppermute x1, waiting for transfers between devices, passed_on(): return lax.ppermute(x, axis, [(i, i + 1) for i in range(count - 1)])  4.33 us
    ppermute x1, starting transfers between devices, passed_on(): return lax.ppermute(x, axis, [(i, i + 1) for i in range(count - 1)])  3.37 us
    ppermute x3, starting transfers between devices, swapped_from(): return lax.ppermute(x, axis, route)  3.05 us
    pallas_call x1, Pallas kernels, prep(): pl.pallas_call(prep_kernel, in_specs=[HBM] * 5, out_specs=[VMEM, HBM, HBM...  2.81 us
  transfers between devices with their start and end apart: 8, of which 2 were waited for; matrix products, arithmetic and copies ran while one was open for 0% of the time, Pallas kernels for 37%

profile of v2, /device:TPU:32, one launch (start us, length us, event | category | flops | bytes accessed | tf_op | source)
XLA Modules:
  0.0 57.6 jit_solution(11802891654024648490)
XLA Ops:
  0.0 2.8 %prep.1 = (bf16[48,256,128]{2,1,0:T(8,128)(2,1)S(1)}, bf16[8,256,128]{2,1,0:T(8,128)(2,1)}, bf16[8,256,128]{2,1,0:T(8,128)(2,1)}, f32[256,128]{1,0:T(8,128)S(1)}...) custom-call(bf16[256,32,128]{2,1,0:T(8,128)(2,1)} %density.1, s32[1,256]{1,0:T(1,128)} %bitcast.6, ...), custom_call_target="tpu_custom_call" | custom-call | tf_op jit(solution)/shard_map/prep/pallas_call | solution.py:156
  2.8 0.0 copy-start.2
  2.8 0.6 %copy-done.2 = f32[32,1,128]{2,1,0:T(1,128)} copy-done((f32[32,1,128]{2,1,0:T(1,128)}, f32[32,1,128]{2,1,0:T(1,128)S(1)}, u32[]{:S(2)}) %copy-start.2) | copy-done | bytes 16408
  3.4 0.0 collective-permute-start
  3.4 1.5 %collective-permute-start.1 = (bf16[8,256,128]{2,1,0:T(8,128)(2,1)}, bf16[8,256,128]{2,1,0:T(8,128)(2,1)}, u32[]{:S(2)}, u32[]{:S(2)}) collective-permute-start(bf16[8,256,128]{2,1,0:T(8,128)(2,1)} %get-tuple-element.20), channel_id=1, source_target_pairs={{1,2},{2,1},{3,4},{4,3},{5,6},{6,5},{9,10},{10,9},{11,12},{12,11},... | collective-permute-start | bytes 1572872 | tf_op jit(solution)/shard_map/ppermute | solution.py:450
  4.9 11.4 %all-to-all-start = ((f32[32,1,128]{2,1,0:T(1,128)}), f32[32,1,128]{2,1,0:T(1,128)S(1)}, u32[]{:S(2)}, u32[]{:S(2)}) async-start(f32[32,1,128]{2,1,0:T(1,128)} %copy-done.2), calls=%async_computation | async-start | bytes 32768 | tf_op jit(solution)/shard_map/all_to_all | solution.py:442
  16.2 0.0 copy-start
  16.2 0.7 %copy-done = s32[32,8]{0,1:T(8,128)S(1)} copy-done((s32[32,8]{0,1:T(8,128)S(1)}, s32[32,8]{0,1:T(8,128)}, u32[]{:S(2)}) %copy-start) | copy-done | bytes 1048
  16.9 9.5 %inner.1 = f32[16,264,128]{2,1,0:T(8,128)} custom-call(s32[8,32]{1,0:T(8,128)S(1)} %bitcast.4, bf16[48,256,128]{2,1,0:T(8,128)(2,1)S(1)} %get-tuple-element.18.window.window_in, bf16[2,32,8,128,128]{4,3,2,1,0:T(8,128)(2,1)} %blocks.3), custom_call_target="tpu_custom_call" | custom-call | tf_op jit(solution)/shard_map/inner/pallas_call | solution.py:275
  26.4 0.0 all-to-all-done.ends
  26.4 0.2 arrive.1.a
  26.6 1.6 %collective-permute-start.2 = (f32[128,128]{1,0:T(8,128)S(1)}, f32[128,128]{1,0:T(8,128)S(1)}, u32[]{:S(2)}, u32[]{:S(2)}) collective-permute-start(f32[128,128]{1,0:T(8,128)S(1)} %arrive.1.a), channel_id=1, source_target_pairs={{0,1},{1,0},{2,3},{3,2},{4,5},{5,4},{6,7},{7,6},{8,9},{9,8},{10,11... | collective-permute-start | bytes 196616 | tf_op jit(solution)/shard_map/ppermute | solution.py:450
  28.2 0.9 %collective-permute-done.2.b = f32[128,128]{1,0:T(8,128)S(1)} collective-permute-done((f32[128,128]{1,0:T(8,128)S(1)}, f32[128,128]{1,0:T(8,128)S(1)}, u32[]{:S(2)}, u32[]{:S(2)}) %collective-permute-start.2) | collective-permute-done | bytes 65568 | tf_op jit(solution)/shard_map/ppermute | solution.py:450
  29.1 1.6 %collective-permute-start.4 = (bf16[128,128]{1,0:T(8,128)(2,1)S(1)}, bf16[128,128]{1,0:T(8,128)(2,1)S(1)}, u32[]{:S(2)}, u32[]{:S(2)}) collective-permute-start(bf16[128,128]{1,0:T(8,128)(2,1)S(1)} %pair_sum.1.refs_0_), channel_id=1, source_target_pairs={{0,2},{1,3},{2,4},{3,5},{4,6},{5,7},{6,0},{7,1},{8,10},{9,11},{10,... | collective-permute-start | bytes 98312 | tf_op jit(solution)/shard_map/ppermute | solution.py:455
  30.7 3.0 %collective-permute-start.5 = (bf16[128,128]{1,0:T(8,128)(2,1)S(1)}, bf16[128,128]{1,0:T(8,128)(2,1)S(1)}, u32[]{:S(2)}, u32[]{:S(2)}) collective-permute-start(bf16[128,128]{1,0:T(8,128)(2,1)S(1)} %pair_sum.1.refs_0_), channel_id=1, source_target_pairs={{0,4},{1,5},{2,6},{3,7},{4,0},{5,1},{6,2},{7,3},{8,12},{9,13},{10,... | collective-permute-start | bytes 98312 | tf_op jit(solution)/shard_map/ppermute | solution.py:455
  33.7 1.2 %collective-permute-start.6 = (bf16[128,128]{1,0:T(8,128)(2,1)S(1)}, bf16[128,128]{1,0:T(8,128)(2,1)S(1)}, u32[]{:S(2)}, u32[]{:S(2)}) collective-permute-start(bf16[128,128]{1,0:T(8,128)(2,1)S(1)} %pair_sum.1.refs_0_), channel_id=1, source_target_pairs={{0,6},{1,7},{2,0},{3,1},{4,2},{5,3},{6,4},{7,5},{8,14},{9,15},{10,... | collective-permute-start | bytes 98312 | tf_op jit(solution)/shard_map/ppermute | solution.py:455
  34.8 0.0 collective-permute-done.from_pair
  34.8 0.0 collective-permute-done.1.from_other
  34.8 0.0 copy-start.1
  34.8 0.7 %copy-done.1 = s32[32,8]{0,1:T(8,128)S(1)} copy-done((s32[32,8]{0,1:T(8,128)S(1)}, s32[32,8]{0,1:T(8,128)}, u32[]{:S(2)}) %copy-start.1) | copy-done | bytes 1048
  35.5 11.6 %outer.1 = (f32[32,264,128]{2,1,0:T(8,128)S(1)}, f32[32,1,128]{2,1,0:T(1,128)S(1)}, bf16[16,128,256]{2,1,0:T(8,128)(2,1)S(1)}, bf16[48,256,128]{2,1,0:T(8,128)(2,1)S(1)}) custom-call(s32[8,32]{1,0:T(8,128)S(1)} %bitcast.5, bf16[48,256,128]{2,1,0:T(8,128)(2,1)S(1)} %get-tuple-element.18.window.window_in, ...), custom_call_target="tpu_custom_call", output_to_operand_aliasing={{3}: (1, {})} | custom-call | tf_op jit(solution)/shard_map/outer/pallas_call | solution.py:353
  47.1 3.4 %collective-permute-start.3 = (f32[32,1,128]{2,1,0:T(1,128)S(1)}, f32[32,1,128]{2,1,0:T(1,128)S(1)}, u32[]{:S(2)}, u32[]{:S(2)}) collective-permute-start(f32[32,1,128]{2,1,0:T(1,128)S(1)} %get-tuple-element.28), channel_id=1, source_target_pairs={{0,8},{8,16},{16,24},{24,32},{32,40},{40,48},{48,56},{56,64},{64,7... | collective-permute-start | bytes 49160 | tf_op jit(solution)/shard_map/ppermute | solution.py:460
  50.5 0.0 collective-permute-done.4.refs_1_
  50.5 0.0 collective-permute-done.5.refs_2_
  50.5 0.0 collective-permute-done.6.refs_3_
  50.5 4.3 %collective-permute-done.3.carry = f32[32,1,128]{2,1,0:T(1,128)S(1)} collective-permute-done((f32[32,1,128]{2,1,0:T(1,128)S(1)}, f32[32,1,128]{2,1,0:T(1,128)S(1)}, u32[]{:S(2)}, u32[]{:S(2)}) %collective-permute-start.3) | collective-permute-done | bytes 16416 | tf_op jit(solution)/shard_map/ppermute | solution.py:460
  54.8 2.6 %final.1 = bf16[256,32,128]{2,1,0:T(8,128)(2,1)} custom-call(f32[32,264,128]{2,1,0:T(8,128)S(1)} %get-tuple-element.27.near, f32[32,1,128]{2,1,0:T(1,128)S(1)} %collective-permute-done.3.carry, bf16[128,128]{1,0:T(8,128)(2,1)S(1)} %pair_sum.1.refs_0_, bf16[128,128]{1,0:T(8,128)(2,1)S(1)} %collective-permute-done.4.refs_1_, ...), custom_call_target="tpu_custom_call" | custom-call | tf_op jit(solution)/shard_map/final/pallas_call | solution.py:426
  (1 shorter events, 0.0 us)
Async XLA Ops:
  2.8 0.6 %copy-start.2 = (f32[32,1,128]{2,1,0:T(1,128)}, f32[32,1,128]{2,1,0:T(1,128)S(1)}, u32[]{:S(2)}) copy-start(f32[32,1,128]{2,1,0:T(1,128)S(1)} %get-tuple-element.21) | copy-start | bytes 49156
  3.4 31.4 %collective-permute-start = (bf16[8,256,128]{2,1,0:T(8,128)(2,1)}, bf16[8,256,128]{2,1,0:T(8,128)(2,1)}, u32[]{:S(2)}, u32[]{:S(2)}) collective-permute-start(bf16[8,256,128]{2,1,0:T(8,128)(2,1)} %get-tuple-element.19), channel_id=1, source_target_pairs={{0,1},{1,0},{2,3},{3,2},{4,5},{5,4},{6,7},{7,6},{8,9},{9,8},{10,11... | collective-permute-start | bytes 1572872 | tf_op jit(solution)/shard_map/ppermute | solution.py:450
  3.4 31.4 %collective-permute-start.1 = (bf16[8,256,128]{2,1,0:T(8,128)(2,1)}, bf16[8,256,128]{2,1,0:T(8,128)(2,1)}, u32[]{:S(2)}, u32[]{:S(2)}) collective-permute-start(bf16[8,256,128]{2,1,0:T(8,128)(2,1)} %get-tuple-element.20), channel_id=1, source_target_pairs={{1,2},{2,1},{3,4},{4,3},{5,6},{6,5},{9,10},{10,9},{11,12},{12,11},... | collective-permute-start | bytes 1572872 | tf_op jit(solution)/shard_map/ppermute | solution.py:450
  4.9 21.6 %all-to-all-start = ((f32[32,1,128]{2,1,0:T(1,128)}), f32[32,1,128]{2,1,0:T(1,128)S(1)}, u32[]{:S(2)}, u32[]{:S(2)}) async-start(f32[32,1,128]{2,1,0:T(1,128)} %copy-done.2), calls=%async_computation | async-start | bytes 32768 | tf_op jit(solution)/shard_map/all_to_all | solution.py:442
  16.2 0.7 %copy-start = (s32[32,8]{0,1:T(8,128)S(1)}, s32[32,8]{0,1:T(8,128)}, u32[]{:S(2)}) copy-start(s32[32,8]{0,1:T(8,128)} %param.10) | copy-start | bytes 3076
  26.6 2.5 %collective-permute-start.2 = (f32[128,128]{1,0:T(8,128)S(1)}, f32[128,128]{1,0:T(8,128)S(1)}, u32[]{:S(2)}, u32[]{:S(2)}) collective-permute-start(f32[128,128]{1,0:T(8,128)S(1)} %arrive.1.a), channel_id=1, source_target_pairs={{0,1},{1,0},{2,3},{3,2},{4,5},{5,4},{6,7},{7,6},{8,9},{9,8},{10,11... | collective-permute-start | bytes 196616 | tf_op jit(solution)/shard_map/ppermute | solution.py:450
  29.1 21.4 %collective-permute-start.4 = (bf16[128,128]{1,0:T(8,128)(2,1)S(1)}, bf16[128,128]{1,0:T(8,128)(2,1)S(1)}, u32[]{:S(2)}, u32[]{:S(2)}) collective-permute-start(bf16[128,128]{1,0:T(8,128)(2,1)S(1)} %pair_sum.1.refs_0_), channel_id=1, source_target_pairs={{0,2},{1,3},{2,4},{3,5},{4,6},{5,7},{6,0},{7,1},{8,10},{9,11},{10,... | collective-permute-start | bytes 98312 | tf_op jit(solution)/shard_map/ppermute | solution.py:455
  30.7 19.8 %collective-permute-start.5 = (bf16[128,128]{1,0:T(8,128)(2,1)S(1)}, bf16[128,128]{1,0:T(8,128)(2,1)S(1)}, u32[]{:S(2)}, u32[]{:S(2)}) collective-permute-start(bf16[128,128]{1,0:T(8,128)(2,1)S(1)} %pair_sum.1.refs_0_), channel_id=1, source_target_pairs={{0,4},{1,5},{2,6},{3,7},{4,0},{5,1},{6,2},{7,3},{8,12},{9,13},{10,... | collective-permute-start | bytes 98312 | tf_op jit(solution)/shard_map/ppermute | solution.py:455
  33.7 16.8 %collective-permute-start.6 = (bf16[128,128]{1,0:T(8,128)(2,1)S(1)}, bf16[128,128]{1,0:T(8,128)(2,1)S(1)}, u32[]{:S(2)}, u32[]{:S(2)}) collective-permute-start(bf16[128,128]{1,0:T(8,128)(2,1)S(1)} %pair_sum.1.refs_0_), channel_id=1, source_target_pairs={{0,6},{1,7},{2,0},{3,1},{4,2},{5,3},{6,4},{7,5},{8,14},{9,15},{10,... | collective-permute-start | bytes 98312 | tf_op jit(solution)/shard_map/ppermute | solution.py:455
  34.8 0.7 %copy-start.1 = (s32[32,8]{0,1:T(8,128)S(1)}, s32[32,8]{0,1:T(8,128)}, u32[]{:S(2)}) copy-start(s32[32,8]{0,1:T(8,128)} %param.10) | copy-start | bytes 3076
  47.1 7.7 %collective-permute-start.3 = (f32[32,1,128]{2,1,0:T(1,128)S(1)}, f32[32,1,128]{2,1,0:T(1,128)S(1)}, u32[]{:S(2)}, u32[]{:S(2)}) collective-permute-start(f32[32,1,128]{2,1,0:T(1,128)S(1)} %get-tuple-element.28), channel_id=1, source_target_pairs={{0,8},{8,16},{16,24},{24,32},{32,40},{40,48},{48,56},{56,64},{64,7... | collective-permute-start | bytes 49160 | tf_op jit(solution)/shard_map/ppermute | solution.py:460

commit v3 on v2

--- a/solution.py
+++ b/solution.py
@@ -12,7 +12,6 @@
 BF16 = jnp.bfloat16
 HBM = pl.BlockSpec(memory_space=pltpu.HBM)
 VMEM = pl.BlockSpec(memory_space=pltpu.VMEM)
-SMEM = pl.BlockSpec(memory_space=pltpu.SMEM)
 
 
 def in_hbm(x):
@@ -63,6 +62,7 @@
     rates_row,
     lengths_row,
     flat,
+    lines,
     sems,
 ):
     steps, clusters, unknowns = density.shape
@@ -140,7 +140,9 @@
     lane = lax.broadcasted_iota(jnp.int32, (1, 2 * terms), 1)
     line = jnp.where(lane < terms, total[steps - 1 :], d[steps - 1 :])
     for k in range(ends.shape[0]):
-        ends[k] = line
+        lines[k] = line
+    sides.append(copy(lines, ends, 10))
+    sides[-1].start()
     scale = jnp.sqrt(2.0 * doubled(rates_row[...]))
     far[...] = shifted_down(total, 1, 0.0) * scale
     decay[...] = shifted_down(d, 1, 1.0) * scale
@@ -156,14 +158,14 @@
     return pl.pallas_call(
         prep_kernel,
         in_specs=[HBM] * 5,
-        out_specs=[VMEM, HBM, HBM] + [VMEM] * 4,
+        out_specs=[VMEM, HBM, HBM, VMEM, VMEM, HBM, VMEM],
         out_shape=[
             jax.ShapeDtypeStruct((clusters + 2 * REACH, steps, unknowns), BF16),
             side,
             side,
             jax.ShapeDtypeStruct((steps, lanes), F32),
             jax.ShapeDtypeStruct((steps, lanes), F32),
-            jax.ShapeDtypeStruct((slabs, 1, lanes), F32),
+            pltpu.HBM((slabs, 1, lanes), F32),
             jax.ShapeDtypeStruct((steps, unknowns), jnp.int32),
         ],
         scratch_shapes=[
@@ -173,7 +175,8 @@
             pltpu.VMEM(rates.shape, F32),
             pltpu.VMEM(lengths.shape, F32),
             pltpu.VMEM((32 * (clusters + 1) + 7, unknowns), F32),
-            pltpu.SemaphoreType.DMA((10,)),
+            pltpu.VMEM((slabs, 1, lanes), F32),
+            pltpu.SemaphoreType.DMA((11,)),
         ],
         compiler_params=pltpu.CompilerParams(vmem_limit_bytes=10 << 20),
         name="prep",
@@ -206,6 +209,9 @@
         out_specs=VMEM,
         out_shape=jax.ShapeDtypeStruct((steps // 2, lanes), F32),
         compiler_params=pltpu.CompilerParams(vmem_limit_bytes=4 << 20),
+        cost_estimate=pl.CostEstimate(
+            flops=10_000_000_000, bytes_accessed=1 << 20, transcendentals=0
+        ),
         name="arrive",
     )(ends, far, decay)
 
@@ -225,162 +231,226 @@
     )(a, b)
 
 
-def near_fetches(blocks, held, sems, order):
-    return [
+def gathered(neighbours, window, cluster, rows):
+    base = lax.axis_index("space") * neighbours.shape[1] - REACH
+    return jnp.concatenate(
+        [window[neighbours[j, cluster] - base, rows, :] for j in range(neighbours.shape[0])], axis=1
+    )
+
+
+def stacked(block):
+    nb, unknowns, width = block.shape
+    return block[...].reshape(nb * unknowns, width)
+
+
+def near_of(neighbours, window, blocks, cluster):
+    steps = window.shape[1]
+    x = gathered(neighbours, window, cluster, pl.ds(0, steps))
+    w = jnp.concatenate([stacked(block) for block in blocks], axis=1)
+    both = jnp.dot(x, w, preferred_element_type=F32)
+    now, later = jnp.split(both, 2, axis=1)
+    return now + shifted_down(later, 1, 0.0), later[steps - 1 :]
+
+
+def inner_kernel(
+    full,
+    ends_only,
+    table,
+    window,
+    blocks,
+    near,
+    carry,
+    neighbours,
+    held,
+    held_later,
+    found,
+    lines,
+    sems,
+    later_sems,
+    out_sems,
+):
+    count = len(full)
+    steps = window.shape[1]
+    lags = blocks.shape[0]
+    fetches = [
         [
             pltpu.make_async_copy(blocks.at[lag, c], held.at[lag, i], sems.at[lag, i])
-            for lag in range(blocks.shape[0])
+            for lag in range(lags)
         ]
-        for i, c in enumerate(order)
-    ]
-
-
-def near_of(neighbours, window, held, fetches, i, cluster):
-    lags, _, nb, unknowns, _ = held.shape
-    base = lax.axis_index("space") * neighbours.shape[1] - REACH
-    for fetch in fetches[i]:
-        fetch.wait()
-    x = jnp.concatenate([window[neighbours[j, cluster] - base] for j in range(nb)], axis=1)
-    w = jnp.concatenate(
-        [held[lag, i].reshape(nb * unknowns, unknowns) for lag in range(lags)], axis=1
-    )
-    both = jnp.dot(x, w, preferred_element_type=F32)
-    now, later = both[:, :unknowns], both[:, unknowns:]
-    last = pltpu.roll(later[later.shape[0] - 8 :], 1, 0)
-    return now + shifted_down(later, 1, 0.0), last
-
-
-def inner_kernel(order, neighbours, window, blocks, near, held, found, sems, out_sems):
-    steps = window.shape[1]
-    fetches = near_fetches(blocks, held, sems, order)
+        for i, c in enumerate(full)
+    ]
+    later_fetches = [
+        pltpu.make_async_copy(blocks.at[lags - 1, c], held_later.at[i], later_sems.at[i])
+        for i, c in enumerate(ends_only)
+    ]
+    listed = pltpu.make_async_copy(table, neighbours, out_sems.at[count + 1])
+    listed.start()
     for some in fetches:
         for fetch in some:
             fetch.start()
+    for fetch in later_fetches:
+        fetch.start()
+    listed.wait()
     stores = []
-    for i, cluster in enumerate(order):
-        x, last = near_of(neighbours, window, held, fetches, i, cluster)
-        found[i, :steps, :] = x
-        found[i, steps:, :] = last
+    for i, cluster in enumerate(full):
+        for fetch in fetches[i]:
+            fetch.wait()
+        blocks_here = [held.at[lag, i] for lag in range(lags)]
+        x, last = near_of(neighbours, window, blocks_here, cluster)
+        found[i] = x
+        lines[cluster - REACH] = last
         stores.append(pltpu.make_async_copy(found.at[i], near.at[i], out_sems.at[i]))
         stores[-1].start()
+    for i, cluster in enumerate(ends_only):
+        later_fetches[i].wait()
+        x = gathered(neighbours, window, cluster, pl.ds(steps - 16, 16))
+        y = jnp.dot(x, stacked(held_later.at[i]), preferred_element_type=F32)
+        lines[cluster - REACH] = y[15:]
+    stores.append(pltpu.make_async_copy(lines, carry, out_sems.at[count]))
+    stores[-1].start()
     for store in stores:
         store.wait()
 
 
-def inner_near(neighbours, window, blocks):
+def inner_near(neighbours, window, blocks, full, ends_only):
     steps, unknowns = window.shape[1:]
     lags, clusters, nb = blocks.shape[:3]
-    order = tuple(range(REACH, clusters - REACH))
-    count = len(order)
-    return pl.pallas_call(
-        functools.partial(inner_kernel, order),
-        in_specs=[SMEM, VMEM, HBM],
-        out_specs=HBM,
-        out_shape=pltpu.HBM((count, steps + 8, unknowns), F32),
+    count, more = len(full), len(ends_only)
+    block = (nb, unknowns, unknowns)
+    return pl.pallas_call(
+        functools.partial(inner_kernel, full, ends_only),
+        in_specs=[HBM, VMEM, HBM],
+        out_specs=[HBM] * 2,
+        out_shape=[
+            pltpu.HBM((count, steps, unknowns), F32),
+            pltpu.HBM((count + more, 1, unknowns), F32),
+        ],
         scratch_shapes=[
-            pltpu.VMEM((lags, count, nb, unknowns, unknowns), BF16),
-            pltpu.VMEM((count, steps + 8, unknowns), F32),
+            pltpu.SMEM(neighbours.shape, jnp.int32),
+            pltpu.VMEM((lags, count, *block), BF16),
+            pltpu.VMEM((more, *block), BF16),
+            pltpu.VMEM((count, steps, unknowns), F32),
+            pltpu.VMEM((count + more, 1, unknowns), F32),
             pltpu.SemaphoreType.DMA((lags, count)),
-            pltpu.SemaphoreType.DMA((count,)),
+            pltpu.SemaphoreType.DMA((more,)),
+            pltpu.SemaphoreType.DMA((count + 2,)),
         ],
         compiler_params=pltpu.CompilerParams(vmem_limit_bytes=16 << 20),
         name="inner",
-    )(neighbours, window, in_hbm(blocks))
-
-
-def outer_kernel(
+    )(in_hbm(neighbours), window, in_hbm(blocks))
+
+
+def edge_kernel(
     order,
-    neighbours,
+    table,
     window_in,
     from_pair,
     from_other,
     blocks,
-    inner,
-    from_moments,
+    inner_carry,
     near,
     carry,
-    maps,
     window,
-    held,
-    rows,
+    neighbours,
     sems,
-    side_sems,
 ):
     del window_in
-    steps = window.shape[1]
     even = is_even()
     above = window.shape[0] - REACH
 
     def copy(src, dst, k):
-        return pltpu.make_async_copy(src, dst, side_sems.at[k])
+        return pltpu.make_async_copy(src, dst, sems.at[k])
 
     sides = [
         copy(from_pair, window.at[pl.ds(jnp.where(even, above, 0), REACH)], 0),
         copy(from_other, window.at[pl.ds(jnp.where(even, 0, above), REACH)], 1),
-    ]
-    inner_copy = copy(inner, near.at[pl.ds(REACH, inner.shape[0])], 2)
-    rows_copy = copy(from_moments, rows, 3)
-    fetches = near_fetches(blocks, held, sems, order)
+        copy(inner_carry, carry.at[pl.ds(REACH, inner_carry.shape[0])], 2),
+        copy(table, neighbours, 3),
+    ]
     for c in sides:
         c.start()
-    for some in fetches:
-        for fetch in some:
-            fetch.start()
-    inner_copy.start()
-    rows_copy.start()
     for c in sides:
         c.wait()
     for i, cluster in enumerate(order):
-        x, last = near_of(neighbours, window, held, fetches, i, cluster)
-        near[cluster, :steps, :] = x
-        carry[cluster] = last[:1]
-    inner_copy.wait()
-    for i in range(inner.shape[0]):
-        carry[REACH + i] = near[REACH + i, steps : steps + 1, :]
-    rows_copy.wait()
+        blocks_here = [blocks.at[lag, cluster] for lag in range(blocks.shape[0])]
+        near[i], carry[cluster] = near_of(neighbours, window, blocks_here, cluster)
+
+
+def edge_near(neighbours, window, from_pair, from_other, blocks, inner_carry, order):
+    steps, unknowns = window.shape[1:]
+    clusters = blocks.shape[1]
+    return pl.pallas_call(
+        functools.partial(edge_kernel, order),
+        in_specs=[HBM, VMEM, HBM, HBM, VMEM, HBM],
+        out_specs=[VMEM] * 3,
+        out_shape=[
+            jax.ShapeDtypeStruct((len(order), steps, unknowns), F32),
+            jax.ShapeDtypeStruct((clusters, 1, unknowns), F32),
+            jax.ShapeDtypeStruct(window.shape, BF16),
+        ],
+        scratch_shapes=[
+            pltpu.SMEM(neighbours.shape, jnp.int32),
+            pltpu.SemaphoreType.DMA((4,)),
+        ],
+        input_output_aliases={1: 2},
+        compiler_params=pltpu.CompilerParams(vmem_limit_bytes=8 << 20),
+        name="edge",
+    )(
+        in_hbm(neighbours),
+        window,
+        in_hbm(from_pair),
+        in_hbm(from_other),
+        in_vmem(blocks),
+        in_hbm(inner_carry),
+    )
+
+
+def rest_kernel(
+    order, table, window, blocks, inner, from_moments, near, maps, neighbours, rows, sems
+):
+    listed = pltpu.make_async_copy(table, neighbours, sems.at[2])
+    listed.start()
+    fetches = [
+        pltpu.make_async_copy(from_moments, rows, sems.at[0]),
+        pltpu.make_async_copy(inner, near.at[pl.ds(len(order), inner.shape[0])], sems.at[1]),
+    ]
+    for fetch in fetches:
+        fetch.start()
+    listed.wait()
+    for i, cluster in enumerate(order):
+        blocks_here = [blocks.at[lag, cluster] for lag in range(blocks.shape[0])]
+        near[i], _ = near_of(neighbours, window, blocks_here, cluster)
+    fetches[0].wait()
     w = jnp.transpose(rows[...], (1, 0, 2))
     for p in range(maps.shape[0]):
         x = jnp.concatenate([w[2 * p], w[2 * p + 1]], axis=1)
         maps[p] = jnp.concatenate([x, x], axis=0)
-
-
-def outer_near(neighbours, window, from_pair, from_other, blocks, inner, from_moments):
+    fetches[1].wait()
+
+
+def rest_near(neighbours, window, blocks, inner, from_moments, order):
     steps, unknowns = window.shape[1:]
-    lags, clusters, nb = blocks.shape[:3]
+    clusters = blocks.shape[1]
     terms = from_moments.shape[0]
-    order = tuple(range(REACH)) + tuple(range(clusters - REACH, clusters))
-    count = len(order)
-    return pl.pallas_call(
-        functools.partial(outer_kernel, order),
-        in_specs=[SMEM, VMEM] + [HBM] * 5,
-        out_specs=[VMEM] * 4,
+    return pl.pallas_call(
+        functools.partial(rest_kernel, order),
+        in_specs=[HBM, VMEM, VMEM, HBM, HBM],
+        out_specs=[VMEM] * 2,
         out_shape=[
-            jax.ShapeDtypeStruct((clusters, steps + 8, unknowns), F32),
-            jax.ShapeDtypeStruct((clusters, 1, unknowns), F32),
+            jax.ShapeDtypeStruct((len(order) + inner.shape[0], steps, unknowns), F32),
             jax.ShapeDtypeStruct((clusters // 2, 2 * terms, 2 * unknowns), BF16),
-            jax.ShapeDtypeStruct(window.shape, BF16),
         ],
         scratch_shapes=[
-            pltpu.VMEM((lags, count, nb, unknowns, unknowns), BF16),
+            pltpu.SMEM(neighbours.shape, jnp.int32),
             pltpu.VMEM(from_moments.shape, BF16),
-            pltpu.SemaphoreType.DMA((lags, count)),
-            pltpu.SemaphoreType.DMA((4,)),
-        ],
-        input_output_aliases={1: 3},
-        compiler_params=pltpu.CompilerParams(vmem_limit_bytes=14 << 20),
-        name="outer",
-    )(
-        neighbours,
-        window,
-        in_hbm(from_pair),
-        in_hbm(from_other),
-        in_hbm(blocks),
-        in_hbm(inner),
-        in_hbm(from_moments),
-    )
-
-
-def final_kernel(near, carry, *refs):
+            pltpu.SemaphoreType.DMA((3,)),
+        ],
+        compiler_params=pltpu.CompilerParams(vmem_limit_bytes=8 << 20),
+        name="rest",
+    )(in_hbm(neighbours), window, in_vmem(blocks), in_hbm(inner), in_hbm(from_moments))
+
+
+def final_kernel(places, edge, rest, carry, *refs):
     parts = refs[:4]
     maps, live, out, major, done, sems = refs[4:]
     steps, clusters, unknowns = out.shape
@@ -402,30 +472,32 @@
             both = jnp.dot(mine, maps[p], preferred_element_type=F32)
             for q in range(2):
                 c = 2 * p + q
-                x = both[:, q * unknowns : (q + 1) * unknowns] + near[c, here, :]
+                which, at = places[c]
+                near = (edge, rest)[which]
+                x = both[:, q * unknowns : (q + 1) * unknowns] + near[at, here, :]
                 if half == 0:
                     head = jnp.where(row == 0, jnp.broadcast_to(carry[c], row.shape), 0.0)
                     x = jnp.concatenate([x[:8] + head, x[8:]], axis=0)
                 major[c] = jnp.where(alive > first + c, x, 0.0).astype(BF16)
         for i in range(size // chunk):
-            at = half * size + i * chunk
-            done[pl.ds(at, chunk)] = jnp.transpose(major[:, pl.ds(i * chunk, chunk), :], (1, 0, 2))
+            start = half * size + i * chunk
+            rows = pl.ds(start, chunk)
+            done[rows] = jnp.transpose(major[:, pl.ds(i * chunk, chunk), :], (1, 0, 2))
             copies.append(
-                pltpu.make_async_copy(
-                    done.at[pl.ds(at, chunk)], out.at[pl.ds(at, chunk)], sems.at[at // chunk]
-                )
+                pltpu.make_async_copy(done.at[rows], out.at[rows], sems.at[start // chunk])
             )
             copies[-1].start()
     for copy in copies:
         copy.wait()
 
 
-def final(near, carry, parts, maps, live):
+def final(edge, rest, carry, parts, maps, live, orders):
     steps, unknowns = live.shape
-    clusters = near.shape[0]
-    return pl.pallas_call(
-        final_kernel,
-        in_specs=[VMEM] * (4 + len(parts)),
+    clusters = carry.shape[0]
+    places = {c: (k, i) for k, order in enumerate(orders) for i, c in enumerate(order)}
+    return pl.pallas_call(
+        functools.partial(final_kernel, places),
+        in_specs=[VMEM] * (5 + len(parts)),
         out_specs=HBM,
         out_shape=jax.ShapeDtypeStruct((steps, clusters, unknowns), BF16),
         scratch_shapes=[
@@ -435,7 +507,7 @@
         ],
         compiler_params=pltpu.CompilerParams(vmem_limit_bytes=10 << 20),
         name="final",
-    )(near, carry, *parts, maps, live)
+    )(edge, rest, carry, *parts, maps, live)
 
 
 def exchanged(x, axis):
@@ -475,17 +547,23 @@
     from_pair = swapped_from(pair, "space", 0)
     from_other = swapped_from(other, "space", 1)
     neighbours = neighbours.T
-    inner = inner_near(neighbours, window, near_blocks)
-    ends, inner = lax.optimization_barrier((ends, inner))
+    clusters = density.shape[1]
+    middle = clusters // 2
+    full = tuple(range(middle - REACH // 2, middle + REACH // 2))
+    sides = tuple(range(REACH)) + tuple(range(clusters - REACH, clusters))
+    others = tuple(c for c in range(clusters) if c not in full + sides)
+    inner, inner_carry = inner_near(neighbours, window, near_blocks, full, others)
+    ends, inner, inner_carry = lax.optimization_barrier((ends, inner, inner_carry))
     mine = arrive(ends, far, decay)
     mine = pair_sum(mine, swapped_from(mine, "space", 0))
     parts = [mine] + [from_chip(mine, "space", d) for d in range(1, chips)]
-    inner, mine = lax.optimization_barrier((inner, mine))
-    near, carry, maps, _ = outer_near(
-        neighbours, window, from_pair, from_other, near_blocks, inner, from_moments
+    inner_carry, mine = lax.optimization_barrier((inner_carry, mine))
+    edge, carry, window = edge_near(
+        neighbours, window, from_pair, from_other, near_blocks, inner_carry, sides
     )
     carry = passed_on(carry, "tm")
-    return final(near, carry, parts, maps, live)
+    rest, maps = rest_near(neighbours, window, near_blocks, inner, from_moments, others)
+    return final(edge, rest, carry, parts, maps, live, (sides, others + full))
 
 
 def solution(mesh):

time: 57.9 us -> 45.7 us (0.79)
  Pallas kernels: 26.7 us -> 18.4 us
  local copies, waits for them, and re-layouts: 1.96 us -> 0.01 us
  waiting for transfers between devices: 5.25 us -> 3.44 us
    pallas_call x3 -> x4, Pallas kernels: 23.7 us -> 15 us  [the longest x1 6.55 us: inner_near(): pl.pallas_call(functools.partial(inner_kernel, full, ends_only), in_specs...]
    ppermute x1, waiting for transfers between devices: 4.33 us -> 2.13 us  [passed_on(): return lax.ppermute(x, axis, [(i, i + 1) for i in range(count - 1)])]
    unnamed x6 -> x8, local copies, waits for them, and re-layouts: 1.96 us -> 0.01 us
  transfers between devices with their start and end apart: 8 -> 8, of which waited for: 2 -> 3; matrix products, arithmetic and copies ran while one was open for 0% -> 0% of each run, Pallas kernels for 37% -> 28%
where the time goes in v3:
time: 45.7 us; the launch traced here: 45.5 us
  starting transfers between devices  23.5 us (51%)
  Pallas kernels  18.4 us (40%)
  waiting for transfers between devices  3.44 us (8%)
    all_to_all x1, starting transfers between devices, exchanged(): return lax.all_to_all(x, axis, split_axis=0, concat_axis=0, tiled=True)  11.4 us
    pallas_call x1, Pallas kernels, inner_near(): pl.pallas_call(functools.partial(inner_kernel, full, ends_only), in_specs...  6.55 us
    ppermute x3, starting transfers between devices, from_chip(): lax.ppermute(x, axis, [(i, (i + 2 * distance) % count) for i in range(cou...  5.44 us
    pallas_call x1, Pallas kernels, edge_near(): pl.pallas_call(functools.partial(edge_kernel, order), in_specs=[HBM, VMEM...  3.6 us
    ppermute x1, starting transfers between devices, passed_on(): return lax.ppermute(x, axis, [(i, i + 1) for i in range(count - 1)])  3.37 us
    ppermute x3, starting transfers between devices, swapped_from(): return lax.ppermute(x, axis, route)  3.36 us
    pallas_call x1, Pallas kernels, prep(): pl.pallas_call(prep_kernel, in_specs=[HBM] * 5, out_specs=[VMEM, HBM, HBM...  3.23 us
    pallas_call x1, Pallas kernels, final(): pl.pallas_call(functools.partial(final_kernel, places), in_specs=[VMEM] *...  2.63 us
  transfers between devices with their start and end apart: 8, of which 3 were waited for; matrix products, arithmetic and copies ran while one was open for 0% of the time, Pallas kernels for 28%

profile of v3, /device:TPU:32, one launch (start us, length us, event | category | flops | bytes accessed | tf_op | source)
XLA Modules:
  0.0 45.5 jit_solution(6161770043262212602)
XLA Ops:
  0.0 3.2 %prep.1 = (bf16[48,256,128]{2,1,0:T(8,128)(2,1)S(1)}, bf16[8,256,128]{2,1,0:T(8,128)(2,1)}, bf16[8,256,128]{2,1,0:T(8,128)(2,1)}, f32[256,128]{1,0:T(8,128)S(1)}...) custom-call(bf16[256,32,128]{2,1,0:T(8,128)(2,1)} %density.1, s32[1,256]{1,0:T(1,128)} %bitcast.9, ...), custom_call_target="tpu_custom_call" | custom-call | tf_op jit(solution)/shard_map/prep/pallas_call | solution.py:158
  3.2 11.4 %all-to-all-start = ((f32[32,1,128]{2,1,0:T(1,128)}), f32[32,1,128]{2,1,0:T(1,128)S(1)}, u32[]{:S(2)}, u32[]{:S(2)}) async-start(f32[32,1,128]{2,1,0:T(1,128)} %get-tuple-element.26), calls=%async_computation | async-start | bytes 32768 | tf_op jit(solution)/shard_map/all_to_all | solution.py:514
  14.6 0.1 collective-permute-start
  14.7 1.5 %collective-permute-start.1 = (bf16[8,256,128]{2,1,0:T(8,128)(2,1)}, bf16[8,256,128]{2,1,0:T(8,128)(2,1)}, u32[]{:S(2)}, u32[]{:S(2)}) collective-permute-start(bf16[8,256,128]{2,1,0:T(8,128)(2,1)} %get-tuple-element.25), channel_id=1, source_target_pairs={{1,2},{2,1},{3,4},{4,3},{5,6},{6,5},{9,10},{10,9},{11,12},{12,11},... | collective-permute-start | bytes 1572872 | tf_op jit(solution)/shard_map/ppermute | solution.py:522
  16.2 6.6 %inner.1 = (f32[8,256,128]{2,1,0:T(8,128)}, f32[16,1,128]{2,1,0:T(1,128)}) custom-call(s32[8,32]{1,0:T(8,128)} %bitcast.6, bf16[48,256,128]{2,1,0:T(8,128)(2,1)S(1)} %get-tuple-element.23.window.window_in, bf16[2,32,8,128,128]{4,3,2,1,0:T(8,128)(2,1)} %blocks.5), custom_call_target="tpu_custom_call" | custom-call | tf_op jit(solution)/shard_map/inner/pallas_call | solution.py:320
  22.8 0.4 all-to-all-done.ends
  23.2 0.0 slice-start
  23.2 0.0 slice-start.1
  23.2 0.0 slice-start.2
  23.2 0.0 slice-start.3
  23.2 0.2 arrive.1.a
  23.3 1.8 %collective-permute-start.2 = (f32[128,128]{1,0:T(8,128)S(1)}, f32[128,128]{1,0:T(8,128)S(1)}, u32[]{:S(2)}, u32[]{:S(2)}) collective-permute-start(f32[128,128]{1,0:T(8,128)S(1)} %arrive.1.a), channel_id=1, source_target_pairs={{0,1},{1,0},{2,3},{3,2},{4,5},{5,4},{6,7},{7,6},{8,9},{9,8},{10,11... | collective-permute-start | bytes 196616 | tf_op jit(solution)/shard_map/ppermute | solution.py:522
  25.1 0.9 %collective-permute-done.2.b = f32[128,128]{1,0:T(8,128)S(1)} collective-permute-done((f32[128,128]{1,0:T(8,128)S(1)}, f32[128,128]{1,0:T(8,128)S(1)}, u32[]{:S(2)}, u32[]{:S(2)}) %collective-permute-start.2) | collective-permute-done | bytes 65568 | tf_op jit(solution)/shard_map/ppermute | solution.py:522
  26.0 1.6 %collective-permute-start.4 = (bf16[128,128]{1,0:T(8,128)(2,1)S(1)}, bf16[128,128]{1,0:T(8,128)(2,1)S(1)}, u32[]{:S(2)}, u32[]{:S(2)}) collective-permute-start(bf16[128,128]{1,0:T(8,128)(2,1)S(1)} %pair_sum.1.refs_0_), channel_id=1, source_target_pairs={{0,2},{1,3},{2,4},{3,5},{4,6},{5,7},{6,0},{7,1},{8,10},{9,11},{10,... | collective-permute-start | bytes 98312 | tf_op jit(solution)/shard_map/ppermute | solution.py:527
  27.6 2.4 %collective-permute-start.5 = (bf16[128,128]{1,0:T(8,128)(2,1)S(1)}, bf16[128,128]{1,0:T(8,128)(2,1)S(1)}, u32[]{:S(2)}, u32[]{:S(2)}) collective-permute-start(bf16[128,128]{1,0:T(8,128)(2,1)S(1)} %pair_sum.1.refs_0_), channel_id=1, source_target_pairs={{0,4},{1,5},{2,6},{3,7},{4,0},{5,1},{6,2},{7,3},{8,12},{9,13},{10,... | collective-permute-start | bytes 98312 | tf_op jit(solution)/shard_map/ppermute | solution.py:527
  30.0 1.5 %collective-permute-start.6 = (bf16[128,128]{1,0:T(8,128)(2,1)S(1)}, bf16[128,128]{1,0:T(8,128)(2,1)S(1)}, u32[]{:S(2)}, u32[]{:S(2)}) collective-permute-start(bf16[128,128]{1,0:T(8,128)(2,1)S(1)} %pair_sum.1.refs_0_), channel_id=1, source_target_pairs={{0,6},{1,7},{2,0},{3,1},{4,2},{5,3},{6,4},{7,5},{8,14},{9,15},{10,... | collective-permute-start | bytes 98312 | tf_op jit(solution)/shard_map/ppermute | solution.py:527
  31.5 0.0 collective-permute-done.from_pair
  31.5 0.0 collective-permute-done.1.from_other
  31.5 0.0 slice-done
  31.5 0.0 slice-done.1
  31.5 0.0 slice-done.2
  31.5 0.0 slice-done.3
  31.5 3.6 %edge.1 = (f32[16,256,128]{2,1,0:T(8,128)S(1)}, f32[32,1,128]{2,1,0:T(1,128)S(1)}, bf16[48,256,128]{2,1,0:T(8,128)(2,1)S(1)}) custom-call(s32[8,32]{1,0:T(8,128)} %bitcast.7, bf16[48,256,128]{2,1,0:T(8,128)(2,1)S(1)} %get-tuple-element.23.window.window_in, bf16[8,256,128]{2,1,0:T(8,128)(2,1)} %collective-permute-done.from_pair, ...), custom_call_target="tpu_custom_call", output_to_operand_aliasing={{2}: (1, {})} | custom-call | tf_op jit(solution)/shard_map/edge/pallas_call | solution.py:382
  35.1 3.4 %collective-permute-start.3 = (f32[32,1,128]{2,1,0:T(1,128)S(1)}, f32[32,1,128]{2,1,0:T(1,128)S(1)}, u32[]{:S(2)}, u32[]{:S(2)}) collective-permute-start(f32[32,1,128]{2,1,0:T(1,128)S(1)} %get-tuple-element.38), channel_id=1, source_target_pairs={{0,8},{8,16},{16,24},{24,32},{32,40},{40,48},{48,56},{56,64},{64,7... | collective-permute-start | bytes 49160 | tf_op jit(solution)/shard_map/ppermute | solution.py:532
  38.5 2.2 %rest.1 = (f32[16,256,128]{2,1,0:T(8,128)S(1)}, bf16[16,128,256]{2,1,0:T(8,128)(2,1)S(1)}) custom-call(s32[8,32]{1,0:T(8,128)} %bitcast.8, bf16[48,256,128]{2,1,0:T(8,128)(2,1)S(1)} %get-tuple-element.35.window, bf16[2,32,8,128,128]{4,3,2,1,0:T(8,128)(2,1)S(1)} %bitcast.5, f32[8,256,128]{2,1,0:T(8,128)} %get-tuple-element.36.inner, ...), custom_call_target="tpu_custom_call" | custom-call | tf_op jit(solution)/shard_map/rest/pallas_call | solution.py:435
  40.7 0.0 collective-permute-done.4.refs_1_
  40.7 0.0 collective-permute-done.5.refs_2_
  40.7 0.0 collective-permute-done.6.refs_3_
  40.7 2.1 %collective-permute-done.3.carry = f32[32,1,128]{2,1,0:T(1,128)S(1)} collective-permute-done((f32[32,1,128]{2,1,0:T(1,128)S(1)}, f32[32,1,128]{2,1,0:T(1,128)S(1)}, u32[]{:S(2)}, u32[]{:S(2)}) %collective-permute-start.3) | collective-permute-done | bytes 16416 | tf_op jit(solution)/shard_map/ppermute | solution.py:532
  42.9 2.6 %final.1 = bf16[256,32,128]{2,1,0:T(8,128)(2,1)} custom-call(f32[16,256,128]{2,1,0:T(8,128)S(1)} %get-tuple-element.34.edge, f32[16,256,128]{2,1,0:T(8,128)S(1)} %get-tuple-element.37.rest, f32[32,1,128]{2,1,0:T(1,128)S(1)} %collective-permute-done.3.carry, bf16[128,128]{1,0:T(8,128)(2,1)S(1)} %pair_sum.1.refs_0_, ...), custom_call_target="tpu_custom_call" | custom-call | tf_op jit(solution)/shard_map/final/pallas_call | solution.py:498
  (2 shorter events, 0.0 us)
Async XLA Ops:
  3.2 19.9 %all-to-all-start = ((f32[32,1,128]{2,1,0:T(1,128)}), f32[32,1,128]{2,1,0:T(1,128)S(1)}, u32[]{:S(2)}, u32[]{:S(2)}) async-start(f32[32,1,128]{2,1,0:T(1,128)} %get-tuple-element.26), calls=%async_computation | async-start | bytes 32768 | tf_op jit(solution)/shard_map/all_to_all | solution.py:514
  14.6 16.9 %collective-permute-start = (bf16[8,256,128]{2,1,0:T(8,128)(2,1)}, bf16[8,256,128]{2,1,0:T(8,128)(2,1)}, u32[]{:S(2)}, u32[]{:S(2)}) collective-permute-start(bf16[8,256,128]{2,1,0:T(8,128)(2,1)} %get-tuple-element.24), channel_id=1, source_target_pairs={{0,1},{1,0},{2,3},{3,2},{4,5},{5,4},{6,7},{7,6},{8,9},{9,8},{10,11... | collective-permute-start | bytes 1572872 | tf_op jit(solution)/shard_map/ppermute | solution.py:522
  14.7 16.8 %collective-permute-start.1 = (bf16[8,256,128]{2,1,0:T(8,128)(2,1)}, bf16[8,256,128]{2,1,0:T(8,128)(2,1)}, u32[]{:S(2)}, u32[]{:S(2)}) collective-permute-start(bf16[8,256,128]{2,1,0:T(8,128)(2,1)} %get-tuple-element.25), channel_id=1, source_target_pairs={{1,2},{2,1},{3,4},{4,3},{5,6},{6,5},{9,10},{10,9},{11,12},{12,11},... | collective-permute-start | bytes 1572872 | tf_op jit(solution)/shard_map/ppermute | solution.py:522
  23.2 8.3 %slice-start = ((s8[16777216]{0:T(1024)(128)(4,1)}), s8[4194304]{0:T(1024)(128)(4,1)S(1)}, s32[]{:S(2)}) async-start(s8[16777216]{0:T(1024)(128)(4,1)} %bitcast.4), calls=%async_computation.1 | async-start | bytes 8388608
  23.2 8.3 %slice-start.1 = ((s8[16777216]{0:T(1024)(128)(4,1)}), s8[4194304]{0:T(1024)(128)(4,1)S(1)}, s32[]{:S(2)}) async-start(s8[16777216]{0:T(1024)(128)(4,1)} %bitcast.4), calls=%async_computation.2 | async-start | bytes 8388608
  23.2 8.3 %slice-start.2 = ((s8[16777216]{0:T(1024)(128)(4,1)}), s8[4194304]{0:T(1024)(128)(4,1)S(1)}, s32[]{:S(2)}) async-start(s8[16777216]{0:T(1024)(128)(4,1)} %bitcast.4), calls=%async_computation.3 | async-start | bytes 8388608
  23.2 8.3 %slice-start.3 = ((s8[16777216]{0:T(1024)(128)(4,1)}), s8[4194304]{0:T(1024)(128)(4,1)S(1)}, s32[]{:S(2)}) async-start(s8[16777216]{0:T(1024)(128)(4,1)} %bitcast.4), calls=%async_computation.4 | async-start | bytes 8388608
  23.3 2.7 %collective-permute-start.2 = (f32[128,128]{1,0:T(8,128)S(1)}, f32[128,128]{1,0:T(8,128)S(1)}, u32[]{:S(2)}, u32[]{:S(2)}) collective-permute-start(f32[128,128]{1,0:T(8,128)S(1)} %arrive.1.a), channel_id=1, source_target_pairs={{0,1},{1,0},{2,3},{3,2},{4,5},{5,4},{6,7},{7,6},{8,9},{9,8},{10,11... | collective-permute-start | bytes 196616 | tf_op jit(solution)/shard_map/ppermute | solution.py:522
  26.0 14.7 %collective-permute-start.4 = (bf16[128,128]{1,0:T(8,128)(2,1)S(1)}, bf16[128,128]{1,0:T(8,128)(2,1)S(1)}, u32[]{:S(2)}, u32[]{:S(2)}) collective-permute-start(bf16[128,128]{1,0:T(8,128)(2,1)S(1)} %pair_sum.1.refs_0_), channel_id=1, source_target_pairs={{0,2},{1,3},{2,4},{3,5},{4,6},{5,7},{6,0},{7,1},{8,10},{9,11},{10,... | collective-permute-start | bytes 98312 | tf_op jit(solution)/shard_map/ppermute | solution.py:527
  27.6 13.1 %collective-permute-start.5 = (bf16[128,128]{1,0:T(8,128)(2,1)S(1)}, bf16[128,128]{1,0:T(8,128)(2,1)S(1)}, u32[]{:S(2)}, u32[]{:S(2)}) collective-permute-start(bf16[128,128]{1,0:T(8,128)(2,1)S(1)} %pair_sum.1.refs_0_), channel_id=1, source_target_pairs={{0,4},{1,5},{2,6},{3,7},{4,0},{5,1},{6,2},{7,3},{8,12},{9,13},{10,... | collective-permute-start | bytes 98312 | tf_op jit(solution)/shard_map/ppermute | solution.py:527
  30.0 10.7 %collective-permute-start.6 = (bf16[128,128]{1,0:T(8,128)(2,1)S(1)}, bf16[128,128]{1,0:T(8,128)(2,1)S(1)}, u32[]{:S(2)}, u32[]{:S(2)}) collective-permute-start(bf16[128,128]{1,0:T(8,128)(2,1)S(1)} %pair_sum.1.refs_0_), channel_id=1, source_target_pairs={{0,6},{1,7},{2,0},{3,1},{4,2},{5,3},{6,4},{7,5},{8,14},{9,15},{10,... | collective-permute-start | bytes 98312 | tf_op jit(solution)/shard_map/ppermute | solution.py:527
  35.1 7.7 %collective-permute-start.3 = (f32[32,1,128]{2,1,0:T(1,128)S(1)}, f32[32,1,128]{2,1,0:T(1,128)S(1)}, u32[]{:S(2)}, u32[]{:S(2)}) collective-permute-start(f32[32,1,128]{2,1,0:T(1,128)S(1)} %get-tuple-element.38), channel_id=1, source_target_pairs={{0,8},{8,16},{16,24},{24,32},{32,40},{40,48},{48,56},{56,64},{64,7... | collective-permute-start | bytes 49160 | tf_op jit(solution)/shard_map/ppermute | solution.py:532

commit v4 on v2

v4 whole, which is shorter than its diff:
```python
import functools

import jax
import jax.numpy as jnp
from jax import lax
from jax.experimental import pallas as pl
from jax.experimental.pallas import tpu as pltpu
from jax.sharding import PartitionSpec as P

REACH = 8
F32 = jnp.float32
BF16 = jnp.bfloat16
HBM = pl.BlockSpec(memory_space=pltpu.HBM)
VMEM = pl.BlockSpec(memory_space=pltpu.VMEM)
SMEM = pl.BlockSpec(memory_space=pltpu.SMEM)


def in_hbm(x):
    return pltpu.with_memory_space_constraint(x, pltpu.HBM)


def in_vmem(x):
    return pltpu.with_memory_space_constraint(x, pltpu.VMEM)


def column(row, lanes):
    return jnp.transpose(jnp.broadcast_to(row, (lanes, row.shape[1])))


def shifted_down(v, steps, fill):
    rows = v.shape[0]
    if steps < 8:
        moved = pltpu.roll(v, steps, 0)
        at = lax.broadcasted_iota(jnp.int32, v.shape, 0)
        return jnp.where(at < steps, jnp.full_like(v, fill), moved)
    return jnp.concatenate([jnp.full((steps, v.shape[1]), fill, v.dtype), v[: rows - steps]], 0)


def doubled(row):
    return jnp.concatenate([row, row], axis=1)


def is_even():
    return lax.rem(lax.axis_index("space"), 2) == 0


def prep_kernel(
    density,
    active,
    to_moments,
    rates,
    lengths,
    neighbours,
    window,
    far,
    decay,
    ends,
    live,
    table,
    dense,
    maps,
    active_row,
    rates_row,
    lengths_row,
    flat,
    sems,
):
    steps, clusters, unknowns = density.shape
    terms = to_moments.shape[0]
    pieces = 4
    size = steps // pieces
    chunk = 32
    pitch = clusters + 1
    first = lax.axis_index("space") * clusters

    def copy(src, dst, k):
        return pltpu.make_async_copy(src, dst, sems.at[k])

    small = [
        copy(active, active_row, 0),
        copy(lengths, lengths_row, 1),
        copy(rates, rates_row, 2),
    ]
    parts = [
        copy(density.at[pl.ds(k * size, size)], dense.at[pl.ds(k * size, size)], 4 + k)
        for k in range(pieces)
    ]
    weights = copy(to_moments, maps, 3)
    listed = copy(neighbours, table, 8)
    for c in small + parts + [weights, listed]:
        c.start()
    for c in small:
        c.wait()
    live[...] = column(active_row[...], unknowns)

    for k in range(pieces):
        parts[k].wait()

        def spread(i, _):
            start = pl.multiple_of(k * size + i * chunk, chunk)
            here = pl.ds(start, chunk)
            x = dense[here].astype(F32)
            for t in range(chunk):
                flat[pl.ds(t * pitch, clusters), :] = x[t]
            alive = live[here, :]
            for c in range(clusters):
                y = flat[pl.ds(c, chunk, stride=pitch), :]
                y = jnp.where(alive > first + c, y, 0.0)
                window[REACH + c, here, :] = y.astype(BF16)
            return 0

        lax.fori_loop(0, size // chunk, spread, 0)

    weights.wait()
    w = jnp.transpose(maps[...], (1, 0, 2))
    total = jnp.zeros((steps, 2 * terms), F32)
    for c in range(0, clusters, 2):
        x = jnp.concatenate([window[REACH + c], window[REACH + c + 1]], axis=1)
        y = jnp.concatenate([w[c], w[c + 1]], axis=1)
        y = jnp.concatenate([y, y], axis=0)
        total = total + lax.dot_general(
            x, y, (((1,), (1,)), ((), ())), preferred_element_type=F32
        )
    d = jnp.exp(-doubled(rates_row[...]) * column(lengths_row[...], 2 * terms))
    s = 1
    while s < steps:
        before = shifted_down(total, s, 0.0)
        factor = shifted_down(d, s, 1.0)
        total = total + d * before
        d = d * factor
        s *= 2
    lane = lax.broadcasted_iota(jnp.int32, (1, 2 * terms), 1)
    line = jnp.where(lane < terms, total[steps - 1 :], d[steps - 1 :])
    ends[...] = line
    scale = jnp.sqrt(2.0 * doubled(rates_row[...]))
    far[...] = shifted_down(total, 1, 0.0) * scale
    decay[...] = shifted_down(d, 1, 1.0) * scale
    listed.wait()


def prep(density, active, to_moments, rates, lengths, neighbours):
    steps, clusters, unknowns = density.shape
    terms = to_moments.shape[0]
    lanes = 2 * terms
    return pl.pallas_call(
        prep_kernel,
        in_specs=[HBM] * 6,
        out_specs=[VMEM] * 6,
        out_shape=[
            jax.ShapeDtypeStruct((clusters + 2 * REACH, steps, unknowns), BF16),
            jax.ShapeDtypeStruct((steps, lanes), F32),
            jax.ShapeDtypeStruct((steps, lanes), F32),
            jax.ShapeDtypeStruct((1, lanes), F32),
            jax.ShapeDtypeStruct((steps, unknowns), jnp.int32),
            jax.ShapeDtypeStruct(neighbours.shape, jnp.int32),
        ],
        scratch_shapes=[
            pltpu.VMEM(density.shape, BF16),
            pltpu.VMEM(to_moments.shape, BF16),
            pltpu.VMEM(active.shape, jnp.int32),
            pltpu.VMEM(rates.shape, F32),
            pltpu.VMEM(lengths.shape, F32),
            pltpu.VMEM((32 * (clusters + 1) + 7, unknowns), F32),
            pltpu.SemaphoreType.DMA((9,)),
        ],
        compiler_params=pltpu.CompilerParams(vmem_limit_bytes=8 << 20),
        cost_estimate=pl.CostEstimate(
            flops=12_000_000_000, bytes_accessed=1 << 20, transcendentals=0
        ),
        name="prep",
    )(*map(in_hbm, (density, active, to_moments, rates, lengths, neighbours)))


def sides_kernel(window, pair, other):
    even = is_even()
    above = window.shape[0] - 2 * REACH
    pair[...] = window[pl.ds(jnp.where(even, above, REACH), REACH)]
    other[...] = window[pl.ds(jnp.where(even, REACH, above), REACH)]


def sides_of(window):
    side = jax.ShapeDtypeStruct((REACH, *window.shape[1:]), BF16)
    return pl.pallas_call(
        sides_kernel,
        in_specs=[VMEM],
        out_specs=[VMEM] * 2,
        out_shape=[side, side],
        compiler_params=pltpu.CompilerParams(vmem_limit_bytes=1 << 20),
        name="sides",
    )(window)


def after(first, second):
    lanes = first.shape[1]
    half = lanes // 2
    lane = lax.broadcasted_iota(jnp.int32, first.shape, 1)
    factor = jnp.where(lane < half, pltpu.roll(second, half, 1), second)
    return factor * first + jnp.where(lane < half, second, 0.0)


def fold_kernel(bit, own, arriving, seen, whole, before):
    upper = lax.rem(lax.axis_index("tm") // bit, 2) == 1
    mine, theirs, past = own[...], seen[...], arriving[...]
    first = jnp.where(upper, theirs, mine)
    second = jnp.where(upper, mine, theirs)
    whole[...] = after(first, second)
    before[...] = jnp.where(upper, after(theirs, past), past)


def fold(bit, own, arriving, seen):
    line = jax.ShapeDtypeStruct(own.shape, F32)
    return pl.pallas_call(
        functools.partial(fold_kernel, bit),
        in_specs=[VMEM] * 3,
        out_specs=[VMEM] * 2,
        out_shape=[line, line],
        compiler_params=pltpu.CompilerParams(vmem_limit_bytes=1 << 20),
        name="fold",
    )(own, arriving, seen)


def arrive_kernel(before, far, decay, out):
    steps, lanes = far.shape
    half = lanes // 2
    line = before[...]
    lane = lax.broadcasted_iota(jnp.int32, line.shape, 1)
    state = jnp.where(lane < half, line, pltpu.roll(line, half, 1))
    x = far[...] + decay[...] * state
    wide = lax.broadcasted_iota(jnp.int32, (steps // 2, lanes), 1)
    out[...] = jnp.where(wide < half, x[: steps // 2], x[steps // 2 :])


def arrive(before, far, decay):
    steps, lanes = far.shape
    return pl.pallas_call(
        arrive_kernel,
        in_specs=[VMEM] * 3,
        out_specs=VMEM,
        out_shape=jax.ShapeDtypeStruct((steps // 2, lanes), F32),
        compiler_params=pltpu.CompilerParams(vmem_limit_bytes=4 << 20),
        name="arrive",
    )(before, far, decay)


def pair_kernel(a, b, out):
    out[...] = (a[...] + b[...]).astype(BF16)


def pair_sum(a, b):
    return pl.pallas_call(
        pair_kernel,
        in_specs=[VMEM] * 2,
        out_specs=VMEM,
        out_shape=jax.ShapeDtypeStruct(a.shape, BF16),
        compiler_params=pltpu.CompilerParams(vmem_limit_bytes=4 << 20),
        name="pair_sum",
    )(a, b)


def gathered(neighbours, window, cluster, rows):
    base = lax.axis_index("space") * neighbours.shape[1] - REACH
    return jnp.concatenate(
        [window[neighbours[j, cluster] - base, rows, :] for j in range(neighbours.shape[0])], axis=1
    )


def stacked(block):
    nb, unknowns, width = block.shape
    return block[...].reshape(nb * unknowns, width)


def near_of(neighbours, window, blocks, cluster):
    steps = window.shape[1]
    x = gathered(neighbours, window, cluster, pl.ds(0, steps))
    w = jnp.concatenate([stacked(block) for block in blocks], axis=1)
    both = jnp.dot(x, w, preferred_element_type=F32)
    now, later = jnp.split(both, 2, axis=1)
    return now + shifted_down(later, 1, 0.0), later[steps - 1 :]


def inner_kernel(order, neighbours, window, blocks, near, carry):
    for i, cluster in enumerate(order):
        blocks_here = [blocks.at[lag, cluster] for lag in range(blocks.shape[0])]
        near[i], carry[i] = near_of(neighbours, window, blocks_here, cluster)


def mapped_kernel(order, neighbours, window, blocks, from_moments, near, carry, maps, rows, sems):
    fetch = pltpu.make_async_copy(from_moments, rows, sems.at[0])
    fetch.start()
    inner_kernel(order, neighbours, window, blocks, near, carry)
    fetch.wait()
    w = jnp.transpose(rows[...], (1, 0, 2))
    for p in range(maps.shape[0]):
        x = jnp.concatenate([w[2 * p], w[2 * p + 1]], axis=1)
        maps[p] = jnp.concatenate([x, x], axis=0)


def joined_kernel(
    order, neighbours, window_in, from_pair, from_other, blocks, near, carry, window
):
    del window_in
    even = is_even()
    above = window.shape[0] - REACH
    window[pl.ds(jnp.where(even, above, 0), REACH)] = from_pair[...]
    window[pl.ds(jnp.where(even, 0, above), REACH)] = from_other[...]
    inner_kernel(order, neighbours, window, blocks, near, carry)


def last_kernel(order, neighbours, window, blocks, *refs):
    earlier = refs[:-3]
    near, carry, lines = refs[-3:]
    inner_kernel(order, neighbours, window, blocks, near, carry)
    for k, ref in enumerate(earlier + (carry,)):
        for i in range(len(order)):
            lines[k * len(order) + i] = ref[i]


def near_call(body, order, operands, specs, window, blocks, more=(), scratch=(), aliases={}):
    steps, unknowns = window.shape[1:]
    shapes = [
        jax.ShapeDtypeStruct((len(order), steps, unknowns), F32),
        jax.ShapeDtypeStruct((len(order), 1, unknowns), F32),
        *more,
    ]
    return pl.pallas_call(
        functools.partial(body, order),
        in_specs=[SMEM] + specs,
        out_specs=[VMEM] * len(shapes),
        out_shape=shapes,
        scratch_shapes=list(scratch),
        input_output_aliases=aliases,
        compiler_params=pltpu.CompilerParams(vmem_limit_bytes=4 << 20),
        name="near",
    )(*operands)


def final_kernel(orders, *refs):
    groups = len(orders)
    nears, carry, parts = refs[:groups], refs[groups], refs[groups + 1 : -6]
    maps, live, out, major, done, sems = refs[-6:]
    places = {c: (k, i) for k, order in enumerate(orders) for i, c in enumerate(order)}
    steps, clusters, unknowns = out.shape
    terms = maps.shape[1] // 2
    first = lax.axis_index("space") * clusters
    total = parts[0][...].astype(F32)
    for part in parts[1:]:
        total = total + part[...].astype(F32)
    lane = lax.broadcasted_iota(jnp.int32, total.shape, 1)
    size = steps // 2
    chunk = 32
    row = lax.broadcasted_iota(jnp.int32, (8, unknowns), 0)
    copies = []
    for half in range(2):
        mine = jnp.where(lane // terms == half, total, 0.0).astype(BF16)
        here = pl.ds(half * size, size)
        alive = live[here, :]
        for p in range(clusters // 2):
            both = jnp.dot(mine, maps[p], preferred_element_type=F32)
            for q in range(2):
                c = 2 * p + q
                k, i = places[c]
                x = both[:, q * unknowns : (q + 1) * unknowns] + nears[k][i, here, :]
                if half == 0:
                    head = jnp.where(row == 0, jnp.broadcast_to(carry[k * REACH + i], row.shape), 0.0)
                    x = jnp.concatenate([x[:8] + head, x[8:]], axis=0)
                major[c] = jnp.where(alive > first + c, x, 0.0).astype(BF16)
        for i in range(size // chunk):
            start = half * size + i * chunk
            rows = pl.ds(start, chunk)
            done[rows] = jnp.transpose(major[:, pl.ds(i * chunk, chunk), :], (1, 0, 2))
            copies.append(
                pltpu.make_async_copy(done.at[rows], out.at[rows], sems.at[start // chunk])
            )
            copies[-1].start()
    for copy in copies:
        copy.wait()


def final(orders, nears, carry, parts, maps, live):
    steps, unknowns = live.shape
    clusters = carry.shape[0]
    return pl.pallas_call(
        functools.partial(final_kernel, orders),
        in_specs=[VMEM] * (len(nears) + len(parts) + 3),
        out_specs=HBM,
        out_shape=jax.ShapeDtypeStruct((steps, clusters, unknowns), BF16),
        scratch_shapes=[
            pltpu.VMEM((clusters, steps // 2, unknowns), BF16),
            pltpu.VMEM((steps, clusters, unknowns), BF16),
            pltpu.SemaphoreType.DMA((steps // 32,)),
        ],
        compiler_params=pltpu.CompilerParams(vmem_limit_bytes=10 << 20),
        name="final",
    )(*nears, carry, *parts, maps, live)


def across(x, axis, bit):
    count = lax.axis_size(axis)
    return lax.ppermute(x, axis, [(i, i ^ bit) for i in range(count)])


def swapped_from(x, axis, start):
    count = lax.axis_size(axis)
    route = []
    for i in range(start, count - 1, 2):
        route += [(i, i + 1), (i + 1, i)]
    return lax.ppermute(x, axis, route)


def from_chip(x, axis, distance):
    count = lax.axis_size(axis)
    return lax.ppermute(x, axis, [(i, (i + 2 * distance) % count) for i in range(count)])


def passed_on(x, axis):
    count = lax.axis_size(axis)
    return lax.ppermute(x, axis, [(i, i + 1) for i in range(count - 1)])


def local(density, active, neighbours, near_blocks, to_moments, from_moments, decay_rates, lengths):
    steps, clusters, unknowns = density.shape
    terms = decay_rates.shape[0]
    chips = lax.axis_size("space") // 2
    window, far, decay, own, live, table = prep(
        density,
        active.reshape(1, steps),
        to_moments,
        decay_rates.reshape(1, -1),
        lengths.reshape(1, steps),
        neighbours.T,
    )
    half = clusters // 2
    orders = (
        tuple(range(REACH, half)),
        tuple(range(half, clusters - REACH)),
        tuple(range(REACH)),
        tuple(range(clusters - REACH, clusters)),
    )
    blocks = in_vmem(near_blocks)
    maps_shape = jax.ShapeDtypeStruct((clusters // 2, 2 * terms, 2 * unknowns), BF16)
    bits = [1 << k for k in range((lax.axis_size("tm") - 1).bit_length())]
    nears, carries = [], []
    lane = lax.broadcasted_iota(jnp.int32, own.shape, 1)
    arriving = jnp.where(lane < terms, 0.0, 1.0)
    pair, other = sides_of(window)
    from_pair = swapped_from(pair, "space", 0)
    from_other = swapped_from(other, "space", 1)
    for turn, bit in enumerate(bits):
        seen = across(own, "tm", bit)
        if turn < len(orders):
            order = orders[turn]
            table, own = lax.optimization_barrier((table, own))
            if turn == 0:
                near, carry, maps = near_call(
                    mapped_kernel,
                    order,
                    (table, window, blocks, in_hbm(from_moments)),
                    [VMEM, VMEM, HBM],
                    window,
                    blocks,
                    (maps_shape,),
                    (
                        pltpu.VMEM(from_moments.shape, BF16),
                        pltpu.SemaphoreType.DMA((1,)),
                    ),
                )
            elif turn == 1:
                near, carry = near_call(
                    inner_kernel, order, (table, window, blocks), [VMEM] * 2, window, blocks
                )
            elif turn == 2:
                near, carry, window = near_call(
                    joined_kernel,
                    order,
                    (table, window, from_pair, from_other, blocks),
                    [VMEM] * 4,
                    window,
                    blocks,
                    (jax.ShapeDtypeStruct(window.shape, BF16),),
                    aliases={1: 2},
                )
            else:
                near, carry, lines = near_call(
                    last_kernel,
                    order,
                    (table, window, blocks, *carries),
                    [VMEM] * (2 + len(carries)),
                    window,
                    blocks,
                    (jax.ShapeDtypeStruct((clusters, 1, unknowns), F32),),
                )
            nears.append(near)
            carries.append(carry)
            if turn < len(orders) - 1:
                seen, carry = lax.optimization_barrier((seen, carry))
            else:
                seen, lines = lax.optimization_barrier((seen, lines))
        own, arriving = fold(bit, own, arriving, seen)
    lines = passed_on(lines, "tm")
    mine = arrive(arriving, far, decay)
    mine = pair_sum(mine, swapped_from(mine, "space", 0))
    parts = [mine] + [from_chip(mine, "space", d) for d in range(1, chips)]
    return final(orders, nears, lines, parts, maps, live)


def solution(mesh):
    placed = (
        P("tm", "space", None),
        P("tm"),
        P("space", None),
        P(None, "space", None, None, None),
        P(None, "space", None),
        P(None, "space", None),
        P(),
        P("tm"),
    )
    return jax.shard_map(
        local, mesh=mesh, in_specs=placed, out_specs=P("tm", "space", None), check_vma=False
    )
```

time: 57.9 us -> 50.5 us (0.87)
  Pallas kernels: 26.7 us -> 15.7 us
  waiting for transfers between devices: 5.25 us -> 8.93 us
  local copies, waits for them, and re-layouts: 1.96 us -> 1.16 us
    ppermute x0 -> x5, starting transfers between devices: none -> 14.8 us  [across(): return lax.ppermute(x, axis, [(i, i ^ bit) for i in range(count)])]
    all_to_all x1 -> x0, starting transfers between devices: 11.4 us -> none  [exchanged(): return lax.all_to_all(x, axis, split_axis=0, concat_axis=0, tiled=True)]
    pallas_call x4 -> x12, Pallas kernels: 26.5 us -> 15.6 us  [the longest x4 9.07 us: near_call(): pl.pallas_call(functools.partial(body, order), in_specs=[SMEM] + specs, o...]
    ppermute x0 -> x5, waiting for transfers between devices: none -> 2.45 us  [across(): return lax.ppermute(x, axis, [(i, i ^ bit) for i in range(count)])]
    ppermute x3, starting transfers between devices: 3.05 us -> 1.01 us  [swapped_from(): return lax.ppermute(x, axis, route)]
    ppermute x1, waiting for transfers between devices: 4.33 us -> 5.22 us  [passed_on(): return lax.ppermute(x, axis, [(i, i + 1) for i in range(count - 1)])]
    ppermute x1, starting transfers between devices: 3.37 us -> 2.5 us  [passed_on(): return lax.ppermute(x, axis, [(i, i + 1) for i in range(count - 1)])]
    unnamed x6 -> x8, local copies, waits for them, and re-layouts: 1.96 us -> 1.16 us
  transfers between devices with their start and end apart: 8 -> 12, of which waited for: 2 -> 3; matrix products, arithmetic and copies ran while one was open for 0% -> 0% of each run, Pallas kernels for 37% -> 19%
where the time goes in v4:
time: 50.5 us; the launch traced here: 49.7 us
  starting transfers between devices  23.8 us (47%)
  Pallas kernels  15.7 us (31%)
  waiting for transfers between devices  8.93 us (18%)
  local copies, waits for them, and re-layouts  1.16 us (2%)
    ppermute x5, starting transfers between devices, across(): return lax.ppermute(x, axis, [(i, i ^ bit) for i in range(count)])  14.8 us
    pallas_call x4, Pallas kernels, near_call(): pl.pallas_call(functools.partial(body, order), in_specs=[SMEM] + specs, o...  9.07 us
    ppermute x3, starting transfers between devices, from_chip(): lax.ppermute(x, axis, [(i, (i + 2 * distance) % count) for i in range(cou...  5.45 us
    ppermute x1, waiting for transfers between devices, passed_on(): return lax.ppermute(x, axis, [(i, i + 1) for i in range(count - 1)])  5.22 us
    pallas_call x1, Pallas kernels, prep(): pl.pallas_call(prep_kernel, in_specs=[HBM] * 6, out_specs=[VMEM] * 6, out...  2.81 us
    pallas_call x1, Pallas kernels, final(): pl.pallas_call(functools.partial(final_kernel, orders), in_specs=[VMEM] *...  2.67 us
    ppermute x1, starting transfers between devices, passed_on(): return lax.ppermute(x, axis, [(i, i + 1) for i in range(count - 1)])  2.5 us
    ppermute x5, waiting for transfers between devices, across(): return lax.ppermute(x, axis, [(i, i ^ bit) for i in range(count)])  2.45 us
  transfers between devices with their start and end apart: 12, of which 3 were waited for; matrix products, arithmetic and copies ran while one was open for 0% of the time, Pallas kernels for 19%

profile of v4, /device:TPU:32, one launch (start us, length us, event | category | flops | bytes accessed | tf_op | source)
XLA Modules:
  0.0 49.7 jit_solution(14173175817125806315)
XLA Ops:
  0.0 0.0 slice-start.3
  0.0 2.8 %prep.1 = (bf16[48,256,128]{2,1,0:T(8,128)(2,1)S(1)}, f32[256,128]{1,0:T(8,128)S(1)}, f32[256,128]{1,0:T(8,128)S(1)}, f32[1,128]{1,0:T(1,128)S(1)}, s32[256,128]{1,0:T(8,128)S(1)}, /*index=5*/s32[8,32]{1,0:T(8,128)S(1)}) custom-call(bf16[256,32,128]{2,1,0:T(8,128)(2,1)} %density.1, s32[1,256]{1,0:T(1,128)} %bitcast.7, bf16[64,32,128]{2,1,0:T(8,128)(2,1)} %to_moments.1, ...), custom_call_target="tpu_custom_call" | custom-call | flops 12000000000 | bytes 1048576 | tf_op jit(solution)/shard_map/prep/pallas_call | solution.py:145
  2.8 0.1 sides.1
  2.9 0.1 collective-permute-start.2
  3.0 0.8 %collective-permute-start.3 = (bf16[8,256,128]{2,1,0:T(8,128)(2,1)S(1)}, bf16[8,256,128]{2,1,0:T(8,128)(2,1)S(1)}, u32[]{:S(2)}, u32[]{:S(2)}) collective-permute-start(bf16[8,256,128]{2,1,0:T(8,128)(2,1)S(1)} %get-tuple-element.63), channel_id=1, source_target_pairs={{1,2},{2,1},{3,4},{4,3},{5,6},{6,5},{9,10},{10,9},{11,12},{12,11},... | collective-permute-start | bytes 1572872 | tf_op jit(solution)/shard_map/ppermute | solution.py:407
  3.9 1.7 %collective-permute-start = (f32[1,128]{1,0:T(1,128)S(1)}, f32[1,128]{1,0:T(1,128)S(1)}, u32[]{:S(2)}, u32[]{:S(2)}) collective-permute-start(f32[1,128]{1,0:T(1,128)S(1)} %get-tuple-element.50.own), channel_id=1, source_target_pairs={{0,8},{8,0},{16,24},{24,16},{32,40},{40,32},{48,56},{56,48},{64,72... | collective-permute-start | bytes 1544 | tf_op jit(solution)/shard_map/ppermute | solution.py:399
  5.5 1.2 %slice-done.3 = s8[4194304]{0:T(1024)(128)(4,1)S(1)} async-done(((s8[16777216]{0:T(1024)(128)(4,1)}), s8[4194304]{0:T(1024)(128)(4,1)S(1)}, s32[]{:S(2)}) %slice-start.3) | async-done | bytes 4194328
  6.7 2.9 %near.4 = (f32[8,256,128]{2,1,0:T(8,128)S(1)}, f32[8,1,128]{2,1,0:T(1,128)S(1)}, bf16[16,128,256]{2,1,0:T(8,128)(2,1)S(1)}) custom-call(s32[8,32]{1,0:T(8,128)S(1)} %get-tuple-element.70.neighbours, bf16[48,256,128]{2,1,0:T(8,128)(2,1)S(1)} %get-tuple-element.48.window.window_in, bf16[2,32,8,128,128]{4,3,2,1,0:T(8,128)(2,1)S(1)} %bitcast.5, ...), custom_call_target="tpu_custom_call" | custom-call | tf_op jit(solution)/shard_map/near/pallas_call | solution.py:325
  9.6 0.0 collective-permute-done.seen
  9.6 0.1 fold.5
  9.7 3.2 %collective-permute-start.1 = (f32[1,128]{1,0:T(1,128)S(1)}, f32[1,128]{1,0:T(1,128)S(1)}, u32[]{:S(2)}, u32[]{:S(2)}) collective-permute-start(f32[1,128]{1,0:T(1,128)S(1)} %get-tuple-element.56.own), channel_id=1, source_target_pairs={{0,16},{8,24},{16,0},{24,8},{32,48},{40,56},{48,32},{56,40},{64,80... | collective-permute-start | bytes 1544 | tf_op jit(solution)/shard_map/ppermute | solution.py:399
  12.9 1.8 %near.5 = (f32[8,256,128]{2,1,0:T(8,128)S(1)}, f32[8,1,128]{2,1,0:T(1,128)S(1)}) custom-call(s32[8,32]{1,0:T(8,128)S(1)} %get-tuple-element.70.neighbours, bf16[48,256,128]{2,1,0:T(8,128)(2,1)S(1)} %get-tuple-element.48.window.window_in, bf16[2,32,8,128,128]{4,3,2,1,0:T(8,128)(2,1)S(1)} %bitcast.5), custom_call_target="tpu_custom_call" | custom-call | tf_op jit(solution)/shard_map/near/pallas_call | solution.py:325
  14.8 0.0 collective-permute-done.1.seen
  14.8 0.1 fold.6
  14.9 1.8 %collective-permute-start.4 = (f32[1,128]{1,0:T(1,128)S(1)}, f32[1,128]{1,0:T(1,128)S(1)}, u32[]{:S(2)}, u32[]{:S(2)}) collective-permute-start(f32[1,128]{1,0:T(1,128)S(1)} %get-tuple-element.65.own), channel_id=1, source_target_pairs={{0,32},{8,40},{16,48},{24,56},{32,0},{40,8},{48,16},{56,24},{64,96... | collective-permute-start | bytes 1544 | tf_op jit(solution)/shard_map/ppermute | solution.py:399
  16.7 1.9 %near.6 = (f32[8,256,128]{2,1,0:T(8,128)S(1)}, f32[8,1,128]{2,1,0:T(1,128)S(1)}, bf16[48,256,128]{2,1,0:T(8,128)(2,1)S(1)}) custom-call(s32[8,32]{1,0:T(8,128)S(1)} %get-tuple-element.70.neighbours, bf16[48,256,128]{2,1,0:T(8,128)(2,1)S(1)} %get-tuple-element.48.window.window_in, ...), custom_call_target="tpu_custom_call", output_to_operand_aliasing={{2}: (1, {})} | custom-call | tf_op jit(solution)/shard_map/near/pallas_call | solution.py:325
  18.6 0.1 fold.7
  18.7 3.1 %collective-permute-start.5 = (f32[1,128]{1,0:T(1,128)S(1)}, f32[1,128]{1,0:T(1,128)S(1)}, u32[]{:S(2)}, u32[]{:S(2)}) collective-permute-start(f32[1,128]{1,0:T(1,128)S(1)} %get-tuple-element.75.own), channel_id=1, source_target_pairs={{0,64},{8,72},{16,80},{24,88},{32,96},{40,104},{48,112},{56,120},{... | collective-permute-start | bytes 1544 | tf_op jit(solution)/shard_map/ppermute | solution.py:399
  21.8 2.4 %near.7 = (f32[8,256,128]{2,1,0:T(8,128)S(1)}, f32[8,1,128]{2,1,0:T(1,128)}, f32[32,1,128]{2,1,0:T(1,128)S(1)}) custom-call(s32[8,32]{1,0:T(8,128)S(1)} %get-tuple-element.70.neighbours, bf16[48,256,128]{2,1,0:T(8,128)(2,1)S(1)} %get-tuple-element.71.window, bf16[2,32,8,128,128]{4,3,2,1,0:T(8,128)(2,1)S(1)} %bitcast.5, ...), custom_call_target="tpu_custom_call" | custom-call | tf_op jit(solution)/shard_map/near/pallas_call | solution.py:325
  24.3 0.1 fold.8
  24.3 5.0 %collective-permute-start.7 = (f32[1,128]{1,0:T(1,128)S(1)}, f32[1,128]{1,0:T(1,128)S(1)}, u32[]{:S(2)}, u32[]{:S(2)}) collective-permute-start(f32[1,128]{1,0:T(1,128)S(1)} %get-tuple-element.78.own), channel_id=1, source_target_pairs={{0,128},{8,136},{16,144},{24,152},{32,160},{40,168},{48,176},{56,1... | collective-permute-start | bytes 1544 | tf_op jit(solution)/shard_map/ppermute | solution.py:399
  29.4 2.4 %collective-permute-done.7.seen = f32[1,128]{1,0:T(1,128)S(1)} collective-permute-done((f32[1,128]{1,0:T(1,128)S(1)}, f32[1,128]{1,0:T(1,128)S(1)}, u32[]{:S(2)}, u32[]{:S(2)}) %collective-permute-start.7) | collective-permute-done | bytes 544 | tf_op jit(solution)/shard_map/ppermute | solution.py:399
  31.8 0.6 %fold.9 = (f32[1,128]{1,0:T(1,128)}, f32[1,128]{1,0:T(1,128)S(1)}) custom-call(f32[1,128]{1,0:T(1,128)S(1)} %get-tuple-element.78.own, f32[1,128]{1,0:T(1,128)S(1)} %get-tuple-element.79.arriving, f32[1,128]{1,0:T(1,128)S(1)} %collective-permute-done.7.seen), custom_call_target="tpu_custom_call" | custom-call | tf_op jit(solution)/shard_map/fold/pallas_call | solution.py:212
  32.4 0.1 arrive.1.a
  32.5 0.1 collective-permute-start.8
  32.6 1.2 %collective-permute-done.8.b = f32[128,128]{1,0:T(8,128)S(1)} collective-permute-done((f32[128,128]{1,0:T(8,128)S(1)}, f32[128,128]{1,0:T(8,128)S(1)}, u32[]{:S(2)}, u32[]{:S(2)}) %collective-permute-start.8) | collective-permute-done | bytes 65568 | tf_op jit(solution)/shard_map/ppermute | solution.py:407
  33.8 4.1 %collective-permute-start.11 = (bf16[128,128]{1,0:T(8,128)(2,1)S(1)}, bf16[128,128]{1,0:T(8,128)(2,1)S(1)}, u32[]{:S(2)}, u32[]{:S(2)}) collective-permute-start(bf16[128,128]{1,0:T(8,128)(2,1)S(1)} %pair_sum.1.refs_5_), channel_id=1, source_target_pairs={{0,6},{1,7},{2,0},{3,1},{4,2},{5,3},{6,4},{7,5},{8,14},{9,15},{10,... | collective-permute-start | bytes 98312 | tf_op jit(solution)/shard_map/ppermute | solution.py:412
  37.9 0.5 %collective-permute-start.10 = (bf16[128,128]{1,0:T(8,128)(2,1)S(1)}, bf16[128,128]{1,0:T(8,128)(2,1)S(1)}, u32[]{:S(2)}, u32[]{:S(2)}) collective-permute-start(bf16[128,128]{1,0:T(8,128)(2,1)S(1)} %pair_sum.1.refs_5_), channel_id=1, source_target_pairs={{0,4},{1,5},{2,6},{3,7},{4,0},{5,1},{6,2},{7,3},{8,12},{9,13},{10,... | collective-permute-start | bytes 98312 | tf_op jit(solution)/shard_map/ppermute | solution.py:412
  38.4 0.9 %collective-permute-start.9 = (bf16[128,128]{1,0:T(8,128)(2,1)S(1)}, bf16[128,128]{1,0:T(8,128)(2,1)S(1)}, u32[]{:S(2)}, u32[]{:S(2)}) collective-permute-start(bf16[128,128]{1,0:T(8,128)(2,1)S(1)} %pair_sum.1.refs_5_), channel_id=1, source_target_pairs={{0,2},{1,3},{2,4},{3,5},{4,6},{5,7},{6,0},{7,1},{8,10},{9,11},{10,... | collective-permute-start | bytes 98312 | tf_op jit(solution)/shard_map/ppermute | solution.py:412
  39.3 2.5 %collective-permute-start.6 = (f32[32,1,128]{2,1,0:T(1,128)S(1)}, f32[32,1,128]{2,1,0:T(1,128)S(1)}, u32[]{:S(2)}, u32[]{:S(2)}) collective-permute-start(f32[32,1,128]{2,1,0:T(1,128)S(1)} %get-tuple-element.74), channel_id=1, source_target_pairs={{0,8},{8,16},{16,24},{24,32},{32,40},{40,48},{48,56},{56,64},{64,7... | collective-permute-start | bytes 49160 | tf_op jit(solution)/shard_map/ppermute | solution.py:417
  41.8 5.2 %collective-permute-done.6.refs_4_ = f32[32,1,128]{2,1,0:T(1,128)S(1)} collective-permute-done((f32[32,1,128]{2,1,0:T(1,128)S(1)}, f32[32,1,128]{2,1,0:T(1,128)S(1)}, u32[]{:S(2)}, u32[]{:S(2)}) %collective-permute-start.6) | collective-permute-done | bytes 16416 | tf_op jit(solution)/shard_map/ppermute | solution.py:417
  47.0 2.7 %final.1 = bf16[256,32,128]{2,1,0:T(8,128)(2,1)} custom-call(f32[8,256,128]{2,1,0:T(8,128)S(1)} %get-tuple-element.49.refs_0_, f32[8,256,128]{2,1,0:T(8,128)S(1)} %get-tuple-element.55.refs_1_, f32[8,256,128]{2,1,0:T(8,128)S(1)} %get-tuple-element.64.refs_2_, f32[8,256,128]{2,1,0:T(8,128)S(1)} %get-tuple-element.72.refs_3_, ...), custom_call_target="tpu_custom_call" | custom-call | tf_op jit(solution)/shard_map/final/pallas_call | solution.py:382
  (16 shorter events, 0.0 us)
Async XLA Ops:
  0.0 5.5 %slice-start = ((s8[16777216]{0:T(1024)(128)(4,1)}), s8[4194304]{0:T(1024)(128)(4,1)S(1)}, s32[]{:S(2)}) async-start(s8[16777216]{0:T(1024)(128)(4,1)} %bitcast.4), calls=%async_computation | async-start | bytes 8388608
  0.0 5.5 %slice-start.1 = ((s8[16777216]{0:T(1024)(128)(4,1)}), s8[4194304]{0:T(1024)(128)(4,1)S(1)}, s32[]{:S(2)}) async-start(s8[16777216]{0:T(1024)(128)(4,1)} %bitcast.4), calls=%async_computation.1 | async-start | bytes 8388608
  0.0 5.5 %slice-start.2 = ((s8[16777216]{0:T(1024)(128)(4,1)}), s8[4194304]{0:T(1024)(128)(4,1)S(1)}, s32[]{:S(2)}) async-start(s8[16777216]{0:T(1024)(128)(4,1)} %bitcast.4), calls=%async_computation.2 | async-start | bytes 8388608
  0.0 6.7 %slice-start.3 = ((s8[16777216]{0:T(1024)(128)(4,1)}), s8[4194304]{0:T(1024)(128)(4,1)S(1)}, s32[]{:S(2)}) async-start(s8[16777216]{0:T(1024)(128)(4,1)} %bitcast.4), calls=%async_computation.3 | async-start | bytes 8388608
  2.9 13.8 %collective-permute-start.2 = (bf16[8,256,128]{2,1,0:T(8,128)(2,1)S(1)}, bf16[8,256,128]{2,1,0:T(8,128)(2,1)S(1)}, u32[]{:S(2)}, u32[]{:S(2)}) collective-permute-start(bf16[8,256,128]{2,1,0:T(8,128)(2,1)S(1)} %get-tuple-element.62), channel_id=1, source_target_pairs={{0,1},{1,0},{2,3},{3,2},{4,5},{5,4},{6,7},{7,6},{8,9},{9,8},{10,11... | collective-permute-start | bytes 1572872 | tf_op jit(solution)/shard_map/ppermute | solution.py:407
  3.0 13.7 %collective-permute-start.3 = (bf16[8,256,128]{2,1,0:T(8,128)(2,1)S(1)}, bf16[8,256,128]{2,1,0:T(8,128)(2,1)S(1)}, u32[]{:S(2)}, u32[]{:S(2)}) collective-permute-start(bf16[8,256,128]{2,1,0:T(8,128)(2,1)S(1)} %get-tuple-element.63), channel_id=1, source_target_pairs={{1,2},{2,1},{3,4},{4,3},{5,6},{6,5},{9,10},{10,9},{11,12},{12,11},... | collective-permute-start | bytes 1572872 | tf_op jit(solution)/shard_map/ppermute | solution.py:407
  3.9 5.7 %collective-permute-start = (f32[1,128]{1,0:T(1,128)S(1)}, f32[1,128]{1,0:T(1,128)S(1)}, u32[]{:S(2)}, u32[]{:S(2)}) collective-permute-start(f32[1,128]{1,0:T(1,128)S(1)} %get-tuple-element.50.own), channel_id=1, source_target_pairs={{0,8},{8,0},{16,24},{24,16},{32,40},{40,32},{48,56},{56,48},{64,72... | collective-permute-start | bytes 1544 | tf_op jit(solution)/shard_map/ppermute | solution.py:399
  9.7 5.1 %collective-permute-start.1 = (f32[1,128]{1,0:T(1,128)S(1)}, f32[1,128]{1,0:T(1,128)S(1)}, u32[]{:S(2)}, u32[]{:S(2)}) collective-permute-start(f32[1,128]{1,0:T(1,128)S(1)} %get-tuple-element.56.own), channel_id=1, source_target_pairs={{0,16},{8,24},{16,0},{24,8},{32,48},{40,56},{48,32},{56,40},{64,80... | collective-permute-start | bytes 1544 | tf_op jit(solution)/shard_map/ppermute | solution.py:399
  14.9 3.8 %collective-permute-start.4 = (f32[1,128]{1,0:T(1,128)S(1)}, f32[1,128]{1,0:T(1,128)S(1)}, u32[]{:S(2)}, u32[]{:S(2)}) collective-permute-start(f32[1,128]{1,0:T(1,128)S(1)} %get-tuple-element.65.own), channel_id=1, source_target_pairs={{0,32},{8,40},{16,48},{24,56},{32,0},{40,8},{48,16},{56,24},{64,96... | collective-permute-start | bytes 1544 | tf_op jit(solution)/shard_map/ppermute | solution.py:399
  18.7 5.5 %collective-permute-start.5 = (f32[1,128]{1,0:T(1,128)S(1)}, f32[1,128]{1,0:T(1,128)S(1)}, u32[]{:S(2)}, u32[]{:S(2)}) collective-permute-start(f32[1,128]{1,0:T(1,128)S(1)} %get-tuple-element.75.own), channel_id=1, source_target_pairs={{0,64},{8,72},{16,80},{24,88},{32,96},{40,104},{48,112},{56,120},{... | collective-permute-start | bytes 1544 | tf_op jit(solution)/shard_map/ppermute | solution.py:399
  24.3 7.5 %collective-permute-start.7 = (f32[1,128]{1,0:T(1,128)S(1)}, f32[1,128]{1,0:T(1,128)S(1)}, u32[]{:S(2)}, u32[]{:S(2)}) collective-permute-start(f32[1,128]{1,0:T(1,128)S(1)} %get-tuple-element.78.own), channel_id=1, source_target_pairs={{0,128},{8,136},{16,144},{24,152},{32,160},{40,168},{48,176},{56,1... | collective-permute-start | bytes 1544 | tf_op jit(solution)/shard_map/ppermute | solution.py:399
  32.5 1.3 %collective-permute-start.8 = (f32[128,128]{1,0:T(8,128)S(1)}, f32[128,128]{1,0:T(8,128)S(1)}, u32[]{:S(2)}, u32[]{:S(2)}) collective-permute-start(f32[128,128]{1,0:T(8,128)S(1)} %arrive.1.a), channel_id=1, source_target_pairs={{0,1},{1,0},{2,3},{3,2},{4,5},{5,4},{6,7},{7,6},{8,9},{9,8},{10,11... | collective-permute-start | bytes 196616 | tf_op jit(solution)/shard_map/ppermute | solution.py:407
  33.8 13.2 %collective-permute-start.11 = (bf16[128,128]{1,0:T(8,128)(2,1)S(1)}, bf16[128,128]{1,0:T(8,128)(2,1)S(1)}, u32[]{:S(2)}, u32[]{:S(2)}) collective-permute-start(bf16[128,128]{1,0:T(8,128)(2,1)S(1)} %pair_sum.1.refs_5_), channel_id=1, source_target_pairs={{0,6},{1,7},{2,0},{3,1},{4,2},{5,3},{6,4},{7,5},{8,14},{9,15},{10,... | collective-permute-start | bytes 98312 | tf_op jit(solution)/shard_map/ppermute | solution.py:412
  37.9 9.1 %collective-permute-start.10 = (bf16[128,128]{1,0:T(8,128)(2,1)S(1)}, bf16[128,128]{1,0:T(8,128)(2,1)S(1)}, u32[]{:S(2)}, u32[]{:S(2)}) collective-permute-start(bf16[128,128]{1,0:T(8,128)(2,1)S(1)} %pair_sum.1.refs_5_), channel_id=1, source_target_pairs={{0,4},{1,5},{2,6},{3,7},{4,0},{5,1},{6,2},{7,3},{8,12},{9,13},{10,... | collective-permute-start | bytes 98312 | tf_op jit(solution)/shard_map/ppermute | solution.py:412
  38.4 8.6 %collective-permute-start.9 = (bf16[128,128]{1,0:T(8,128)(2,1)S(1)}, bf16[128,128]{1,0:T(8,128)(2,1)S(1)}, u32[]{:S(2)}, u32[]{:S(2)}) collective-permute-start(bf16[128,128]{1,0:T(8,128)(2,1)S(1)} %pair_sum.1.refs_5_), channel_id=1, source_target_pairs={{0,2},{1,3},{2,4},{3,5},{4,6},{5,7},{6,0},{7,1},{8,10},{9,11},{10,... | collective-permute-start | bytes 98312 | tf_op jit(solution)/shard_map/ppermute | solution.py:412
  39.3 7.7 %collective-permute-start.6 = (f32[32,1,128]{2,1,0:T(1,128)S(1)}, f32[32,1,128]{2,1,0:T(1,128)S(1)}, u32[]{:S(2)}, u32[]{:S(2)}) collective-permute-start(f32[32,1,128]{2,1,0:T(1,128)S(1)} %get-tuple-element.74), channel_id=1, source_target_pairs={{0,8},{8,16},{16,24},{24,32},{32,40},{40,48},{48,56},{56,64},{64,7... | collective-permute-start | bytes 49160 | tf_op jit(solution)/shard_map/ppermute | solution.py:417

commit v5 on v3

--- a/solution.py
+++ b/solution.py
@@ -216,18 +216,18 @@
     )(ends, far, decay)
 
 
-def pair_kernel(a, b, out):
-    out[...] = (a[...] + b[...]).astype(BF16)
-
-
-def pair_sum(a, b):
+def sum_kernel(a, b, out):
+    out[...] = a[...] + b[...]
+
+
+def summed(a, b):
     return pl.pallas_call(
-        pair_kernel,
+        sum_kernel,
         in_specs=[VMEM] * 2,
         out_specs=VMEM,
-        out_shape=jax.ShapeDtypeStruct(a.shape, BF16),
-        compiler_params=pltpu.CompilerParams(vmem_limit_bytes=4 << 20),
-        name="pair_sum",
+        out_shape=jax.ShapeDtypeStruct(a.shape, F32),
+        compiler_params=pltpu.CompilerParams(vmem_limit_bytes=1 << 20),
+        name="summed",
     )(a, b)
 
 
@@ -252,9 +252,41 @@
     return now + shifted_down(later, 1, 0.0), later[steps - 1 :]
 
 
+def fetches_of(blocks, lags, groups, held, sems):
+    waits, at = [], 0
+    for k, (start, count) in enumerate(groups):
+        waits.append(
+            [
+                pltpu.make_async_copy(
+                    blocks.at[lag, pl.ds(start, count)],
+                    held.at[n, pl.ds(at, count)],
+                    sems.at[n, k],
+                )
+                for n, lag in enumerate(lags)
+            ]
+        )
+        at += count
+    return waits
+
+
+def clusters_of(groups):
+    return tuple(c for start, count in groups for c in range(start, start + count))
+
+
+def near_groups(neighbours, window, groups, fetches, held, put):
+    i = 0
+    for (start, count), some in zip(groups, fetches):
+        for fetch in some:
+            fetch.wait()
+        for cluster in range(start, start + count):
+            blocks_here = [held.at[n, i] for n in range(held.shape[0])]
+            put(i, cluster, *near_of(neighbours, window, blocks_here, cluster))
+            i += 1
+
+
 def inner_kernel(
-    full,
-    ends_only,
+    groups,
+    later_groups,
     table,
     window,
     blocks,
@@ -269,56 +301,46 @@
     later_sems,
     out_sems,
 ):
-    count = len(full)
     steps = window.shape[1]
     lags = blocks.shape[0]
-    fetches = [
-        [
-            pltpu.make_async_copy(blocks.at[lag, c], held.at[lag, i], sems.at[lag, i])
-            for lag in range(lags)
-        ]
-        for i, c in enumerate(full)
-    ]
-    later_fetches = [
-        pltpu.make_async_copy(blocks.at[lags - 1, c], held_later.at[i], later_sems.at[i])
-        for i, c in enumerate(ends_only)
-    ]
-    listed = pltpu.make_async_copy(table, neighbours, out_sems.at[count + 1])
+    listed = pltpu.make_async_copy(table, neighbours, out_sems.at[0])
     listed.start()
-    for some in fetches:
+    fetches = fetches_of(blocks, range(lags), groups, held, sems)
+    later_fetches = fetches_of(blocks, (lags - 1,), later_groups, held_later, later_sems)
+    for some in fetches + later_fetches:
         for fetch in some:
             fetch.start()
-    for fetch in later_fetches:
-        fetch.start()
     listed.wait()
-    stores = []
-    for i, cluster in enumerate(full):
-        for fetch in fetches[i]:
-            fetch.wait()
-        blocks_here = [held.at[lag, i] for lag in range(lags)]
-        x, last = near_of(neighbours, window, blocks_here, cluster)
+
+    def put(i, cluster, x, last):
         found[i] = x
         lines[cluster - REACH] = last
-        stores.append(pltpu.make_async_copy(found.at[i], near.at[i], out_sems.at[i]))
-        stores[-1].start()
-    for i, cluster in enumerate(ends_only):
-        later_fetches[i].wait()
-        x = gathered(neighbours, window, cluster, pl.ds(steps - 16, 16))
-        y = jnp.dot(x, stacked(held_later.at[i]), preferred_element_type=F32)
-        lines[cluster - REACH] = y[15:]
-    stores.append(pltpu.make_async_copy(lines, carry, out_sems.at[count]))
-    stores[-1].start()
-    for store in stores:
-        store.wait()
-
-
-def inner_near(neighbours, window, blocks, full, ends_only):
+
+    near_groups(neighbours, window, groups, fetches, held, put)
+    store = pltpu.make_async_copy(found, near, out_sems.at[1])
+    store.start()
+    i = 0
+    for (start, count), some in zip(later_groups, later_fetches):
+        for fetch in some:
+            fetch.wait()
+        for cluster in range(start, start + count):
+            x = gathered(neighbours, window, cluster, pl.ds(steps - 16, 16))
+            y = jnp.dot(x, stacked(held_later.at[0, i]), preferred_element_type=F32)
+            lines[cluster - REACH] = y[15:]
+            i += 1
+    lines_store = pltpu.make_async_copy(lines, carry, out_sems.at[2])
+    lines_store.start()
+    store.wait()
+    lines_store.wait()
+
+
+def inner_near(neighbours, window, blocks, groups, later_groups):
     steps, unknowns = window.shape[1:]
     lags, clusters, nb = blocks.shape[:3]
-    count, more = len(full), len(ends_only)
+    count, more = len(clusters_of(groups)), len(clusters_of(later_groups))
     block = (nb, unknowns, unknowns)
     return pl.pallas_call(
-        functools.partial(inner_kernel, full, ends_only),
+        functools.partial(inner_kernel, groups, later_groups),
         in_specs=[HBM, VMEM, HBM],
         out_specs=[HBM] * 2,
         out_shape=[
@@ -328,12 +350,12 @@
         scratch_shapes=[
             pltpu.SMEM(neighbours.shape, jnp.int32),
             pltpu.VMEM((lags, count, *block), BF16),
-            pltpu.VMEM((more, *block), BF16),
+            pltpu.VMEM((1, more, *block), BF16),
             pltpu.VMEM((count, steps, unknowns), F32),
             pltpu.VMEM((count + more, 1, unknowns), F32),
-            pltpu.SemaphoreType.DMA((lags, count)),
-            pltpu.SemaphoreType.DMA((more,)),
-            pltpu.SemaphoreType.DMA((count + 2,)),
+            pltpu.SemaphoreType.DMA((lags, len(groups))),
+            pltpu.SemaphoreType.DMA((1, len(later_groups))),
+            pltpu.SemaphoreType.DMA((3,)),
         ],
         compiler_params=pltpu.CompilerParams(vmem_limit_bytes=16 << 20),
         name="inner",
@@ -341,7 +363,7 @@
 
 
 def edge_kernel(
-    order,
+    groups,
     table,
     window_in,
     from_pair,
@@ -352,6 +374,8 @@
     carry,
     window,
     neighbours,
+    held,
+    side_sems,
     sems,
 ):
     del window_in
@@ -359,106 +383,124 @@
     above = window.shape[0] - REACH
 
     def copy(src, dst, k):
-        return pltpu.make_async_copy(src, dst, sems.at[k])
+        return pltpu.make_async_copy(src, dst, side_sems.at[k])
 
     sides = [
+        copy(table, neighbours, 3),
         copy(from_pair, window.at[pl.ds(jnp.where(even, above, 0), REACH)], 0),
         copy(from_other, window.at[pl.ds(jnp.where(even, 0, above), REACH)], 1),
         copy(inner_carry, carry.at[pl.ds(REACH, inner_carry.shape[0])], 2),
-        copy(table, neighbours, 3),
     ]
+    fetches = fetches_of(blocks, range(blocks.shape[0]), groups, held, sems)
     for c in sides:
         c.start()
+    for some in fetches:
+        for fetch in some:
+            fetch.start()
     for c in sides:
         c.wait()
-    for i, cluster in enumerate(order):
-        blocks_here = [blocks.at[lag, cluster] for lag in range(blocks.shape[0])]
-        near[i], carry[cluster] = near_of(neighbours, window, blocks_here, cluster)
-
-
-def edge_near(neighbours, window, from_pair, from_other, blocks, inner_carry, order):
+
+    def put(i, cluster, x, last):
+        near[i] = x
+        carry[cluster] = last
+
+    near_groups(neighbours, window, groups, fetches, held, put)
+
+
+def edge_near(neighbours, window, from_pair, from_other, blocks, inner_carry, groups):
     steps, unknowns = window.shape[1:]
-    clusters = blocks.shape[1]
+    lags, clusters, nb = blocks.shape[:3]
+    count = len(clusters_of(groups))
     return pl.pallas_call(
-        functools.partial(edge_kernel, order),
-        in_specs=[HBM, VMEM, HBM, HBM, VMEM, HBM],
+        functools.partial(edge_kernel, groups),
+        in_specs=[HBM, VMEM, HBM, HBM, HBM, HBM],
         out_specs=[VMEM] * 3,
         out_shape=[
-            jax.ShapeDtypeStruct((len(order), steps, unknowns), F32),
+            jax.ShapeDtypeStruct((count, steps, unknowns), F32),
             jax.ShapeDtypeStruct((clusters, 1, unknowns), F32),
             jax.ShapeDtypeStruct(window.shape, BF16),
         ],
         scratch_shapes=[
             pltpu.SMEM(neighbours.shape, jnp.int32),
+            pltpu.VMEM((lags, count, nb, unknowns, unknowns), BF16),
             pltpu.SemaphoreType.DMA((4,)),
+            pltpu.SemaphoreType.DMA((lags, len(groups))),
         ],
         input_output_aliases={1: 2},
-        compiler_params=pltpu.CompilerParams(vmem_limit_bytes=8 << 20),
+        compiler_params=pltpu.CompilerParams(vmem_limit_bytes=12 << 20),
         name="edge",
     )(
         in_hbm(neighbours),
         window,
         in_hbm(from_pair),
         in_hbm(from_other),
-        in_vmem(blocks),
+        in_hbm(blocks),
         in_hbm(inner_carry),
     )
 
 
 def rest_kernel(
-    order, table, window, blocks, inner, from_moments, near, maps, neighbours, rows, sems
+    groups, table, window, blocks, inner, from_moments, near, maps, neighbours, rows, held, side_sems, sems
 ):
-    listed = pltpu.make_async_copy(table, neighbours, sems.at[2])
-    listed.start()
-    fetches = [
-        pltpu.make_async_copy(from_moments, rows, sems.at[0]),
-        pltpu.make_async_copy(inner, near.at[pl.ds(len(order), inner.shape[0])], sems.at[1]),
+    count = held.shape[1]
+    sides = [
+        pltpu.make_async_copy(table, neighbours, side_sems.at[0]),
+        pltpu.make_async_copy(from_moments, rows, side_sems.at[1]),
+        pltpu.make_async_copy(inner, near.at[pl.ds(count, inner.shape[0])], side_sems.at[2]),
     ]
-    for fetch in fetches:
-        fetch.start()
-    listed.wait()
-    for i, cluster in enumerate(order):
-        blocks_here = [blocks.at[lag, cluster] for lag in range(blocks.shape[0])]
-        near[i], _ = near_of(neighbours, window, blocks_here, cluster)
-    fetches[0].wait()
+    fetches = fetches_of(blocks, range(blocks.shape[0]), groups, held, sems)
+    for c in sides[:2]:
+        c.start()
+    for some in fetches:
+        for fetch in some:
+            fetch.start()
+    sides[2].start()
+    sides[0].wait()
+    sides[1].wait()
     w = jnp.transpose(rows[...], (1, 0, 2))
     for p in range(maps.shape[0]):
         x = jnp.concatenate([w[2 * p], w[2 * p + 1]], axis=1)
         maps[p] = jnp.concatenate([x, x], axis=0)
-    fetches[1].wait()
-
-
-def rest_near(neighbours, window, blocks, inner, from_moments, order):
+
+    def put(i, cluster, x, last):
+        near[i] = x
+
+    near_groups(neighbours, window, groups, fetches, held, put)
+    sides[2].wait()
+
+
+def rest_near(neighbours, window, blocks, inner, from_moments, groups):
     steps, unknowns = window.shape[1:]
-    clusters = blocks.shape[1]
+    lags, clusters, nb = blocks.shape[:3]
     terms = from_moments.shape[0]
+    count = len(clusters_of(groups))
     return pl.pallas_call(
-        functools.partial(rest_kernel, order),
-        in_specs=[HBM, VMEM, VMEM, HBM, HBM],
+        functools.partial(rest_kernel, groups),
+        in_specs=[HBM, VMEM, HBM, HBM, HBM],
         out_specs=[VMEM] * 2,
         out_shape=[
-            jax.ShapeDtypeStruct((len(order) + inner.shape[0], steps, unknowns), F32),
+            jax.ShapeDtypeStruct((count + inner.shape[0], steps, unknowns), F32),
             jax.ShapeDtypeStruct((clusters // 2, 2 * terms, 2 * unknowns), BF16),
         ],
         scratch_shapes=[
             pltpu.SMEM(neighbours.shape, jnp.int32),
             pltpu.VMEM(from_moments.shape, BF16),
+            pltpu.VMEM((lags, count, nb, unknowns, unknowns), BF16),
             pltpu.SemaphoreType.DMA((3,)),
-        ],
-        compiler_params=pltpu.CompilerParams(vmem_limit_bytes=8 << 20),
+            pltpu.SemaphoreType.DMA((lags, len(groups))),
+        ],
+        compiler_params=pltpu.CompilerParams(vmem_limit_bytes=10 << 20),
         name="rest",
-    )(in_hbm(neighbours), window, in_vmem(blocks), in_hbm(inner), in_hbm(from_moments))
+    )(in_hbm(neighbours), window, in_hbm(blocks), in_hbm(inner), in_hbm(from_moments))
 
 
 def final_kernel(places, edge, rest, carry, *refs):
-    parts = refs[:4]
-    maps, live, out, major, done, sems = refs[4:]
+    parts = refs[:-6]
+    maps, live, out, major, done, sems = refs[-6:]
     steps, clusters, unknowns = out.shape
     terms = maps.shape[1] // 2
     first = lax.axis_index("space") * clusters
-    total = parts[0][...].astype(F32)
-    for part in parts[1:]:
-        total = total + part[...].astype(F32)
+    total = sum(part[...] for part in parts)
     lane = lax.broadcasted_iota(jnp.int32, total.shape, 1)
     size = steps // 2
     chunk = 32
@@ -514,6 +556,11 @@
     return lax.all_to_all(x, axis, split_axis=0, concat_axis=0, tiled=True)
 
 
+def across(x, axis, bit):
+    count = lax.axis_size(axis)
+    return lax.ppermute(x, axis, [(i, i ^ bit) for i in range(count)])
+
+
 def swapped_from(x, axis, start):
     count = lax.axis_size(axis)
     route = []
@@ -522,11 +569,6 @@
     return lax.ppermute(x, axis, route)
 
 
-def from_chip(x, axis, distance):
-    count = lax.axis_size(axis)
-    return lax.ppermute(x, axis, [(i, (i + 2 * distance) % count) for i in range(count)])
-
-
 def passed_on(x, axis):
     count = lax.axis_size(axis)
     return lax.ppermute(x, axis, [(i, i + 1) for i in range(count - 1)])
@@ -534,7 +576,7 @@
 
 def local(density, active, neighbours, near_blocks, to_moments, from_moments, decay_rates, lengths):
     steps = density.shape[0]
-    slabs, chips = lax.axis_size("tm"), lax.axis_size("space") // 2
+    slabs = lax.axis_size("tm")
     window, pair, other, far, decay, ends, live = prep(
         density,
         active.reshape(1, steps),
@@ -548,22 +590,27 @@
     from_other = swapped_from(other, "space", 1)
     neighbours = neighbours.T
     clusters = density.shape[1]
-    middle = clusters // 2
-    full = tuple(range(middle - REACH // 2, middle + REACH // 2))
-    sides = tuple(range(REACH)) + tuple(range(clusters - REACH, clusters))
-    others = tuple(c for c in range(clusters) if c not in full + sides)
+    end = clusters - REACH
+    full = ((12, 2), (14, 2), (16, 4))
+    others = ((8, 4), (20, 4))
+    sides = ((0, 2), (2, 2), (4, 4), (end, 4), (end + 4, 4))
     inner, inner_carry = inner_near(neighbours, window, near_blocks, full, others)
     ends, inner, inner_carry = lax.optimization_barrier((ends, inner, inner_carry))
     mine = arrive(ends, far, decay)
-    mine = pair_sum(mine, swapped_from(mine, "space", 0))
-    parts = [mine] + [from_chip(mine, "space", d) for d in range(1, chips)]
+    mine = summed(mine, across(mine, "space", 1))
+    theirs = across(mine, "space", 2)
     inner_carry, mine = lax.optimization_barrier((inner_carry, mine))
     edge, carry, window = edge_near(
         neighbours, window, from_pair, from_other, near_blocks, inner_carry, sides
     )
+    theirs, carry = lax.optimization_barrier((theirs, carry))
+    mine = summed(mine, theirs)
+    theirs = across(mine, "space", 4)
     carry = passed_on(carry, "tm")
+    inner, mine = lax.optimization_barrier((inner, mine))
     rest, maps = rest_near(neighbours, window, near_blocks, inner, from_moments, others)
-    return final(edge, rest, carry, parts, maps, live, (sides, others + full))
+    orders = (clusters_of(sides), clusters_of(others + full))
+    return final(edge, rest, carry, (mine, theirs), maps, live, orders)
 
 
 def solution(mesh):

time: 45.7 us -> 46.5 us (1.018)
  starting transfers between devices: 23.5 us -> 20.3 us
  Pallas kernels: 18.4 us -> 20.6 us
  waiting for transfers between devices: 3.44 us -> 5.3 us
    pallas_call x4 -> x5, Pallas kernels: 12.4 us -> 14.6 us  [the longest x1 6.83 us: edge_near(): pl.pallas_call(functools.partial(edge_kernel, groups), in_specs=[HBM, VME...]
    all_to_all x1, waiting for transfers between devices: 0.4 us -> 2.59 us  [exchanged(): return lax.all_to_all(x, axis, split_axis=0, concat_axis=0, tiled=True)]
    ppermute x3 -> x2, starting transfers between devices: 3.36 us -> 1.56 us  [swapped_from(): return lax.ppermute(x, axis, route)]
    ppermute x3, waiting for transfers between devices: 0.01 us -> 1.25 us  [across(): return lax.ppermute(x, axis, [(i, i ^ bit) for i in range(count)])]
    ppermute x3, starting transfers between devices: 5.44 us -> 4.49 us  [across(): return lax.ppermute(x, axis, [(i, i ^ bit) for i in range(count)])]
    ppermute x3 -> x2, waiting for transfers between devices: 0.91 us -> 0.01 us  [swapped_from(): return lax.ppermute(x, axis, route)]
    ppermute x1, waiting for transfers between devices: 2.13 us -> 1.46 us  [passed_on(): return lax.ppermute(x, axis, [(i, i + 1) for i in range(count - 1)])]
    ppermute x1, starting transfers between devices: 3.37 us -> 2.9 us  [passed_on(): return lax.ppermute(x, axis, [(i, i + 1) for i in range(count - 1)])]
  transfers between devices with their start and end apart: 8 -> 7, of which waited for: 3 -> 3; matrix products, arithmetic and copies ran while one was open for 0% -> 0% of each run, Pallas kernels for 28% -> 32%
where the time goes in v5:
time: 46.5 us; the launch traced here: 46.3 us
  Pallas kernels  20.6 us (44%)
  starting transfers between devices  20.3 us (44%)
  waiting for transfers between devices  5.3 us (11%)
    all_to_all x1, starting transfers between devices, exchanged(): return lax.all_to_all(x, axis, split_axis=0, concat_axis=0, tiled=True)  11.4 us
    pallas_call x1, Pallas kernels, edge_near(): pl.pallas_call(functools.partial(edge_kernel, groups), in_specs=[HBM, VME...  6.83 us
    ppermute x3, starting transfers between devices, across(): return lax.ppermute(x, axis, [(i, i ^ bit) for i in range(count)])  4.49 us
    pallas_call x1, Pallas kernels, inner_near(): pl.pallas_call(functools.partial(inner_kernel, groups, later_groups), in_...  4.4 us
    pallas_call x1, Pallas kernels, rest_near(): pl.pallas_call(functools.partial(rest_kernel, groups), in_specs=[HBM, VME...  3.35 us
    pallas_call x1, Pallas kernels, prep(): pl.pallas_call(prep_kernel, in_specs=[HBM] * 5, out_specs=[VMEM, HBM, HBM...  3.23 us
    ppermute x1, starting transfers between devices, passed_on(): return lax.ppermute(x, axis, [(i, i + 1) for i in range(count - 1)])  2.9 us
    pallas_call x1, Pallas kernels, final(): pl.pallas_call(functools.partial(final_kernel, places), in_specs=[VMEM] *...  2.62 us
  transfers between devices with their start and end apart: 7, of which 3 were waited for; matrix products, arithmetic and copies ran while one was open for 0% of the time, Pallas kernels for 32%

profile of v5, /device:TPU:32, one launch (start us, length us, event | category | flops | bytes accessed | tf_op | source)
XLA Modules:
  0.0 46.3 jit_solution(9063880546206190877)
XLA Ops:
  0.0 3.2 %prep.1 = (bf16[48,256,128]{2,1,0:T(8,128)(2,1)S(1)}, bf16[8,256,128]{2,1,0:T(8,128)(2,1)}, bf16[8,256,128]{2,1,0:T(8,128)(2,1)}, f32[256,128]{1,0:T(8,128)S(1)}...) custom-call(bf16[256,32,128]{2,1,0:T(8,128)(2,1)} %density.1, s32[1,256]{1,0:T(1,128)} %bitcast.7, ...), custom_call_target="tpu_custom_call" | custom-call | tf_op jit(solution)/shard_map/prep/pallas_call | solution.py:158
  3.2 11.4 %all-to-all-start = ((f32[32,1,128]{2,1,0:T(1,128)}), f32[32,1,128]{2,1,0:T(1,128)S(1)}, u32[]{:S(2)}, u32[]{:S(2)}) async-start(f32[32,1,128]{2,1,0:T(1,128)} %get-tuple-element.31), calls=%async_computation | async-start | bytes 32768 | tf_op jit(solution)/shard_map/all_to_all | solution.py:556
  14.6 0.1 collective-permute-start
  14.7 1.5 %collective-permute-start.1 = (bf16[8,256,128]{2,1,0:T(8,128)(2,1)}, bf16[8,256,128]{2,1,0:T(8,128)(2,1)}, u32[]{:S(2)}, u32[]{:S(2)}) collective-permute-start(bf16[8,256,128]{2,1,0:T(8,128)(2,1)} %get-tuple-element.30), channel_id=1, source_target_pairs={{1,2},{2,1},{3,4},{4,3},{5,6},{6,5},{9,10},{10,9},{11,12},{12,11},... | collective-permute-start | bytes 1572872 | tf_op jit(solution)/shard_map/ppermute | solution.py:569
  16.2 4.4 %inner.1 = (f32[8,256,128]{2,1,0:T(8,128)}, f32[16,1,128]{2,1,0:T(1,128)}) custom-call(s32[8,32]{1,0:T(8,128)} %bitcast.4, bf16[48,256,128]{2,1,0:T(8,128)(2,1)S(1)} %get-tuple-element.28.window.window_in, bf16[2,32,8,128,128]{4,3,2,1,0:T(8,128)(2,1)} %blocks.5), custom_call_target="tpu_custom_call" | custom-call | tf_op jit(solution)/shard_map/inner/pallas_call | solution.py:342
  20.6 2.6 %all-to-all-done.ends = f32[32,1,128]{2,1,0:T(1,128)S(1)} async-done(((f32[32,1,128]{2,1,0:T(1,128)}), f32[32,1,128]{2,1,0:T(1,128)S(1)}, u32[]{:S(2)}, u32[]{:S(2)}) %all-to-all-start) | async-done | bytes 16416 | tf_op jit(solution)/shard_map/all_to_all | solution.py:556
  23.2 0.2 arrive.1.a
  23.4 0.1 collective-permute-start.2
  23.5 1.2 %collective-permute-done.2.b = f32[128,128]{1,0:T(8,128)S(1)} collective-permute-done((f32[128,128]{1,0:T(8,128)S(1)}, f32[128,128]{1,0:T(8,128)S(1)}, u32[]{:S(2)}, u32[]{:S(2)}) %collective-permute-start.2) | collective-permute-done | bytes 65568 | tf_op jit(solution)/shard_map/ppermute | solution.py:561
  24.7 1.6 %collective-permute-start.3 = (f32[128,128]{1,0:T(8,128)S(1)}, f32[128,128]{1,0:T(8,128)S(1)}, u32[]{:S(2)}, u32[]{:S(2)}) collective-permute-start(f32[128,128]{1,0:T(8,128)S(1)} %summed.2.a), channel_id=1, source_target_pairs={{0,2},{1,3},{2,0},{3,1},{4,6},{5,7},{6,4},{7,5},{8,10},{9,11},{10,... | collective-permute-start | bytes 196616 | tf_op jit(solution)/shard_map/ppermute | solution.py:561
  26.3 0.0 collective-permute-done.from_pair
  26.3 0.0 collective-permute-done.1.from_other
  26.3 6.8 %edge.1 = (f32[16,256,128]{2,1,0:T(8,128)S(1)}, f32[32,1,128]{2,1,0:T(1,128)S(1)}, bf16[48,256,128]{2,1,0:T(8,128)(2,1)S(1)}) custom-call(s32[8,32]{1,0:T(8,128)} %bitcast.5, bf16[48,256,128]{2,1,0:T(8,128)(2,1)S(1)} %get-tuple-element.28.window.window_in, bf16[8,256,128]{2,1,0:T(8,128)(2,1)} %collective-permute-done.from_pair, ...), custom_call_target="tpu_custom_call", output_to_operand_aliasing={{2}: (1, {})} | custom-call | tf_op jit(solution)/shard_map/edge/pallas_call | solution.py:414
  33.1 0.0 collective-permute-done.3.b
  33.2 2.8 %collective-permute-start.5 = (f32[128,128]{1,0:T(8,128)S(1)}, f32[128,128]{1,0:T(8,128)S(1)}, u32[]{:S(2)}, u32[]{:S(2)}) collective-permute-start(f32[128,128]{1,0:T(8,128)S(1)} %summed.3.refs_0_), channel_id=1, source_target_pairs={{0,4},{1,5},{2,6},{3,7},{4,0},{5,1},{6,2},{7,3},{8,12},{9,13},{10,... | collective-permute-start | bytes 196616 | tf_op jit(solution)/shard_map/ppermute | solution.py:561
  36.0 2.9 %collective-permute-start.4 = (f32[32,1,128]{2,1,0:T(1,128)S(1)}, f32[32,1,128]{2,1,0:T(1,128)S(1)}, u32[]{:S(2)}, u32[]{:S(2)}) collective-permute-start(f32[32,1,128]{2,1,0:T(1,128)S(1)} %get-tuple-element.47), channel_id=1, source_target_pairs={{0,8},{8,16},{16,24},{24,32},{32,40},{40,48},{48,56},{56,64},{64,7... | collective-permute-start | bytes 49160 | tf_op jit(solution)/shard_map/ppermute | solution.py:574
  38.9 3.4 %rest.1 = (f32[16,256,128]{2,1,0:T(8,128)S(1)}, bf16[16,128,256]{2,1,0:T(8,128)(2,1)S(1)}) custom-call(s32[8,32]{1,0:T(8,128)} %bitcast.6, bf16[48,256,128]{2,1,0:T(8,128)(2,1)S(1)} %get-tuple-element.40.window, bf16[2,32,8,128,128]{4,3,2,1,0:T(8,128)(2,1)} %blocks.5, f32[8,256,128]{2,1,0:T(8,128)} %get-tuple-element.45.inner, bf16[64,32,128]{2,1,0:T(8,128)(2,1)} %from_moments.1), custom_call_target="tpu_custom_call" | custom-call | tf_op jit(solution)/shard_map/rest/pallas_call | solution.py:477
  42.2 1.5 %collective-permute-done.4.carry = f32[32,1,128]{2,1,0:T(1,128)S(1)} collective-permute-done((f32[32,1,128]{2,1,0:T(1,128)S(1)}, f32[32,1,128]{2,1,0:T(1,128)S(1)}, u32[]{:S(2)}, u32[]{:S(2)}) %collective-permute-start.4) | collective-permute-done | bytes 16416 | tf_op jit(solution)/shard_map/ppermute | solution.py:574
  43.7 0.0 collective-permute-done.5.refs_1_
  43.7 2.6 %final.1 = bf16[256,32,128]{2,1,0:T(8,128)(2,1)} custom-call(f32[16,256,128]{2,1,0:T(8,128)S(1)} %get-tuple-element.39.edge, f32[16,256,128]{2,1,0:T(8,128)S(1)} %get-tuple-element.46.rest, f32[32,1,128]{2,1,0:T(1,128)S(1)} %collective-permute-done.4.carry, f32[128,128]{1,0:T(8,128)S(1)} %summed.3.refs_0_, f32[128,128]{1,0:T(8,128)S(1)} %collective-permute-done.5.refs_1_, ...), custom_call_target="tpu_custom_call" | custom-call | tf_op jit(solution)/shard_map/final/pallas_call | solution.py:540
  (2 shorter events, 0.0 us)
Async XLA Ops:
  3.2 19.9 %all-to-all-start = ((f32[32,1,128]{2,1,0:T(1,128)}), f32[32,1,128]{2,1,0:T(1,128)S(1)}, u32[]{:S(2)}, u32[]{:S(2)}) async-start(f32[32,1,128]{2,1,0:T(1,128)} %get-tuple-element.31), calls=%async_computation | async-start | bytes 32768 | tf_op jit(solution)/shard_map/all_to_all | solution.py:556
  14.6 11.7 %collective-permute-start = (bf16[8,256,128]{2,1,0:T(8,128)(2,1)}, bf16[8,256,128]{2,1,0:T(8,128)(2,1)}, u32[]{:S(2)}, u32[]{:S(2)}) collective-permute-start(bf16[8,256,128]{2,1,0:T(8,128)(2,1)} %get-tuple-element.29), channel_id=1, source_target_pairs={{0,1},{1,0},{2,3},{3,2},{4,5},{5,4},{6,7},{7,6},{8,9},{9,8},{10,11... | collective-permute-start | bytes 1572872 | tf_op jit(solution)/shard_map/ppermute | solution.py:569
  14.7 11.6 %collective-permute-start.1 = (bf16[8,256,128]{2,1,0:T(8,128)(2,1)}, bf16[8,256,128]{2,1,0:T(8,128)(2,1)}, u32[]{:S(2)}, u32[]{:S(2)}) collective-permute-start(bf16[8,256,128]{2,1,0:T(8,128)(2,1)} %get-tuple-element.30), channel_id=1, source_target_pairs={{1,2},{2,1},{3,4},{4,3},{5,6},{6,5},{9,10},{10,9},{11,12},{12,11},... | collective-permute-start | bytes 1572872 | tf_op jit(solution)/shard_map/ppermute | solution.py:569
  23.4 1.3 %collective-permute-start.2 = (f32[128,128]{1,0:T(8,128)S(1)}, f32[128,128]{1,0:T(8,128)S(1)}, u32[]{:S(2)}, u32[]{:S(2)}) collective-permute-start(f32[128,128]{1,0:T(8,128)S(1)} %arrive.1.a), channel_id=1, source_target_pairs={{0,1},{1,0},{2,3},{3,2},{4,5},{5,4},{6,7},{7,6},{8,9},{9,8},{10,11... | collective-permute-start | bytes 196616 | tf_op jit(solution)/shard_map/ppermute | solution.py:561
  24.7 8.4 %collective-permute-start.3 = (f32[128,128]{1,0:T(8,128)S(1)}, f32[128,128]{1,0:T(8,128)S(1)}, u32[]{:S(2)}, u32[]{:S(2)}) collective-permute-start(f32[128,128]{1,0:T(8,128)S(1)} %summed.2.a), channel_id=1, source_target_pairs={{0,2},{1,3},{2,0},{3,1},{4,6},{5,7},{6,4},{7,5},{8,10},{9,11},{10,... | collective-permute-start | bytes 196616 | tf_op jit(solution)/shard_map/ppermute | solution.py:561
  33.2 10.5 %collective-permute-start.5 = (f32[128,128]{1,0:T(8,128)S(1)}, f32[128,128]{1,0:T(8,128)S(1)}, u32[]{:S(2)}, u32[]{:S(2)}) collective-permute-start(f32[128,128]{1,0:T(8,128)S(1)} %summed.3.refs_0_), channel_id=1, source_target_pairs={{0,4},{1,5},{2,6},{3,7},{4,0},{5,1},{6,2},{7,3},{8,12},{9,13},{10,... | collective-permute-start | bytes 196616 | tf_op jit(solution)/shard_map/ppermute | solution.py:561
  36.0 7.7 %collective-permute-start.4 = (f32[32,1,128]{2,1,0:T(1,128)S(1)}, f32[32,1,128]{2,1,0:T(1,128)S(1)}, u32[]{:S(2)}, u32[]{:S(2)}) collective-permute-start(f32[32,1,128]{2,1,0:T(1,128)S(1)} %get-tuple-element.47), channel_id=1, source_target_pairs={{0,8},{8,16},{16,24},{24,32},{32,40},{40,48},{48,56},{56,64},{64,7... | collective-permute-start | bytes 49160 | tf_op jit(solution)/shard_map/ppermute | solution.py:574

commit v6 on v3

--- a/solution.py
+++ b/solution.py
@@ -252,96 +252,57 @@
     return now + shifted_down(later, 1, 0.0), later[steps - 1 :]
 
 
-def inner_kernel(
-    full,
-    ends_only,
-    table,
-    window,
-    blocks,
-    near,
-    carry,
-    neighbours,
-    held,
-    held_later,
-    found,
-    lines,
-    sems,
-    later_sems,
-    out_sems,
-):
-    count = len(full)
+def ends_kernel(starts, table, window, blocks, carry, neighbours, held, lines, sems):
     steps = window.shape[1]
     lags = blocks.shape[0]
+    count = held.shape[0] // len(starts)
+    listed = pltpu.make_async_copy(table, neighbours, sems.at[0])
+    listed.start()
     fetches = [
-        [
-            pltpu.make_async_copy(blocks.at[lag, c], held.at[lag, i], sems.at[lag, i])
-            for lag in range(lags)
-        ]
-        for i, c in enumerate(full)
+        pltpu.make_async_copy(
+            blocks.at[lags - 1, pl.ds(start, count)],
+            held.at[pl.ds(k * count, count)],
+            sems.at[1 + k],
+        )
+        for k, start in enumerate(starts)
     ]
-    later_fetches = [
-        pltpu.make_async_copy(blocks.at[lags - 1, c], held_later.at[i], later_sems.at[i])
-        for i, c in enumerate(ends_only)
-    ]
-    listed = pltpu.make_async_copy(table, neighbours, out_sems.at[count + 1])
-    listed.start()
-    for some in fetches:
-        for fetch in some:
-            fetch.start()
-    for fetch in later_fetches:
+    for fetch in fetches:
         fetch.start()
     listed.wait()
-    stores = []
-    for i, cluster in enumerate(full):
-        for fetch in fetches[i]:
-            fetch.wait()
-        blocks_here = [held.at[lag, i] for lag in range(lags)]
-        x, last = near_of(neighbours, window, blocks_here, cluster)
-        found[i] = x
-        lines[cluster - REACH] = last
-        stores.append(pltpu.make_async_copy(found.at[i], near.at[i], out_sems.at[i]))
-        stores[-1].start()
-    for i, cluster in enumerate(ends_only):
-        later_fetches[i].wait()
-        x = gathered(neighbours, window, cluster, pl.ds(steps - 16, 16))
-        y = jnp.dot(x, stacked(held_later.at[i]), preferred_element_type=F32)
-        lines[cluster - REACH] = y[15:]
-    stores.append(pltpu.make_async_copy(lines, carry, out_sems.at[count]))
-    stores[-1].start()
-    for store in stores:
-        store.wait()
-
-
-def inner_near(neighbours, window, blocks, full, ends_only):
-    steps, unknowns = window.shape[1:]
-    lags, clusters, nb = blocks.shape[:3]
-    count, more = len(full), len(ends_only)
-    block = (nb, unknowns, unknowns)
-    return pl.pallas_call(
-        functools.partial(inner_kernel, full, ends_only),
+    for k, start in enumerate(starts):
+        fetches[k].wait()
+        for i in range(count):
+            x = gathered(neighbours, window, start + i, pl.ds(steps - 16, 16))
+            w = stacked(held.at[k * count + i])
+            lines[k * count + i] = jnp.dot(x, w, preferred_element_type=F32)[15:]
+    store = pltpu.make_async_copy(lines, carry, sems.at[1 + len(starts)])
+    store.start()
+    store.wait()
+
+
+def ends_near(neighbours, window, blocks, starts, count):
+    unknowns = window.shape[2]
+    nb = blocks.shape[2]
+    more = len(starts) * count
+    return pl.pallas_call(
+        functools.partial(ends_kernel, starts),
         in_specs=[HBM, VMEM, HBM],
-        out_specs=[HBM] * 2,
-        out_shape=[
-            pltpu.HBM((count, steps, unknowns), F32),
-            pltpu.HBM((count + more, 1, unknowns), F32),
-        ],
+        out_specs=HBM,
+        out_shape=pltpu.HBM((more, 1, unknowns), F32),
         scratch_shapes=[
             pltpu.SMEM(neighbours.shape, jnp.int32),
-            pltpu.VMEM((lags, count, *block), BF16),
-            pltpu.VMEM((more, *block), BF16),
-            pltpu.VMEM((count, steps, unknowns), F32),
-            pltpu.VMEM((count + more, 1, unknowns), F32),
-            pltpu.SemaphoreType.DMA((lags, count)),
-            pltpu.SemaphoreType.DMA((more,)),
-            pltpu.SemaphoreType.DMA((count + 2,)),
-        ],
-        compiler_params=pltpu.CompilerParams(vmem_limit_bytes=16 << 20),
-        name="inner",
+            pltpu.VMEM((more, nb, unknowns, unknowns), BF16),
+            pltpu.VMEM((more, 1, unknowns), F32),
+            pltpu.SemaphoreType.DMA((2 + len(starts),)),
+        ],
+        compiler_params=pltpu.CompilerParams(vmem_limit_bytes=4 << 20),
+        name="ends",
     )(in_hbm(neighbours), window, in_hbm(blocks))
 
 
 def edge_kernel(
     order,
+    starts,
     table,
     window_in,
     from_pair,
@@ -361,26 +322,35 @@
     def copy(src, dst, k):
         return pltpu.make_async_copy(src, dst, sems.at[k])
 
+    count = inner_carry.shape[0] // len(starts)
+    listed = copy(table, neighbours, 0)
     sides = [
-        copy(from_pair, window.at[pl.ds(jnp.where(even, above, 0), REACH)], 0),
-        copy(from_other, window.at[pl.ds(jnp.where(even, 0, above), REACH)], 1),
-        copy(inner_carry, carry.at[pl.ds(REACH, inner_carry.shape[0])], 2),
-        copy(table, neighbours, 3),
+        copy(from_pair, window.at[pl.ds(jnp.where(even, above, 0), REACH)], 1),
+        copy(from_other, window.at[pl.ds(jnp.where(even, 0, above), REACH)], 2),
     ]
-    for c in sides:
+    rows = [
+        copy(inner_carry.at[pl.ds(k * count, count)], carry.at[pl.ds(start, count)], 3 + k)
+        for k, start in enumerate(starts)
+    ]
+    listed.start()
+    for c in sides + rows:
         c.start()
-    for c in sides:
-        c.wait()
+    listed.wait()
     for i, cluster in enumerate(order):
+        if i == REACH:
+            for c in sides:
+                c.wait()
         blocks_here = [blocks.at[lag, cluster] for lag in range(blocks.shape[0])]
         near[i], carry[cluster] = near_of(neighbours, window, blocks_here, cluster)
-
-
-def edge_near(neighbours, window, from_pair, from_other, blocks, inner_carry, order):
+    for c in rows:
+        c.wait()
+
+
+def edge_near(neighbours, window, from_pair, from_other, blocks, inner_carry, order, starts):
     steps, unknowns = window.shape[1:]
     clusters = blocks.shape[1]
     return pl.pallas_call(
-        functools.partial(edge_kernel, order),
+        functools.partial(edge_kernel, order, starts),
         in_specs=[HBM, VMEM, HBM, HBM, VMEM, HBM],
         out_specs=[VMEM] * 3,
         out_shape=[
@@ -390,7 +360,7 @@
         ],
         scratch_shapes=[
             pltpu.SMEM(neighbours.shape, jnp.int32),
-            pltpu.SemaphoreType.DMA((4,)),
+            pltpu.SemaphoreType.DMA((3 + len(starts),)),
         ],
         input_output_aliases={1: 2},
         compiler_params=pltpu.CompilerParams(vmem_limit_bytes=8 << 20),
@@ -405,49 +375,42 @@
     )
 
 
-def rest_kernel(
-    order, table, window, blocks, inner, from_moments, near, maps, neighbours, rows, sems
-):
-    listed = pltpu.make_async_copy(table, neighbours, sems.at[2])
+def rest_kernel(order, table, window, blocks, from_moments, near, maps, neighbours, rows, sems):
+    listed = pltpu.make_async_copy(table, neighbours, sems.at[0])
+    fetch = pltpu.make_async_copy(from_moments, rows, sems.at[1])
     listed.start()
-    fetches = [
-        pltpu.make_async_copy(from_moments, rows, sems.at[0]),
-        pltpu.make_async_copy(inner, near.at[pl.ds(len(order), inner.shape[0])], sems.at[1]),
-    ]
-    for fetch in fetches:
-        fetch.start()
+    fetch.start()
     listed.wait()
     for i, cluster in enumerate(order):
         blocks_here = [blocks.at[lag, cluster] for lag in range(blocks.shape[0])]
         near[i], _ = near_of(neighbours, window, blocks_here, cluster)
-    fetches[0].wait()
+    fetch.wait()
     w = jnp.transpose(rows[...], (1, 0, 2))
     for p in range(maps.shape[0]):
         x = jnp.concatenate([w[2 * p], w[2 * p + 1]], axis=1)
         maps[p] = jnp.concatenate([x, x], axis=0)
-    fetches[1].wait()
-
-
-def rest_near(neighbours, window, blocks, inner, from_moments, order):
+
+
+def rest_near(neighbours, window, blocks, from_moments, order):
     steps, unknowns = window.shape[1:]
     clusters = blocks.shape[1]
     terms = from_moments.shape[0]
     return pl.pallas_call(
         functools.partial(rest_kernel, order),
-        in_specs=[HBM, VMEM, VMEM, HBM, HBM],
+        in_specs=[HBM, VMEM, VMEM, HBM],
         out_specs=[VMEM] * 2,
         out_shape=[
-            jax.ShapeDtypeStruct((len(order) + inner.shape[0], steps, unknowns), F32),
+            jax.ShapeDtypeStruct((len(order), steps, unknowns), F32),
             jax.ShapeDtypeStruct((clusters // 2, 2 * terms, 2 * unknowns), BF16),
         ],
         scratch_shapes=[
             pltpu.SMEM(neighbours.shape, jnp.int32),
             pltpu.VMEM(from_moments.shape, BF16),
-            pltpu.SemaphoreType.DMA((3,)),
+            pltpu.SemaphoreType.DMA((2,)),
         ],
         compiler_params=pltpu.CompilerParams(vmem_limit_bytes=8 << 20),
         name="rest",
-    )(in_hbm(neighbours), window, in_vmem(blocks), in_hbm(inner), in_hbm(from_moments))
+    )(in_hbm(neighbours), window, in_vmem(blocks), in_hbm(from_moments))
 
 
 def final_kernel(places, edge, rest, carry, *refs):
@@ -548,22 +511,23 @@
     from_other = swapped_from(other, "space", 1)
     neighbours = neighbours.T
     clusters = density.shape[1]
-    middle = clusters // 2
-    full = tuple(range(middle - REACH // 2, middle + REACH // 2))
+    half = REACH // 2
+    starts = (REACH, clusters - REACH - half)
+    later = tuple(c for start in starts for c in range(start, start + half))
     sides = tuple(range(REACH)) + tuple(range(clusters - REACH, clusters))
-    others = tuple(c for c in range(clusters) if c not in full + sides)
-    inner, inner_carry = inner_near(neighbours, window, near_blocks, full, others)
-    ends, inner, inner_carry = lax.optimization_barrier((ends, inner, inner_carry))
+    early = tuple(c for c in range(clusters) if c not in later + sides) + sides
+    inner_carry = ends_near(neighbours, window, near_blocks, starts, half)
+    ends, inner_carry = lax.optimization_barrier((ends, inner_carry))
     mine = arrive(ends, far, decay)
     mine = pair_sum(mine, swapped_from(mine, "space", 0))
     parts = [mine] + [from_chip(mine, "space", d) for d in range(1, chips)]
     inner_carry, mine = lax.optimization_barrier((inner_carry, mine))
     edge, carry, window = edge_near(
-        neighbours, window, from_pair, from_other, near_blocks, inner_carry, sides
+        neighbours, window, from_pair, from_other, near_blocks, inner_carry, early, starts
     )
     carry = passed_on(carry, "tm")
-    rest, maps = rest_near(neighbours, window, near_blocks, inner, from_moments, others)
-    return final(edge, rest, carry, parts, maps, live, (sides, others + full))
+    rest, maps = rest_near(neighbours, window, near_blocks, from_moments, later)
+    return final(edge, rest, carry, parts, maps, live, (early, later))
 
 
 def solution(mesh):

time: 45.7 us -> 45.5 us (level)
  waiting for transfers between devices: 3.44 us -> 8.85 us
  Pallas kernels: 18.4 us -> 15 us
  starting transfers between devices: 23.5 us -> 21.2 us
    all_to_all x1, waiting for transfers between devices: 0.4 us -> 4.55 us  [exchanged(): return lax.all_to_all(x, axis, split_axis=0, concat_axis=0, tiled=True)]
    pallas_call x2, Pallas kernels: 10.2 us -> 6.79 us  [the longest x1 4.37 us: edge_near(): pl.pallas_call(functools.partial(edge_kernel, order, starts), in_specs=[H...]
    ppermute x3, starting transfers between devices: 3.36 us -> 1.67 us  [swapped_from(): return lax.ppermute(x, axis, route)]
    ppermute x1, waiting for transfers between devices: 2.13 us -> 3.05 us  [passed_on(): return lax.ppermute(x, axis, [(i, i + 1) for i in range(count - 1)])]
    ppermute x1, starting transfers between devices: 3.37 us -> 2.47 us  [passed_on(): return lax.ppermute(x, axis, [(i, i + 1) for i in range(count - 1)])]
  transfers between devices with their start and end apart: 8 -> 8, of which waited for: 3 -> 3; matrix products, arithmetic and copies ran while one was open for 0% -> 0% of each run, Pallas kernels for 28% -> 20%
where the time goes in v6:
time: 45.5 us; the launch traced here: 45.2 us
  starting transfers between devices  21.2 us (47%)
  Pallas kernels  15 us (33%)
  waiting for transfers between devices  8.85 us (19%)
    all_to_all x1, starting transfers between devices, exchanged(): return lax.all_to_all(x, axis, split_axis=0, concat_axis=0, tiled=True)  11.4 us
    ppermute x3, starting transfers between devices, from_chip(): lax.ppermute(x, axis, [(i, (i + 2 * distance) % count) for i in range(cou...  5.73 us
    all_to_all x1, waiting for transfers between devices, exchanged(): return lax.all_to_all(x, axis, split_axis=0, concat_axis=0, tiled=True)  4.55 us
    pallas_call x1, Pallas kernels, edge_near(): pl.pallas_call(functools.partial(edge_kernel, order, starts), in_specs=[H...  4.37 us
    pallas_call x1, Pallas kernels, prep(): pl.pallas_call(prep_kernel, in_specs=[HBM] * 5, out_specs=[VMEM, HBM, HBM...  3.23 us
    ppermute x1, waiting for transfers between devices, passed_on(): return lax.ppermute(x, axis, [(i, i + 1) for i in range(count - 1)])  3.05 us
    pallas_call x1, Pallas kernels, final(): pl.pallas_call(functools.partial(final_kernel, places), in_specs=[VMEM] *...  2.62 us
    ppermute x1, starting transfers between devices, passed_on(): return lax.ppermute(x, axis, [(i, i + 1) for i in range(count - 1)])  2.47 us
  transfers between devices with their start and end apart: 8, of which 3 were waited for; matrix products, arithmetic and copies ran while one was open for 0% of the time, Pallas kernels for 20%

profile of v6, /device:TPU:32, one launch (start us, length us, event | category | flops | bytes accessed | tf_op | source)
XLA Modules:
  0.0 45.2 jit_solution(11560683793346737639)
XLA Ops:
  0.0 3.2 %prep.1 = (bf16[48,256,128]{2,1,0:T(8,128)(2,1)S(1)}, bf16[8,256,128]{2,1,0:T(8,128)(2,1)}, bf16[8,256,128]{2,1,0:T(8,128)(2,1)}, f32[256,128]{1,0:T(8,128)S(1)}...) custom-call(bf16[256,32,128]{2,1,0:T(8,128)(2,1)} %density.1, s32[1,256]{1,0:T(1,128)} %bitcast.9, ...), custom_call_target="tpu_custom_call" | custom-call | tf_op jit(solution)/shard_map/prep/pallas_call | solution.py:158
  3.2 11.4 %all-to-all-start = ((f32[32,1,128]{2,1,0:T(1,128)}), f32[32,1,128]{2,1,0:T(1,128)S(1)}, u32[]{:S(2)}, u32[]{:S(2)}) async-start(f32[32,1,128]{2,1,0:T(1,128)} %get-tuple-element.23), calls=%async_computation | async-start | bytes 32768 | tf_op jit(solution)/shard_map/all_to_all | solution.py:477
  14.6 0.1 collective-permute-start
  14.7 1.5 %collective-permute-start.1 = (bf16[8,256,128]{2,1,0:T(8,128)(2,1)}, bf16[8,256,128]{2,1,0:T(8,128)(2,1)}, u32[]{:S(2)}, u32[]{:S(2)}) collective-permute-start(bf16[8,256,128]{2,1,0:T(8,128)(2,1)} %get-tuple-element.22), channel_id=1, source_target_pairs={{1,2},{2,1},{3,4},{4,3},{5,6},{6,5},{9,10},{10,9},{11,12},{12,11},... | collective-permute-start | bytes 1572872 | tf_op jit(solution)/shard_map/ppermute | solution.py:485
  16.2 2.4 %ends.1.inner_carry = f32[8,1,128]{2,1,0:T(1,128)} custom-call(s32[8,32]{1,0:T(8,128)} %bitcast.6, bf16[48,256,128]{2,1,0:T(8,128)(2,1)S(1)} %get-tuple-element.20.window.window_in, bf16[2,32,8,128,128]{4,3,2,1,0:T(8,128)(2,1)} %blocks.5), custom_call_target="tpu_custom_call" | custom-call | tf_op jit(solution)/shard_map/ends/pallas_call | solution.py:287
  18.6 4.5 %all-to-all-done.ends = f32[32,1,128]{2,1,0:T(1,128)S(1)} async-done(((f32[32,1,128]{2,1,0:T(1,128)}), f32[32,1,128]{2,1,0:T(1,128)S(1)}, u32[]{:S(2)}, u32[]{:S(2)}) %all-to-all-start) | async-done | bytes 16416 | tf_op jit(solution)/shard_map/all_to_all | solution.py:477
  23.2 0.0 slice-start
  23.2 0.0 slice-start.1
  23.2 0.0 slice-start.2
  23.2 0.0 slice-start.3
  23.2 0.2 arrive.1.a
  23.4 0.1 collective-permute-start.2
  23.5 1.2 %collective-permute-done.2.b = f32[128,128]{1,0:T(8,128)S(1)} collective-permute-done((f32[128,128]{1,0:T(8,128)S(1)}, f32[128,128]{1,0:T(8,128)S(1)}, u32[]{:S(2)}, u32[]{:S(2)}) %collective-permute-start.2) | collective-permute-done | bytes 65568 | tf_op jit(solution)/shard_map/ppermute | solution.py:485
  24.7 1.6 %collective-permute-start.4 = (bf16[128,128]{1,0:T(8,128)(2,1)S(1)}, bf16[128,128]{1,0:T(8,128)(2,1)S(1)}, u32[]{:S(2)}, u32[]{:S(2)}) collective-permute-start(bf16[128,128]{1,0:T(8,128)(2,1)S(1)} %pair_sum.1.refs_0_), channel_id=1, source_target_pairs={{0,2},{1,3},{2,4},{3,5},{4,6},{5,7},{6,0},{7,1},{8,10},{9,11},{10,... | collective-permute-start | bytes 98312 | tf_op jit(solution)/shard_map/ppermute | solution.py:490
  26.3 2.7 %collective-permute-start.5 = (bf16[128,128]{1,0:T(8,128)(2,1)S(1)}, bf16[128,128]{1,0:T(8,128)(2,1)S(1)}, u32[]{:S(2)}, u32[]{:S(2)}) collective-permute-start(bf16[128,128]{1,0:T(8,128)(2,1)S(1)} %pair_sum.1.refs_0_), channel_id=1, source_target_pairs={{0,4},{1,5},{2,6},{3,7},{4,0},{5,1},{6,2},{7,3},{8,12},{9,13},{10,... | collective-permute-start | bytes 98312 | tf_op jit(solution)/shard_map/ppermute | solution.py:490
  29.0 1.4 %collective-permute-start.6 = (bf16[128,128]{1,0:T(8,128)(2,1)S(1)}, bf16[128,128]{1,0:T(8,128)(2,1)S(1)}, u32[]{:S(2)}, u32[]{:S(2)}) collective-permute-start(bf16[128,128]{1,0:T(8,128)(2,1)S(1)} %pair_sum.1.refs_0_), channel_id=1, source_target_pairs={{0,6},{1,7},{2,0},{3,1},{4,2},{5,3},{6,4},{7,5},{8,14},{9,15},{10,... | collective-permute-start | bytes 98312 | tf_op jit(solution)/shard_map/ppermute | solution.py:490
  30.4 0.0 collective-permute-done.from_pair
  30.4 0.0 collective-permute-done.1.from_other
  30.5 0.0 slice-done
  30.5 0.0 slice-done.1
  30.5 0.0 slice-done.2
  30.5 0.0 slice-done.3
  30.5 4.4 %edge.1 = (f32[24,256,128]{2,1,0:T(8,128)S(1)}, f32[32,1,128]{2,1,0:T(1,128)S(1)}, bf16[48,256,128]{2,1,0:T(8,128)(2,1)S(1)}) custom-call(s32[8,32]{1,0:T(8,128)} %bitcast.7, bf16[48,256,128]{2,1,0:T(8,128)(2,1)S(1)} %get-tuple-element.20.window.window_in, bf16[8,256,128]{2,1,0:T(8,128)(2,1)} %collective-permute-done.from_pair, ...), custom_call_target="tpu_custom_call", output_to_operand_aliasing={{2}: (1, {})} | custom-call | tf_op jit(solution)/shard_map/edge/pallas_call | solution.py:352
  34.9 2.5 %collective-permute-start.3 = (f32[32,1,128]{2,1,0:T(1,128)S(1)}, f32[32,1,128]{2,1,0:T(1,128)S(1)}, u32[]{:S(2)}, u32[]{:S(2)}) collective-permute-start(f32[32,1,128]{2,1,0:T(1,128)S(1)} %get-tuple-element.32), channel_id=1, source_target_pairs={{0,8},{8,16},{16,24},{24,32},{32,40},{40,48},{48,56},{56,64},{64,7... | collective-permute-start | bytes 49160 | tf_op jit(solution)/shard_map/ppermute | solution.py:495
  37.3 2.2 %rest.1 = (f32[8,256,128]{2,1,0:T(8,128)S(1)}, bf16[16,128,256]{2,1,0:T(8,128)(2,1)S(1)}) custom-call(s32[8,32]{1,0:T(8,128)} %bitcast.8, bf16[48,256,128]{2,1,0:T(8,128)(2,1)S(1)} %get-tuple-element.30.window, bf16[2,32,8,128,128]{4,3,2,1,0:T(8,128)(2,1)S(1)} %bitcast.5, bf16[64,32,128]{2,1,0:T(8,128)(2,1)} %from_moments.1), custom_call_target="tpu_custom_call" | custom-call | tf_op jit(solution)/shard_map/rest/pallas_call | solution.py:398
  39.5 0.0 collective-permute-done.4.refs_1_
  39.5 0.0 collective-permute-done.5.refs_2_
  39.6 0.0 collective-permute-done.6.refs_3_
  39.6 3.0 %collective-permute-done.3.carry = f32[32,1,128]{2,1,0:T(1,128)S(1)} collective-permute-done((f32[32,1,128]{2,1,0:T(1,128)S(1)}, f32[32,1,128]{2,1,0:T(1,128)S(1)}, u32[]{:S(2)}, u32[]{:S(2)}) %collective-permute-start.3) | collective-permute-done | bytes 16416 | tf_op jit(solution)/shard_map/ppermute | solution.py:495
  42.6 2.6 %final.1 = bf16[256,32,128]{2,1,0:T(8,128)(2,1)} custom-call(f32[24,256,128]{2,1,0:T(8,128)S(1)} %get-tuple-element.29.edge, f32[8,256,128]{2,1,0:T(8,128)S(1)} %get-tuple-element.31.rest, f32[32,1,128]{2,1,0:T(1,128)S(1)} %collective-permute-done.3.carry, bf16[128,128]{1,0:T(8,128)(2,1)S(1)} %pair_sum.1.refs_0_, ...), custom_call_target="tpu_custom_call" | custom-call | tf_op jit(solution)/shard_map/final/pallas_call | solution.py:461
  (2 shorter events, 0.0 us)
Async XLA Ops:
  3.2 19.9 %all-to-all-start = ((f32[32,1,128]{2,1,0:T(1,128)}), f32[32,1,128]{2,1,0:T(1,128)S(1)}, u32[]{:S(2)}, u32[]{:S(2)}) async-start(f32[32,1,128]{2,1,0:T(1,128)} %get-tuple-element.23), calls=%async_computation | async-start | bytes 32768 | tf_op jit(solution)/shard_map/all_to_all | solution.py:477
  14.6 15.8 %collective-permute-start = (bf16[8,256,128]{2,1,0:T(8,128)(2,1)}, bf16[8,256,128]{2,1,0:T(8,128)(2,1)}, u32[]{:S(2)}, u32[]{:S(2)}) collective-permute-start(bf16[8,256,128]{2,1,0:T(8,128)(2,1)} %get-tuple-element.21), channel_id=1, source_target_pairs={{0,1},{1,0},{2,3},{3,2},{4,5},{5,4},{6,7},{7,6},{8,9},{9,8},{10,11... | collective-permute-start | bytes 1572872 | tf_op jit(solution)/shard_map/ppermute | solution.py:485
  14.7 15.7 %collective-permute-start.1 = (bf16[8,256,128]{2,1,0:T(8,128)(2,1)}, bf16[8,256,128]{2,1,0:T(8,128)(2,1)}, u32[]{:S(2)}, u32[]{:S(2)}) collective-permute-start(bf16[8,256,128]{2,1,0:T(8,128)(2,1)} %get-tuple-element.22), channel_id=1, source_target_pairs={{1,2},{2,1},{3,4},{4,3},{5,6},{6,5},{9,10},{10,9},{11,12},{12,11},... | collective-permute-start | bytes 1572872 | tf_op jit(solution)/shard_map/ppermute | solution.py:485
  23.2 7.3 %slice-start = ((s8[16777216]{0:T(1024)(128)(4,1)}), s8[4194304]{0:T(1024)(128)(4,1)S(1)}, s32[]{:S(2)}) async-start(s8[16777216]{0:T(1024)(128)(4,1)} %bitcast.4), calls=%async_computation.1 | async-start | bytes 8388608
  23.2 7.3 %slice-start.1 = ((s8[16777216]{0:T(1024)(128)(4,1)}), s8[4194304]{0:T(1024)(128)(4,1)S(1)}, s32[]{:S(2)}) async-start(s8[16777216]{0:T(1024)(128)(4,1)} %bitcast.4), calls=%async_computation.2 | async-start | bytes 8388608
  23.2 7.3 %slice-start.2 = ((s8[16777216]{0:T(1024)(128)(4,1)}), s8[4194304]{0:T(1024)(128)(4,1)S(1)}, s32[]{:S(2)}) async-start(s8[16777216]{0:T(1024)(128)(4,1)} %bitcast.4), calls=%async_computation.3 | async-start | bytes 8388608
  23.2 7.3 %slice-start.3 = ((s8[16777216]{0:T(1024)(128)(4,1)}), s8[4194304]{0:T(1024)(128)(4,1)S(1)}, s32[]{:S(2)}) async-start(s8[16777216]{0:T(1024)(128)(4,1)} %bitcast.4), calls=%async_computation.4 | async-start | bytes 8388608
  23.4 1.3 %collective-permute-start.2 = (f32[128,128]{1,0:T(8,128)S(1)}, f32[128,128]{1,0:T(8,128)S(1)}, u32[]{:S(2)}, u32[]{:S(2)}) collective-permute-start(f32[128,128]{1,0:T(8,128)S(1)} %arrive.1.a), channel_id=1, source_target_pairs={{0,1},{1,0},{2,3},{3,2},{4,5},{5,4},{6,7},{7,6},{8,9},{9,8},{10,11... | collective-permute-start | bytes 196616 | tf_op jit(solution)/shard_map/ppermute | solution.py:485
  24.7 14.8 %collective-permute-start.4 = (bf16[128,128]{1,0:T(8,128)(2,1)S(1)}, bf16[128,128]{1,0:T(8,128)(2,1)S(1)}, u32[]{:S(2)}, u32[]{:S(2)}) collective-permute-start(bf16[128,128]{1,0:T(8,128)(2,1)S(1)} %pair_sum.1.refs_0_), channel_id=1, source_target_pairs={{0,2},{1,3},{2,4},{3,5},{4,6},{5,7},{6,0},{7,1},{8,10},{9,11},{10,... | collective-permute-start | bytes 98312 | tf_op jit(solution)/shard_map/ppermute | solution.py:490
  26.3 13.3 %collective-permute-start.5 = (bf16[128,128]{1,0:T(8,128)(2,1)S(1)}, bf16[128,128]{1,0:T(8,128)(2,1)S(1)}, u32[]{:S(2)}, u32[]{:S(2)}) collective-permute-start(bf16[128,128]{1,0:T(8,128)(2,1)S(1)} %pair_sum.1.refs_0_), channel_id=1, source_target_pairs={{0,4},{1,5},{2,6},{3,7},{4,0},{5,1},{6,2},{7,3},{8,12},{9,13},{10,... | collective-permute-start | bytes 98312 | tf_op jit(solution)/shard_map/ppermute | solution.py:490
  29.0 10.5 %collective-permute-start.6 = (bf16[128,128]{1,0:T(8,128)(2,1)S(1)}, bf16[128,128]{1,0:T(8,128)(2,1)S(1)}, u32[]{:S(2)}, u32[]{:S(2)}) collective-permute-start(bf16[128,128]{1,0:T(8,128)(2,1)S(1)} %pair_sum.1.refs_0_), channel_id=1, source_target_pairs={{0,6},{1,7},{2,0},{3,1},{4,2},{5,3},{6,4},{7,5},{8,14},{9,15},{10,... | collective-permute-start | bytes 98312 | tf_op jit(solution)/shard_map/ppermute | solution.py:490
  34.9 7.7 %collective-permute-start.3 = (f32[32,1,128]{2,1,0:T(1,128)S(1)}, f32[32,1,128]{2,1,0:T(1,128)S(1)}, u32[]{:S(2)}, u32[]{:S(2)}) collective-permute-start(f32[32,1,128]{2,1,0:T(1,128)S(1)} %get-tuple-element.32), channel_id=1, source_target_pairs={{0,8},{8,16},{16,24},{24,32},{32,40},{40,48},{48,56},{56,64},{64,7... | collective-permute-start | bytes 49160 | tf_op jit(solution)/shard_map/ppermute | solution.py:495

commit v7 on v3

--- a/solution.py
+++ b/solution.py
@@ -252,9 +252,41 @@
     return now + shifted_down(later, 1, 0.0), later[steps - 1 :]
 
 
+def fetches_of(blocks, lags, groups, held, sems):
+    waits, at = [], 0
+    for k, (start, count) in enumerate(groups):
+        waits.append(
+            [
+                pltpu.make_async_copy(
+                    blocks.at[lag, pl.ds(start, count)],
+                    held.at[n, pl.ds(at, count)],
+                    sems.at[n, k],
+                )
+                for n, lag in enumerate(lags)
+            ]
+        )
+        at += count
+    return waits
+
+
+def clusters_of(groups):
+    return tuple(c for start, count in groups for c in range(start, start + count))
+
+
+def near_groups(neighbours, window, groups, fetches, held, put):
+    i = 0
+    for (start, count), some in zip(groups, fetches):
+        for fetch in some:
+            fetch.wait()
+        for cluster in range(start, start + count):
+            blocks_here = [held.at[n, i] for n in range(held.shape[0])]
+            put(i, cluster, *near_of(neighbours, window, blocks_here, cluster))
+            i += 1
+
+
 def inner_kernel(
-    full,
-    ends_only,
+    groups,
+    later_groups,
     table,
     window,
     blocks,
@@ -269,56 +301,43 @@
     later_sems,
     out_sems,
 ):
-    count = len(full)
-    steps = window.shape[1]
     lags = blocks.shape[0]
-    fetches = [
-        [
-            pltpu.make_async_copy(blocks.at[lag, c], held.at[lag, i], sems.at[lag, i])
-            for lag in range(lags)
-        ]
-        for i, c in enumerate(full)
-    ]
-    later_fetches = [
-        pltpu.make_async_copy(blocks.at[lags - 1, c], held_later.at[i], later_sems.at[i])
-        for i, c in enumerate(ends_only)
-    ]
-    listed = pltpu.make_async_copy(table, neighbours, out_sems.at[count + 1])
+    listed = pltpu.make_async_copy(table, neighbours, out_sems.at[0])
     listed.start()
-    for some in fetches:
+    fetches = fetches_of(blocks, range(lags), groups, held, sems)
+    later_fetches = fetches_of(blocks, (lags - 1,), later_groups, held_later, later_sems)
+    for some in fetches + later_fetches:
         for fetch in some:
             fetch.start()
-    for fetch in later_fetches:
-        fetch.start()
     listed.wait()
-    stores = []
-    for i, cluster in enumerate(full):
-        for fetch in fetches[i]:
-            fetch.wait()
-        blocks_here = [held.at[lag, i] for lag in range(lags)]
-        x, last = near_of(neighbours, window, blocks_here, cluster)
+
+    def put(i, cluster, x, last):
         found[i] = x
         lines[cluster - REACH] = last
-        stores.append(pltpu.make_async_copy(found.at[i], near.at[i], out_sems.at[i]))
-        stores[-1].start()
-    for i, cluster in enumerate(ends_only):
-        later_fetches[i].wait()
-        x = gathered(neighbours, window, cluster, pl.ds(steps - 16, 16))
-        y = jnp.dot(x, stacked(held_later.at[i]), preferred_element_type=F32)
-        lines[cluster - REACH] = y[15:]
-    stores.append(pltpu.make_async_copy(lines, carry, out_sems.at[count]))
-    stores[-1].start()
-    for store in stores:
-        store.wait()
-
-
-def inner_near(neighbours, window, blocks, full, ends_only):
+
+    near_groups(neighbours, window, groups, fetches, held, put)
+    store = pltpu.make_async_copy(found, near, out_sems.at[1])
+    store.start()
+    i = 0
+    for (start, count), some in zip(later_groups, later_fetches):
+        for fetch in some:
+            fetch.wait()
+        for cluster in range(start, start + count):
+            lines[cluster - REACH] = last_row(neighbours, window, held_later.at[0, i], cluster)
+            i += 1
+    lines_store = pltpu.make_async_copy(lines, carry, out_sems.at[2])
+    lines_store.start()
+    store.wait()
+    lines_store.wait()
+
+
+def inner_near(neighbours, window, blocks, groups, later_groups):
     steps, unknowns = window.shape[1:]
     lags, clusters, nb = blocks.shape[:3]
-    count, more = len(full), len(ends_only)
+    count, more = len(clusters_of(groups)), len(clusters_of(later_groups))
     block = (nb, unknowns, unknowns)
     return pl.pallas_call(
-        functools.partial(inner_kernel, full, ends_only),
+        functools.partial(inner_kernel, groups, later_groups),
         in_specs=[HBM, VMEM, HBM],
         out_specs=[HBM] * 2,
         out_shape=[
@@ -328,20 +347,27 @@
         scratch_shapes=[
             pltpu.SMEM(neighbours.shape, jnp.int32),
             pltpu.VMEM((lags, count, *block), BF16),
-            pltpu.VMEM((more, *block), BF16),
+            pltpu.VMEM((1, more, *block), BF16),
             pltpu.VMEM((count, steps, unknowns), F32),
             pltpu.VMEM((count + more, 1, unknowns), F32),
-            pltpu.SemaphoreType.DMA((lags, count)),
-            pltpu.SemaphoreType.DMA((more,)),
-            pltpu.SemaphoreType.DMA((count + 2,)),
+            pltpu.SemaphoreType.DMA((lags, len(groups))),
+            pltpu.SemaphoreType.DMA((1, len(later_groups))),
+            pltpu.SemaphoreType.DMA((3,)),
         ],
         compiler_params=pltpu.CompilerParams(vmem_limit_bytes=16 << 20),
         name="inner",
     )(in_hbm(neighbours), window, in_hbm(blocks))
 
 
+def last_row(neighbours, window, block, cluster):
+    steps = window.shape[1]
+    x = gathered(neighbours, window, cluster, pl.ds(steps - 16, 16))
+    return jnp.dot(x, stacked(block), preferred_element_type=F32)[15:]
+
+
 def edge_kernel(
     order,
+    ends_only,
     table,
     window_in,
     from_pair,
@@ -357,30 +383,35 @@
     del window_in
     even = is_even()
     above = window.shape[0] - REACH
+    lags = blocks.shape[0]
 
     def copy(src, dst, k):
         return pltpu.make_async_copy(src, dst, sems.at[k])
 
     sides = [
-        copy(from_pair, window.at[pl.ds(jnp.where(even, above, 0), REACH)], 0),
-        copy(from_other, window.at[pl.ds(jnp.where(even, 0, above), REACH)], 1),
-        copy(inner_carry, carry.at[pl.ds(REACH, inner_carry.shape[0])], 2),
-        copy(table, neighbours, 3),
+        copy(table, neighbours, 0),
+        copy(from_pair, window.at[pl.ds(jnp.where(even, above, 0), REACH)], 1),
+        copy(from_other, window.at[pl.ds(jnp.where(even, 0, above), REACH)], 2),
+        copy(inner_carry, carry.at[pl.ds(REACH, inner_carry.shape[0])], 3),
     ]
     for c in sides:
         c.start()
     for c in sides:
         c.wait()
     for i, cluster in enumerate(order):
-        blocks_here = [blocks.at[lag, cluster] for lag in range(blocks.shape[0])]
+        blocks_here = [blocks.at[lag, cluster] for lag in range(lags)]
         near[i], carry[cluster] = near_of(neighbours, window, blocks_here, cluster)
-
-
-def edge_near(neighbours, window, from_pair, from_other, blocks, inner_carry, order):
+    for cluster in ends_only:
+        carry[cluster] = last_row(neighbours, window, blocks.at[lags - 1, cluster], cluster)
+
+
+def edge_near(
+    neighbours, window, from_pair, from_other, blocks, inner_carry, order, ends_only
+):
     steps, unknowns = window.shape[1:]
     clusters = blocks.shape[1]
     return pl.pallas_call(
-        functools.partial(edge_kernel, order),
+        functools.partial(edge_kernel, order, ends_only),
         in_specs=[HBM, VMEM, HBM, HBM, VMEM, HBM],
         out_specs=[VMEM] * 3,
         out_shape=[
@@ -408,24 +439,21 @@
 def rest_kernel(
     order, table, window, blocks, inner, from_moments, near, maps, neighbours, rows, sems
 ):
-    listed = pltpu.make_async_copy(table, neighbours, sems.at[2])
-    listed.start()
-    fetches = [
-        pltpu.make_async_copy(from_moments, rows, sems.at[0]),
-        pltpu.make_async_copy(inner, near.at[pl.ds(len(order), inner.shape[0])], sems.at[1]),
-    ]
-    for fetch in fetches:
-        fetch.start()
+    listed = pltpu.make_async_copy(table, neighbours, sems.at[0])
+    fetch = pltpu.make_async_copy(from_moments, rows, sems.at[1])
+    found = pltpu.make_async_copy(inner, near.at[pl.ds(len(order), inner.shape[0])], sems.at[2])
+    for c in (listed, fetch, found):
+        c.start()
     listed.wait()
     for i, cluster in enumerate(order):
         blocks_here = [blocks.at[lag, cluster] for lag in range(blocks.shape[0])]
         near[i], _ = near_of(neighbours, window, blocks_here, cluster)
-    fetches[0].wait()
+    fetch.wait()
     w = jnp.transpose(rows[...], (1, 0, 2))
     for p in range(maps.shape[0]):
         x = jnp.concatenate([w[2 * p], w[2 * p + 1]], axis=1)
         maps[p] = jnp.concatenate([x, x], axis=0)
-    fetches[1].wait()
+    found.wait()
 
 
 def rest_near(neighbours, window, blocks, inner, from_moments, order):
@@ -548,22 +576,25 @@
     from_other = swapped_from(other, "space", 1)
     neighbours = neighbours.T
     clusters = density.shape[1]
+    quarter = REACH // 2
     middle = clusters // 2
-    full = tuple(range(middle - REACH // 2, middle + REACH // 2))
-    sides = tuple(range(REACH)) + tuple(range(clusters - REACH, clusters))
-    others = tuple(c for c in range(clusters) if c not in full + sides)
-    inner, inner_carry = inner_near(neighbours, window, near_blocks, full, others)
+    full = ((middle - 4, 2), (middle - 2, 2), (middle, 4))
+    later = ((REACH, quarter), (clusters - REACH - quarter, quarter))
+    low = tuple(range(REACH))
+    high = tuple(range(clusters - REACH, clusters))
+    inner, inner_carry = inner_near(neighbours, window, near_blocks, full, later)
     ends, inner, inner_carry = lax.optimization_barrier((ends, inner, inner_carry))
     mine = arrive(ends, far, decay)
     mine = pair_sum(mine, swapped_from(mine, "space", 0))
     parts = [mine] + [from_chip(mine, "space", d) for d in range(1, chips)]
     inner_carry, mine = lax.optimization_barrier((inner_carry, mine))
     edge, carry, window = edge_near(
-        neighbours, window, from_pair, from_other, near_blocks, inner_carry, sides
+        neighbours, window, from_pair, from_other, near_blocks, inner_carry, low, high
     )
     carry = passed_on(carry, "tm")
+    others = clusters_of(later) + high
     rest, maps = rest_near(neighbours, window, near_blocks, inner, from_moments, others)
-    return final(edge, rest, carry, parts, maps, live, (sides, others + full))
+    return final(edge, rest, carry, parts, maps, live, (low, others + clusters_of(full)))
 
 
 def solution(mesh):

time: 45.7 us -> 43.9 us (0.961)
  waiting for transfers between devices: 3.44 us -> 5.72 us
  starting transfers between devices: 23.5 us -> 21.3 us
  Pallas kernels: 18.4 us -> 16.5 us
    pallas_call x2, Pallas kernels: 10.2 us -> 7.19 us  [the longest x1 4.41 us: inner_near(): pl.pallas_call(functools.partial(inner_kernel, groups, later_groups), in_...]
    all_to_all x1, waiting for transfers between devices: 0.4 us -> 2.54 us  [exchanged(): return lax.all_to_all(x, axis, split_axis=0, concat_axis=0, tiled=True)]
    ppermute x3, starting transfers between devices: 3.36 us -> 1.68 us  [swapped_from(): return lax.ppermute(x, axis, route)]
    pallas_call x1, Pallas kernels: 2.19 us -> 3.28 us  [rest_near(): pl.pallas_call(functools.partial(rest_kernel, order), in_specs=[HBM, VMEM...]
    ppermute x1, starting transfers between devices: 3.37 us -> 2.49 us  [passed_on(): return lax.ppermute(x, axis, [(i, i + 1) for i in range(count - 1)])]
  transfers between devices with their start and end apart: 8 -> 8, of which waited for: 3 -> 3; matrix products, arithmetic and copies ran while one was open for 0% -> 0% of each run, Pallas kernels for 28% -> 24%
where the time goes in v7:
time: 43.9 us; the launch traced here: 43.6 us
  starting transfers between devices  21.3 us (49%)
  Pallas kernels  16.5 us (38%)
  waiting for transfers between devices  5.72 us (13%)
    all_to_all x1, starting transfers between devices, exchanged(): return lax.all_to_all(x, axis, split_axis=0, concat_axis=0, tiled=True)  11.4 us
    ppermute x3, starting transfers between devices, from_chip(): lax.ppermute(x, axis, [(i, (i + 2 * distance) % count) for i in range(cou...  5.73 us
    pallas_call x1, Pallas kernels, inner_near(): pl.pallas_call(functools.partial(inner_kernel, groups, later_groups), in_...  4.41 us
    pallas_call x1, Pallas kernels, rest_near(): pl.pallas_call(functools.partial(rest_kernel, order), in_specs=[HBM, VMEM...  3.28 us
    pallas_call x1, Pallas kernels, prep(): pl.pallas_call(prep_kernel, in_specs=[HBM] * 5, out_specs=[VMEM, HBM, HBM...  3.23 us
    pallas_call x1, Pallas kernels, edge_near(): pl.pallas_call(functools.partial(edge_kernel, order, ends_only), in_specs...  2.77 us
    pallas_call x1, Pallas kernels, final(): pl.pallas_call(functools.partial(final_kernel, places), in_specs=[VMEM] *...  2.62 us
    all_to_all x1, waiting for transfers between devices, exchanged(): return lax.all_to_all(x, axis, split_axis=0, concat_axis=0, tiled=True)  2.54 us
  transfers between devices with their start and end apart: 8, of which 3 were waited for; matrix products, arithmetic and copies ran while one was open for 0% of the time, Pallas kernels for 24%

profile of v7, /device:TPU:32, one launch (start us, length us, event | category | flops | bytes accessed | tf_op | source)
XLA Modules:
  0.0 43.6 jit_solution(10950795456393720976)
XLA Ops:
  0.0 3.2 %prep.1 = (bf16[48,256,128]{2,1,0:T(8,128)(2,1)S(1)}, bf16[8,256,128]{2,1,0:T(8,128)(2,1)}, bf16[8,256,128]{2,1,0:T(8,128)(2,1)}, f32[256,128]{1,0:T(8,128)S(1)}...) custom-call(bf16[256,32,128]{2,1,0:T(8,128)(2,1)} %density.1, s32[1,256]{1,0:T(1,128)} %bitcast.9, ...), custom_call_target="tpu_custom_call" | custom-call | tf_op jit(solution)/shard_map/prep/pallas_call | solution.py:158
  3.2 11.4 %all-to-all-start = ((f32[32,1,128]{2,1,0:T(1,128)}), f32[32,1,128]{2,1,0:T(1,128)S(1)}, u32[]{:S(2)}, u32[]{:S(2)}) async-start(f32[32,1,128]{2,1,0:T(1,128)} %get-tuple-element.26), calls=%async_computation | async-start | bytes 32768 | tf_op jit(solution)/shard_map/all_to_all | solution.py:542
  14.6 0.1 collective-permute-start
  14.7 1.5 %collective-permute-start.1 = (bf16[8,256,128]{2,1,0:T(8,128)(2,1)}, bf16[8,256,128]{2,1,0:T(8,128)(2,1)}, u32[]{:S(2)}, u32[]{:S(2)}) collective-permute-start(bf16[8,256,128]{2,1,0:T(8,128)(2,1)} %get-tuple-element.25), channel_id=1, source_target_pairs={{1,2},{2,1},{3,4},{4,3},{5,6},{6,5},{9,10},{10,9},{11,12},{12,11},... | collective-permute-start | bytes 1572872 | tf_op jit(solution)/shard_map/ppermute | solution.py:550
  16.2 4.4 %inner.1 = (f32[8,256,128]{2,1,0:T(8,128)}, f32[16,1,128]{2,1,0:T(1,128)}) custom-call(s32[8,32]{1,0:T(8,128)} %bitcast.6, bf16[48,256,128]{2,1,0:T(8,128)(2,1)S(1)} %get-tuple-element.23.window.window_in, bf16[2,32,8,128,128]{4,3,2,1,0:T(8,128)(2,1)} %blocks.5), custom_call_target="tpu_custom_call" | custom-call | tf_op jit(solution)/shard_map/inner/pallas_call | solution.py:339
  20.6 2.5 %all-to-all-done.ends = f32[32,1,128]{2,1,0:T(1,128)S(1)} async-done(((f32[32,1,128]{2,1,0:T(1,128)}), f32[32,1,128]{2,1,0:T(1,128)S(1)}, u32[]{:S(2)}, u32[]{:S(2)}) %all-to-all-start) | async-done | bytes 16416 | tf_op jit(solution)/shard_map/all_to_all | solution.py:542
  23.2 0.0 slice-start
  23.2 0.0 slice-start.1
  23.2 0.0 slice-start.2
  23.2 0.0 slice-start.3
  23.2 0.2 arrive.1.a
  23.3 0.1 collective-permute-start.2
  23.4 1.2 %collective-permute-done.2.b = f32[128,128]{1,0:T(8,128)S(1)} collective-permute-done((f32[128,128]{1,0:T(8,128)S(1)}, f32[128,128]{1,0:T(8,128)S(1)}, u32[]{:S(2)}, u32[]{:S(2)}) %collective-permute-start.2) | collective-permute-done | bytes 65568 | tf_op jit(solution)/shard_map/ppermute | solution.py:550
  24.7 1.6 %collective-permute-start.4 = (bf16[128,128]{1,0:T(8,128)(2,1)S(1)}, bf16[128,128]{1,0:T(8,128)(2,1)S(1)}, u32[]{:S(2)}, u32[]{:S(2)}) collective-permute-start(bf16[128,128]{1,0:T(8,128)(2,1)S(1)} %pair_sum.1.refs_0_), channel_id=1, source_target_pairs={{0,2},{1,3},{2,4},{3,5},{4,6},{5,7},{6,0},{7,1},{8,10},{9,11},{10,... | collective-permute-start | bytes 98312 | tf_op jit(solution)/shard_map/ppermute | solution.py:555
  26.3 2.7 %collective-permute-start.5 = (bf16[128,128]{1,0:T(8,128)(2,1)S(1)}, bf16[128,128]{1,0:T(8,128)(2,1)S(1)}, u32[]{:S(2)}, u32[]{:S(2)}) collective-permute-start(bf16[128,128]{1,0:T(8,128)(2,1)S(1)} %pair_sum.1.refs_0_), channel_id=1, source_target_pairs={{0,4},{1,5},{2,6},{3,7},{4,0},{5,1},{6,2},{7,3},{8,12},{9,13},{10,... | collective-permute-start | bytes 98312 | tf_op jit(solution)/shard_map/ppermute | solution.py:555
  29.0 1.4 %collective-permute-start.6 = (bf16[128,128]{1,0:T(8,128)(2,1)S(1)}, bf16[128,128]{1,0:T(8,128)(2,1)S(1)}, u32[]{:S(2)}, u32[]{:S(2)}) collective-permute-start(bf16[128,128]{1,0:T(8,128)(2,1)S(1)} %pair_sum.1.refs_0_), channel_id=1, source_target_pairs={{0,6},{1,7},{2,0},{3,1},{4,2},{5,3},{6,4},{7,5},{8,14},{9,15},{10,... | collective-permute-start | bytes 98312 | tf_op jit(solution)/shard_map/ppermute | solution.py:555
  30.4 0.0 collective-permute-done.from_pair
  30.4 0.0 collective-permute-done.1.from_other
  30.4 0.0 slice-done
  30.5 0.0 slice-done.1
  30.5 0.0 slice-done.2
  30.5 0.0 slice-done.3
  30.5 2.8 %edge.1 = (f32[8,256,128]{2,1,0:T(8,128)S(1)}, f32[32,1,128]{2,1,0:T(1,128)S(1)}, bf16[48,256,128]{2,1,0:T(8,128)(2,1)S(1)}) custom-call(s32[8,32]{1,0:T(8,128)} %bitcast.7, bf16[48,256,128]{2,1,0:T(8,128)(2,1)S(1)} %get-tuple-element.23.window.window_in, bf16[8,256,128]{2,1,0:T(8,128)(2,1)} %collective-permute-done.from_pair, ...), custom_call_target="tpu_custom_call", output_to_operand_aliasing={{2}: (1, {})} | custom-call | tf_op jit(solution)/shard_map/edge/pallas_call | solution.py:413
  33.3 2.5 %collective-permute-start.3 = (f32[32,1,128]{2,1,0:T(1,128)S(1)}, f32[32,1,128]{2,1,0:T(1,128)S(1)}, u32[]{:S(2)}, u32[]{:S(2)}) collective-permute-start(f32[32,1,128]{2,1,0:T(1,128)S(1)} %get-tuple-element.38), channel_id=1, source_target_pairs={{0,8},{8,16},{16,24},{24,32},{32,40},{40,48},{48,56},{56,64},{64,7... | collective-permute-start | bytes 49160 | tf_op jit(solution)/shard_map/ppermute | solution.py:560
  35.8 3.3 %rest.1 = (f32[24,256,128]{2,1,0:T(8,128)S(1)}, bf16[16,128,256]{2,1,0:T(8,128)(2,1)S(1)}) custom-call(s32[8,32]{1,0:T(8,128)} %bitcast.8, bf16[48,256,128]{2,1,0:T(8,128)(2,1)S(1)} %get-tuple-element.35.window, bf16[2,32,8,128,128]{4,3,2,1,0:T(8,128)(2,1)S(1)} %bitcast.5, f32[8,256,128]{2,1,0:T(8,128)} %get-tuple-element.36.inner, ...), custom_call_target="tpu_custom_call" | custom-call | tf_op jit(solution)/shard_map/rest/pallas_call | solution.py:463
  39.0 0.0 collective-permute-done.4.refs_1_
  39.1 0.0 collective-permute-done.5.refs_2_
  39.1 0.0 collective-permute-done.6.refs_3_
  39.1 1.9 %collective-permute-done.3.carry = f32[32,1,128]{2,1,0:T(1,128)S(1)} collective-permute-done((f32[32,1,128]{2,1,0:T(1,128)S(1)}, f32[32,1,128]{2,1,0:T(1,128)S(1)}, u32[]{:S(2)}, u32[]{:S(2)}) %collective-permute-start.3) | collective-permute-done | bytes 16416 | tf_op jit(solution)/shard_map/ppermute | solution.py:560
  41.0 2.6 %final.1 = bf16[256,32,128]{2,1,0:T(8,128)(2,1)} custom-call(f32[8,256,128]{2,1,0:T(8,128)S(1)} %get-tuple-element.34.edge, f32[24,256,128]{2,1,0:T(8,128)S(1)} %get-tuple-element.37.rest, f32[32,1,128]{2,1,0:T(1,128)S(1)} %collective-permute-done.3.carry, bf16[128,128]{1,0:T(8,128)(2,1)S(1)} %pair_sum.1.refs_0_, ...), custom_call_target="tpu_custom_call" | custom-call | tf_op jit(solution)/shard_map/final/pallas_call | solution.py:526
  (2 shorter events, 0.0 us)
Async XLA Ops:
  3.2 19.9 %all-to-all-start = ((f32[32,1,128]{2,1,0:T(1,128)}), f32[32,1,128]{2,1,0:T(1,128)S(1)}, u32[]{:S(2)}, u32[]{:S(2)}) async-start(f32[32,1,128]{2,1,0:T(1,128)} %get-tuple-element.26), calls=%async_computation | async-start | bytes 32768 | tf_op jit(solution)/shard_map/all_to_all | solution.py:542
  14.6 15.8 %collective-permute-start = (bf16[8,256,128]{2,1,0:T(8,128)(2,1)}, bf16[8,256,128]{2,1,0:T(8,128)(2,1)}, u32[]{:S(2)}, u32[]{:S(2)}) collective-permute-start(bf16[8,256,128]{2,1,0:T(8,128)(2,1)} %get-tuple-element.24), channel_id=1, source_target_pairs={{0,1},{1,0},{2,3},{3,2},{4,5},{5,4},{6,7},{7,6},{8,9},{9,8},{10,11... | collective-permute-start | bytes 1572872 | tf_op jit(solution)/shard_map/ppermute | solution.py:550
  14.7 15.7 %collective-permute-start.1 = (bf16[8,256,128]{2,1,0:T(8,128)(2,1)}, bf16[8,256,128]{2,1,0:T(8,128)(2,1)}, u32[]{:S(2)}, u32[]{:S(2)}) collective-permute-start(bf16[8,256,128]{2,1,0:T(8,128)(2,1)} %get-tuple-element.25), channel_id=1, source_target_pairs={{1,2},{2,1},{3,4},{4,3},{5,6},{6,5},{9,10},{10,9},{11,12},{12,11},... | collective-permute-start | bytes 1572872 | tf_op jit(solution)/shard_map/ppermute | solution.py:550
  23.2 7.3 %slice-start = ((s8[16777216]{0:T(1024)(128)(4,1)}), s8[4194304]{0:T(1024)(128)(4,1)S(1)}, s32[]{:S(2)}) async-start(s8[16777216]{0:T(1024)(128)(4,1)} %bitcast.4), calls=%async_computation.1 | async-start | bytes 8388608
  23.2 7.3 %slice-start.1 = ((s8[16777216]{0:T(1024)(128)(4,1)}), s8[4194304]{0:T(1024)(128)(4,1)S(1)}, s32[]{:S(2)}) async-start(s8[16777216]{0:T(1024)(128)(4,1)} %bitcast.4), calls=%async_computation.2 | async-start | bytes 8388608
  23.2 7.3 %slice-start.2 = ((s8[16777216]{0:T(1024)(128)(4,1)}), s8[4194304]{0:T(1024)(128)(4,1)S(1)}, s32[]{:S(2)}) async-start(s8[16777216]{0:T(1024)(128)(4,1)} %bitcast.4), calls=%async_computation.3 | async-start | bytes 8388608
  23.2 7.3 %slice-start.3 = ((s8[16777216]{0:T(1024)(128)(4,1)}), s8[4194304]{0:T(1024)(128)(4,1)S(1)}, s32[]{:S(2)}) async-start(s8[16777216]{0:T(1024)(128)(4,1)} %bitcast.4), calls=%async_computation.4 | async-start | bytes 8388608
  23.3 1.3 %collective-permute-start.2 = (f32[128,128]{1,0:T(8,128)S(1)}, f32[128,128]{1,0:T(8,128)S(1)}, u32[]{:S(2)}, u32[]{:S(2)}) collective-permute-start(f32[128,128]{1,0:T(8,128)S(1)} %arrive.1.a), channel_id=1, source_target_pairs={{0,1},{1,0},{2,3},{3,2},{4,5},{5,4},{6,7},{7,6},{8,9},{9,8},{10,11... | collective-permute-start | bytes 196616 | tf_op jit(solution)/shard_map/ppermute | solution.py:550
  24.7 14.3 %collective-permute-start.4 = (bf16[128,128]{1,0:T(8,128)(2,1)S(1)}, bf16[128,128]{1,0:T(8,128)(2,1)S(1)}, u32[]{:S(2)}, u32[]{:S(2)}) collective-permute-start(bf16[128,128]{1,0:T(8,128)(2,1)S(1)} %pair_sum.1.refs_0_), channel_id=1, source_target_pairs={{0,2},{1,3},{2,4},{3,5},{4,6},{5,7},{6,0},{7,1},{8,10},{9,11},{10,... | collective-permute-start | bytes 98312 | tf_op jit(solution)/shard_map/ppermute | solution.py:555
  26.3 12.8 %collective-permute-start.5 = (bf16[128,128]{1,0:T(8,128)(2,1)S(1)}, bf16[128,128]{1,0:T(8,128)(2,1)S(1)}, u32[]{:S(2)}, u32[]{:S(2)}) collective-permute-start(bf16[128,128]{1,0:T(8,128)(2,1)S(1)} %pair_sum.1.refs_0_), channel_id=1, source_target_pairs={{0,4},{1,5},{2,6},{3,7},{4,0},{5,1},{6,2},{7,3},{8,12},{9,13},{10,... | collective-permute-start | bytes 98312 | tf_op jit(solution)/shard_map/ppermute | solution.py:555
  29.0 10.1 %collective-permute-start.6 = (bf16[128,128]{1,0:T(8,128)(2,1)S(1)}, bf16[128,128]{1,0:T(8,128)(2,1)S(1)}, u32[]{:S(2)}, u32[]{:S(2)}) collective-permute-start(bf16[128,128]{1,0:T(8,128)(2,1)S(1)} %pair_sum.1.refs_0_), channel_id=1, source_target_pairs={{0,6},{1,7},{2,0},{3,1},{4,2},{5,3},{6,4},{7,5},{8,14},{9,15},{10,... | collective-permute-start | bytes 98312 | tf_op jit(solution)/shard_map/ppermute | solution.py:555
  33.3 7.7 %collective-permute-start.3 = (f32[32,1,128]{2,1,0:T(1,128)S(1)}, f32[32,1,128]{2,1,0:T(1,128)S(1)}, u32[]{:S(2)}, u32[]{:S(2)}) collective-permute-start(f32[32,1,128]{2,1,0:T(1,128)S(1)} %get-tuple-element.38), channel_id=1, source_target_pairs={{0,8},{8,16},{16,24},{24,32},{32,40},{40,48},{48,56},{56,64},{64,7... | collective-permute-start | bytes 49160 | tf_op jit(solution)/shard_map/ppermute | solution.py:560

commit v8 on v7

--- a/solution.py
+++ b/solution.py
@@ -290,13 +290,17 @@
     table,
     window,
     blocks,
+    from_moments,
     near,
     carry,
+    maps,
     neighbours,
     held,
     held_later,
     found,
     lines,
+    rows,
+    built,
     sems,
     later_sems,
     out_sems,
@@ -309,6 +313,8 @@
     for some in fetches + later_fetches:
         for fetch in some:
             fetch.start()
+    rows_fetch = pltpu.make_async_copy(from_moments, rows, out_sems.at[3])
+    rows_fetch.start()
     listed.wait()
 
     def put(i, cluster, x, last):
@@ -327,22 +333,32 @@
             i += 1
     lines_store = pltpu.make_async_copy(lines, carry, out_sems.at[2])
     lines_store.start()
+    rows_fetch.wait()
+    w = jnp.transpose(rows[...], (1, 0, 2))
+    for p in range(maps.shape[0]):
+        x = jnp.concatenate([w[2 * p], w[2 * p + 1]], axis=1)
+        built[p] = jnp.concatenate([x, x], axis=0)
+    maps_store = pltpu.make_async_copy(built, maps, out_sems.at[4])
+    maps_store.start()
     store.wait()
     lines_store.wait()
-
-
-def inner_near(neighbours, window, blocks, groups, later_groups):
+    maps_store.wait()
+
+
+def inner_near(neighbours, window, blocks, from_moments, groups, later_groups):
     steps, unknowns = window.shape[1:]
     lags, clusters, nb = blocks.shape[:3]
     count, more = len(clusters_of(groups)), len(clusters_of(later_groups))
+    maps = (clusters // 2, 2 * from_moments.shape[0], 2 * unknowns)
     block = (nb, unknowns, unknowns)
     return pl.pallas_call(
         functools.partial(inner_kernel, groups, later_groups),
-        in_specs=[HBM, VMEM, HBM],
-        out_specs=[HBM] * 2,
+        in_specs=[HBM, VMEM, HBM, HBM],
+        out_specs=[HBM] * 3,
         out_shape=[
             pltpu.HBM((count, steps, unknowns), F32),
             pltpu.HBM((count + more, 1, unknowns), F32),
+            pltpu.HBM(maps, BF16),
         ],
         scratch_shapes=[
             pltpu.SMEM(neighbours.shape, jnp.int32),
@@ -350,13 +366,15 @@
             pltpu.VMEM((1, more, *block), BF16),
             pltpu.VMEM((count, steps, unknowns), F32),
             pltpu.VMEM((count + more, 1, unknowns), F32),
+            pltpu.VMEM(from_moments.shape, BF16),
+            pltpu.VMEM(maps, BF16),
             pltpu.SemaphoreType.DMA((lags, len(groups))),
             pltpu.SemaphoreType.DMA((1, len(later_groups))),
-            pltpu.SemaphoreType.DMA((3,)),
-        ],
-        compiler_params=pltpu.CompilerParams(vmem_limit_bytes=16 << 20),
+            pltpu.SemaphoreType.DMA((5,)),
+        ],
+        compiler_params=pltpu.CompilerParams(vmem_limit_bytes=18 << 20),
         name="inner",
-    )(in_hbm(neighbours), window, in_hbm(blocks))
+    )(in_hbm(neighbours), window, in_hbm(blocks), in_hbm(from_moments))
 
 
 def last_row(neighbours, window, block, cluster):
@@ -366,6 +384,7 @@
 
 
 def edge_kernel(
+    early,
     order,
     ends_only,
     table,
@@ -396,9 +415,13 @@
     ]
     for c in sides:
         c.start()
-    for c in sides:
+    sides[0].wait()
+    for i, cluster in enumerate(early):
+        blocks_here = [blocks.at[lag, cluster] for lag in range(lags)]
+        near[i], _ = near_of(neighbours, window, blocks_here, cluster)
+    for c in sides[1:]:
         c.wait()
-    for i, cluster in enumerate(order):
+    for i, cluster in enumerate(order, len(early)):
         blocks_here = [blocks.at[lag, cluster] for lag in range(lags)]
         near[i], carry[cluster] = near_of(neighbours, window, blocks_here, cluster)
     for cluster in ends_only:
@@ -406,16 +429,16 @@
 
 
 def edge_near(
-    neighbours, window, from_pair, from_other, blocks, inner_carry, order, ends_only
+    neighbours, window, from_pair, from_other, blocks, inner_carry, early, order, ends_only
 ):
     steps, unknowns = window.shape[1:]
     clusters = blocks.shape[1]
     return pl.pallas_call(
-        functools.partial(edge_kernel, order, ends_only),
+        functools.partial(edge_kernel, early, order, ends_only),
         in_specs=[HBM, VMEM, HBM, HBM, VMEM, HBM],
         out_specs=[VMEM] * 3,
         out_shape=[
-            jax.ShapeDtypeStruct((len(order), steps, unknowns), F32),
+            jax.ShapeDtypeStruct((len(early) + len(order), steps, unknowns), F32),
             jax.ShapeDtypeStruct((clusters, 1, unknowns), F32),
             jax.ShapeDtypeStruct(window.shape, BF16),
         ],
@@ -436,46 +459,40 @@
     )
 
 
-def rest_kernel(
-    order, table, window, blocks, inner, from_moments, near, maps, neighbours, rows, sems
-):
+def rest_kernel(order, table, window, blocks, inner, found_maps, near, maps, neighbours, sems):
     listed = pltpu.make_async_copy(table, neighbours, sems.at[0])
-    fetch = pltpu.make_async_copy(from_moments, rows, sems.at[1])
-    found = pltpu.make_async_copy(inner, near.at[pl.ds(len(order), inner.shape[0])], sems.at[2])
-    for c in (listed, fetch, found):
-        c.start()
+    fetches = [
+        pltpu.make_async_copy(found_maps, maps, sems.at[1]),
+        pltpu.make_async_copy(inner, near.at[pl.ds(len(order), inner.shape[0])], sems.at[2]),
+    ]
+    listed.start()
+    for fetch in fetches:
+        fetch.start()
     listed.wait()
     for i, cluster in enumerate(order):
         blocks_here = [blocks.at[lag, cluster] for lag in range(blocks.shape[0])]
         near[i], _ = near_of(neighbours, window, blocks_here, cluster)
-    fetch.wait()
-    w = jnp.transpose(rows[...], (1, 0, 2))
-    for p in range(maps.shape[0]):
-        x = jnp.concatenate([w[2 * p], w[2 * p + 1]], axis=1)
-        maps[p] = jnp.concatenate([x, x], axis=0)
-    found.wait()
-
-
-def rest_near(neighbours, window, blocks, inner, from_moments, order):
+    for fetch in fetches:
+        fetch.wait()
+
+
+def rest_near(neighbours, window, blocks, inner, maps, order):
     steps, unknowns = window.shape[1:]
-    clusters = blocks.shape[1]
-    terms = from_moments.shape[0]
     return pl.pallas_call(
         functools.partial(rest_kernel, order),
         in_specs=[HBM, VMEM, VMEM, HBM, HBM],
         out_specs=[VMEM] * 2,
         out_shape=[
             jax.ShapeDtypeStruct((len(order) + inner.shape[0], steps, unknowns), F32),
-            jax.ShapeDtypeStruct((clusters // 2, 2 * terms, 2 * unknowns), BF16),
+            jax.ShapeDtypeStruct(maps.shape, BF16),
         ],
         scratch_shapes=[
             pltpu.SMEM(neighbours.shape, jnp.int32),
-            pltpu.VMEM(from_moments.shape, BF16),
             pltpu.SemaphoreType.DMA((3,)),
         ],
         compiler_params=pltpu.CompilerParams(vmem_limit_bytes=8 << 20),
         name="rest",
-    )(in_hbm(neighbours), window, in_vmem(blocks), in_hbm(inner), in_hbm(from_moments))
+    )(in_hbm(neighbours), window, in_vmem(blocks), in_hbm(inner), in_hbm(maps))
 
 
 def final_kernel(places, edge, rest, carry, *refs):
@@ -582,19 +599,22 @@
     later = ((REACH, quarter), (clusters - REACH - quarter, quarter))
     low = tuple(range(REACH))
     high = tuple(range(clusters - REACH, clusters))
-    inner, inner_carry = inner_near(neighbours, window, near_blocks, full, later)
+    inner, inner_carry, maps = inner_near(
+        neighbours, window, near_blocks, from_moments, full, later
+    )
     ends, inner, inner_carry = lax.optimization_barrier((ends, inner, inner_carry))
     mine = arrive(ends, far, decay)
     mine = pair_sum(mine, swapped_from(mine, "space", 0))
     parts = [mine] + [from_chip(mine, "space", d) for d in range(1, chips)]
     inner_carry, mine = lax.optimization_barrier((inner_carry, mine))
+    later = clusters_of(later)
+    early, others = later[:3], later[3:] + high
     edge, carry, window = edge_near(
-        neighbours, window, from_pair, from_other, near_blocks, inner_carry, low, high
+        neighbours, window, from_pair, from_other, near_blocks, inner_carry, early, low, high
     )
     carry = passed_on(carry, "tm")
-    others = clusters_of(later) + high
-    rest, maps = rest_near(neighbours, window, near_blocks, inner, from_moments, others)
-    return final(edge, rest, carry, parts, maps, live, (low, others + clusters_of(full)))
+    rest, maps = rest_near(neighbours, window, near_blocks, inner, maps, others)
+    return final(edge, rest, carry, parts, maps, live, (early + low, others + clusters_of(full)))
 
 
 def solution(mesh):

time: 43.9 us -> 44.3 us (level)
  waiting for transfers between devices: 5.72 us -> 5.26 us
    pallas_call x1, Pallas kernels: 4.41 us -> 5.01 us  [inner_near(): pl.pallas_call(functools.partial(inner_kernel, groups, later_groups), in_...]
    pallas_call x1, Pallas kernels: 3.28 us -> 2.69 us  [rest_near(): pl.pallas_call(functools.partial(rest_kernel, order), in_specs=[HBM, VMEM...]
    all_to_all x1, waiting for transfers between devices: 2.54 us -> 1.98 us  [exchanged(): return lax.all_to_all(x, axis, split_axis=0, concat_axis=0, tiled=True)]
  transfers between devices with their start and end apart: 8 -> 8, of which waited for: 3 -> 3; matrix products, arithmetic and copies ran while one was open for 0% -> 0% of each run, Pallas kernels for 24% -> 25%
where the time goes in v8:
time: 44.3 us; the launch traced here: 44 us
  starting transfers between devices  21.7 us (49%)
  Pallas kernels  16.8 us (38%)
  waiting for transfers between devices  5.26 us (12%)
    all_to_all x1, starting transfers between devices, exchanged(): return lax.all_to_all(x, axis, split_axis=0, concat_axis=0, tiled=True)  11.4 us
    ppermute x3, starting transfers between devices, from_chip(): lax.ppermute(x, axis, [(i, (i + 2 * distance) % count) for i in range(cou...  5.73 us
    pallas_call x1, Pallas kernels, inner_near(): pl.pallas_call(functools.partial(inner_kernel, groups, later_groups), in_...  5.01 us
    pallas_call x1, Pallas kernels, prep(): pl.pallas_call(prep_kernel, in_specs=[HBM] * 5, out_specs=[VMEM, HBM, HBM...  3.23 us
    pallas_call x1, Pallas kernels, edge_near(): pl.pallas_call(functools.partial(edge_kernel, early, order, ends_only), i...  3.13 us
    ppermute x1, starting transfers between devices, passed_on(): return lax.ppermute(x, axis, [(i, i + 1) for i in range(count - 1)])  2.86 us
    pallas_call x1, Pallas kernels, rest_near(): pl.pallas_call(functools.partial(rest_kernel, order), in_specs=[HBM, VMEM...  2.69 us
    pallas_call x1, Pallas kernels, final(): pl.pallas_call(functools.partial(final_kernel, places), in_specs=[VMEM] *...  2.62 us
  transfers between devices with their start and end apart: 8, of which 3 were waited for; matrix products, arithmetic and copies ran while one was open for 0% of the time, Pallas kernels for 25%

profile of v8, /device:TPU:32, one launch (start us, length us, event | category | flops | bytes accessed | tf_op | source)
XLA Modules:
  0.0 44.0 jit_solution(17832041318892508440)
XLA Ops:
  0.0 3.2 %prep.1 = (bf16[48,256,128]{2,1,0:T(8,128)(2,1)S(1)}, bf16[8,256,128]{2,1,0:T(8,128)(2,1)}, bf16[8,256,128]{2,1,0:T(8,128)(2,1)}, f32[256,128]{1,0:T(8,128)S(1)}...) custom-call(bf16[256,32,128]{2,1,0:T(8,128)(2,1)} %density.1, s32[1,256]{1,0:T(1,128)} %bitcast.9, ...), custom_call_target="tpu_custom_call" | custom-call | tf_op jit(solution)/shard_map/prep/pallas_call | solution.py:158
  3.2 11.4 %all-to-all-start = ((f32[32,1,128]{2,1,0:T(1,128)}), f32[32,1,128]{2,1,0:T(1,128)S(1)}, u32[]{:S(2)}, u32[]{:S(2)}) async-start(f32[32,1,128]{2,1,0:T(1,128)} %get-tuple-element.27), calls=%async_computation | async-start | bytes 32768 | tf_op jit(solution)/shard_map/all_to_all | solution.py:559
  14.6 0.1 collective-permute-start
  14.7 1.5 %collective-permute-start.1 = (bf16[8,256,128]{2,1,0:T(8,128)(2,1)}, bf16[8,256,128]{2,1,0:T(8,128)(2,1)}, u32[]{:S(2)}, u32[]{:S(2)}) collective-permute-start(bf16[8,256,128]{2,1,0:T(8,128)(2,1)} %get-tuple-element.26), channel_id=1, source_target_pairs={{1,2},{2,1},{3,4},{4,3},{5,6},{6,5},{9,10},{10,9},{11,12},{12,11},... | collective-permute-start | bytes 1572872 | tf_op jit(solution)/shard_map/ppermute | solution.py:567
  16.2 5.0 %inner.1 = (f32[8,256,128]{2,1,0:T(8,128)}, f32[16,1,128]{2,1,0:T(1,128)}, bf16[16,128,256]{2,1,0:T(8,128)(2,1)}) custom-call(s32[8,32]{1,0:T(8,128)} %bitcast.6, bf16[48,256,128]{2,1,0:T(8,128)(2,1)S(1)} %get-tuple-element.24.window.window_in, bf16[2,32,8,128,128]{4,3,2,1,0:T(8,128)(2,1)} %blocks.5, bf16[64,32,128]{2,1,0:T(8,128)(2,1)} %from_moments.1), custom_call_target="tpu_custom_call" | custom-call | tf_op jit(solution)/shard_map/inner/pallas_call | solution.py:354
  21.2 2.0 %all-to-all-done.ends = f32[32,1,128]{2,1,0:T(1,128)S(1)} async-done(((f32[32,1,128]{2,1,0:T(1,128)}), f32[32,1,128]{2,1,0:T(1,128)S(1)}, u32[]{:S(2)}, u32[]{:S(2)}) %all-to-all-start) | async-done | bytes 16416 | tf_op jit(solution)/shard_map/all_to_all | solution.py:559
  23.2 0.0 slice-start
  23.2 0.0 slice-start.1
  23.2 0.0 slice-start.2
  23.2 0.0 slice-start.3
  23.2 0.2 arrive.1.a
  23.4 0.2 collective-permute-start.2
  23.6 1.1 %collective-permute-done.2.b = f32[128,128]{1,0:T(8,128)S(1)} collective-permute-done((f32[128,128]{1,0:T(8,128)S(1)}, f32[128,128]{1,0:T(8,128)S(1)}, u32[]{:S(2)}, u32[]{:S(2)}) %collective-permute-start.2) | collective-permute-done | bytes 65568 | tf_op jit(solution)/shard_map/ppermute | solution.py:567
  24.7 1.6 %collective-permute-start.4 = (bf16[128,128]{1,0:T(8,128)(2,1)S(1)}, bf16[128,128]{1,0:T(8,128)(2,1)S(1)}, u32[]{:S(2)}, u32[]{:S(2)}) collective-permute-start(bf16[128,128]{1,0:T(8,128)(2,1)S(1)} %pair_sum.1.refs_0_), channel_id=1, source_target_pairs={{0,2},{1,3},{2,4},{3,5},{4,6},{5,7},{6,0},{7,1},{8,10},{9,11},{10,... | collective-permute-start | bytes 98312 | tf_op jit(solution)/shard_map/ppermute | solution.py:572
  26.3 2.7 %collective-permute-start.5 = (bf16[128,128]{1,0:T(8,128)(2,1)S(1)}, bf16[128,128]{1,0:T(8,128)(2,1)S(1)}, u32[]{:S(2)}, u32[]{:S(2)}) collective-permute-start(bf16[128,128]{1,0:T(8,128)(2,1)S(1)} %pair_sum.1.refs_0_), channel_id=1, source_target_pairs={{0,4},{1,5},{2,6},{3,7},{4,0},{5,1},{6,2},{7,3},{8,12},{9,13},{10,... | collective-permute-start | bytes 98312 | tf_op jit(solution)/shard_map/ppermute | solution.py:572
  29.0 1.4 %collective-permute-start.6 = (bf16[128,128]{1,0:T(8,128)(2,1)S(1)}, bf16[128,128]{1,0:T(8,128)(2,1)S(1)}, u32[]{:S(2)}, u32[]{:S(2)}) collective-permute-start(bf16[128,128]{1,0:T(8,128)(2,1)S(1)} %pair_sum.1.refs_0_), channel_id=1, source_target_pairs={{0,6},{1,7},{2,0},{3,1},{4,2},{5,3},{6,4},{7,5},{8,14},{9,15},{10,... | collective-permute-start | bytes 98312 | tf_op jit(solution)/shard_map/ppermute | solution.py:572
  30.4 0.0 collective-permute-done.from_pair
  30.5 0.0 collective-permute-done.1.from_other
  30.5 0.0 slice-done
  30.5 0.0 slice-done.1
  30.5 0.0 slice-done.2
  30.5 0.0 slice-done.3
  30.5 3.1 %edge.1 = (f32[11,256,128]{2,1,0:T(8,128)S(1)}, f32[32,1,128]{2,1,0:T(1,128)S(1)}, bf16[48,256,128]{2,1,0:T(8,128)(2,1)S(1)}) custom-call(s32[8,32]{1,0:T(8,128)} %bitcast.7, bf16[48,256,128]{2,1,0:T(8,128)(2,1)S(1)} %get-tuple-element.24.window.window_in, bf16[8,256,128]{2,1,0:T(8,128)(2,1)} %collective-permute-done.from_pair, ...), custom_call_target="tpu_custom_call", output_to_operand_aliasing={{2}: (1, {})} | custom-call | tf_op jit(solution)/shard_map/edge/pallas_call | solution.py:436
  33.6 2.9 %collective-permute-start.3 = (f32[32,1,128]{2,1,0:T(1,128)S(1)}, f32[32,1,128]{2,1,0:T(1,128)S(1)}, u32[]{:S(2)}, u32[]{:S(2)}) collective-permute-start(f32[32,1,128]{2,1,0:T(1,128)S(1)} %get-tuple-element.40), channel_id=1, source_target_pairs={{0,8},{8,16},{16,24},{24,32},{32,40},{40,48},{48,56},{56,64},{64,7... | collective-permute-start | bytes 49160 | tf_op jit(solution)/shard_map/ppermute | solution.py:577
  36.5 2.7 %rest.1 = (f32[21,256,128]{2,1,0:T(8,128)S(1)}, bf16[16,128,256]{2,1,0:T(8,128)(2,1)S(1)}) custom-call(s32[8,32]{1,0:T(8,128)} %bitcast.8, bf16[48,256,128]{2,1,0:T(8,128)(2,1)S(1)} %get-tuple-element.36.window, bf16[2,32,8,128,128]{4,3,2,1,0:T(8,128)(2,1)S(1)} %bitcast.5, f32[8,256,128]{2,1,0:T(8,128)} %get-tuple-element.37.inner, ...), custom_call_target="tpu_custom_call" | custom-call | tf_op jit(solution)/shard_map/rest/pallas_call | solution.py:481
  39.2 0.0 collective-permute-done.4.refs_1_
  39.2 0.0 collective-permute-done.5.refs_2_
  39.2 0.0 collective-permute-done.6.refs_3_
  39.2 2.1 %collective-permute-done.3.carry = f32[32,1,128]{2,1,0:T(1,128)S(1)} collective-permute-done((f32[32,1,128]{2,1,0:T(1,128)S(1)}, f32[32,1,128]{2,1,0:T(1,128)S(1)}, u32[]{:S(2)}, u32[]{:S(2)}) %collective-permute-start.3) | collective-permute-done | bytes 16416 | tf_op jit(solution)/shard_map/ppermute | solution.py:577
  41.4 2.6 %final.1 = bf16[256,32,128]{2,1,0:T(8,128)(2,1)} custom-call(f32[11,256,128]{2,1,0:T(8,128)S(1)} %get-tuple-element.35.edge, f32[21,256,128]{2,1,0:T(8,128)S(1)} %get-tuple-element.39.rest, f32[32,1,128]{2,1,0:T(1,128)S(1)} %collective-permute-done.3.carry, bf16[128,128]{1,0:T(8,128)(2,1)S(1)} %pair_sum.1.refs_0_, ...), custom_call_target="tpu_custom_call" | custom-call | tf_op jit(solution)/shard_map/final/pallas_call | solution.py:543
  (2 shorter events, 0.0 us)
Async XLA Ops:
  3.2 19.9 %all-to-all-start = ((f32[32,1,128]{2,1,0:T(1,128)}), f32[32,1,128]{2,1,0:T(1,128)S(1)}, u32[]{:S(2)}, u32[]{:S(2)}) async-start(f32[32,1,128]{2,1,0:T(1,128)} %get-tuple-element.27), calls=%async_computation | async-start | bytes 32768 | tf_op jit(solution)/shard_map/all_to_all | solution.py:559
  14.6 15.8 %collective-permute-start = (bf16[8,256,128]{2,1,0:T(8,128)(2,1)}, bf16[8,256,128]{2,1,0:T(8,128)(2,1)}, u32[]{:S(2)}, u32[]{:S(2)}) collective-permute-start(bf16[8,256,128]{2,1,0:T(8,128)(2,1)} %get-tuple-element.25), channel_id=1, source_target_pairs={{0,1},{1,0},{2,3},{3,2},{4,5},{5,4},{6,7},{7,6},{8,9},{9,8},{10,11... | collective-permute-start | bytes 1572872 | tf_op jit(solution)/shard_map/ppermute | solution.py:567
  14.7 15.7 %collective-permute-start.1 = (bf16[8,256,128]{2,1,0:T(8,128)(2,1)}, bf16[8,256,128]{2,1,0:T(8,128)(2,1)}, u32[]{:S(2)}, u32[]{:S(2)}) collective-permute-start(bf16[8,256,128]{2,1,0:T(8,128)(2,1)} %get-tuple-element.26), channel_id=1, source_target_pairs={{1,2},{2,1},{3,4},{4,3},{5,6},{6,5},{9,10},{10,9},{11,12},{12,11},... | collective-permute-start | bytes 1572872 | tf_op jit(solution)/shard_map/ppermute | solution.py:567
  23.2 7.3 %slice-start = ((s8[16777216]{0:T(1024)(128)(4,1)}), s8[4194304]{0:T(1024)(128)(4,1)S(1)}, s32[]{:S(2)}) async-start(s8[16777216]{0:T(1024)(128)(4,1)} %bitcast.4), calls=%async_computation.1 | async-start | bytes 8388608
  23.2 7.3 %slice-start.1 = ((s8[16777216]{0:T(1024)(128)(4,1)}), s8[4194304]{0:T(1024)(128)(4,1)S(1)}, s32[]{:S(2)}) async-start(s8[16777216]{0:T(1024)(128)(4,1)} %bitcast.4), calls=%async_computation.2 | async-start | bytes 8388608
  23.2 7.3 %slice-start.2 = ((s8[16777216]{0:T(1024)(128)(4,1)}), s8[4194304]{0:T(1024)(128)(4,1)S(1)}, s32[]{:S(2)}) async-start(s8[16777216]{0:T(1024)(128)(4,1)} %bitcast.4), calls=%async_computation.3 | async-start | bytes 8388608
  23.2 7.3 %slice-start.3 = ((s8[16777216]{0:T(1024)(128)(4,1)}), s8[4194304]{0:T(1024)(128)(4,1)S(1)}, s32[]{:S(2)}) async-start(s8[16777216]{0:T(1024)(128)(4,1)} %bitcast.4), calls=%async_computation.4 | async-start | bytes 8388608
  23.4 1.3 %collective-permute-start.2 = (f32[128,128]{1,0:T(8,128)S(1)}, f32[128,128]{1,0:T(8,128)S(1)}, u32[]{:S(2)}, u32[]{:S(2)}) collective-permute-start(f32[128,128]{1,0:T(8,128)S(1)} %arrive.1.a), channel_id=1, source_target_pairs={{0,1},{1,0},{2,3},{3,2},{4,5},{5,4},{6,7},{7,6},{8,9},{9,8},{10,11... | collective-permute-start | bytes 196616 | tf_op jit(solution)/shard_map/ppermute | solution.py:567
  24.7 14.5 %collective-permute-start.4 = (bf16[128,128]{1,0:T(8,128)(2,1)S(1)}, bf16[128,128]{1,0:T(8,128)(2,1)S(1)}, u32[]{:S(2)}, u32[]{:S(2)}) collective-permute-start(bf16[128,128]{1,0:T(8,128)(2,1)S(1)} %pair_sum.1.refs_0_), channel_id=1, source_target_pairs={{0,2},{1,3},{2,4},{3,5},{4,6},{5,7},{6,0},{7,1},{8,10},{9,11},{10,... | collective-permute-start | bytes 98312 | tf_op jit(solution)/shard_map/ppermute | solution.py:572
  26.3 12.9 %collective-permute-start.5 = (bf16[128,128]{1,0:T(8,128)(2,1)S(1)}, bf16[128,128]{1,0:T(8,128)(2,1)S(1)}, u32[]{:S(2)}, u32[]{:S(2)}) collective-permute-start(bf16[128,128]{1,0:T(8,128)(2,1)S(1)} %pair_sum.1.refs_0_), channel_id=1, source_target_pairs={{0,4},{1,5},{2,6},{3,7},{4,0},{5,1},{6,2},{7,3},{8,12},{9,13},{10,... | collective-permute-start | bytes 98312 | tf_op jit(solution)/shard_map/ppermute | solution.py:572
  29.0 10.2 %collective-permute-start.6 = (bf16[128,128]{1,0:T(8,128)(2,1)S(1)}, bf16[128,128]{1,0:T(8,128)(2,1)S(1)}, u32[]{:S(2)}, u32[]{:S(2)}) collective-permute-start(bf16[128,128]{1,0:T(8,128)(2,1)S(1)} %pair_sum.1.refs_0_), channel_id=1, source_target_pairs={{0,6},{1,7},{2,0},{3,1},{4,2},{5,3},{6,4},{7,5},{8,14},{9,15},{10,... | collective-permute-start | bytes 98312 | tf_op jit(solution)/shard_map/ppermute | solution.py:572
  33.6 7.7 %collective-permute-start.3 = (f32[32,1,128]{2,1,0:T(1,128)S(1)}, f32[32,1,128]{2,1,0:T(1,128)S(1)}, u32[]{:S(2)}, u32[]{:S(2)}) collective-permute-start(f32[32,1,128]{2,1,0:T(1,128)S(1)} %get-tuple-element.40), channel_id=1, source_target_pairs={{0,8},{8,16},{16,24},{24,32},{32,40},{40,48},{48,56},{56,64},{64,7... | collective-permute-start | bytes 49160 | tf_op jit(solution)/shard_map/ppermute | solution.py:577

commit v9 on v8

--- a/solution.py
+++ b/solution.py
@@ -608,7 +608,7 @@
     parts = [mine] + [from_chip(mine, "space", d) for d in range(1, chips)]
     inner_carry, mine = lax.optimization_barrier((inner_carry, mine))
     later = clusters_of(later)
-    early, others = later[:3], later[3:] + high
+    early, others = (), later + high
     edge, carry, window = edge_near(
         neighbours, window, from_pair, from_other, near_blocks, inner_carry, early, low, high
     )

time: 44.3 us -> 43.9 us (level)
  no operation moved by 1% of the time
where the time goes in v9:
time: 43.9 us; the launch traced here: 43.6 us
  starting transfers between devices  21.7 us (49%)
  Pallas kernels  16.9 us (38%)
  waiting for transfers between devices  4.86 us (11%)
    all_to_all x1, starting transfers between devices, exchanged(): return lax.all_to_all(x, axis, split_axis=0, concat_axis=0, tiled=True)  11.4 us
    ppermute x3, starting transfers between devices, from_chip(): lax.ppermute(x, axis, [(i, (i + 2 * distance) % count) for i in range(cou...  5.73 us
    pallas_call x1, Pallas kernels, inner_near(): pl.pallas_call(functools.partial(inner_kernel, groups, later_groups), in_...  5.01 us
    pallas_call x1, Pallas kernels, prep(): pl.pallas_call(prep_kernel, in_specs=[HBM] * 5, out_specs=[VMEM, HBM, HBM...  3.23 us
    pallas_call x1, Pallas kernels, rest_near(): pl.pallas_call(functools.partial(rest_kernel, order), in_specs=[HBM, VMEM...  3.09 us
    ppermute x1, starting transfers between devices, passed_on(): return lax.ppermute(x, axis, [(i, i + 1) for i in range(count - 1)])  2.85 us
    pallas_call x1, Pallas kernels, edge_near(): pl.pallas_call(functools.partial(edge_kernel, early, order, ends_only), i...  2.77 us
    pallas_call x1, Pallas kernels, final(): pl.pallas_call(functools.partial(final_kernel, places), in_specs=[VMEM] *...  2.62 us
  transfers between devices with their start and end apart: 8, of which 3 were waited for; matrix products, arithmetic and copies ran while one was open for 0% of the time, Pallas kernels for 25%

profile of v9, /device:TPU:32, one launch (start us, length us, event | category | flops | bytes accessed | tf_op | source)
XLA Modules:
  0.0 43.6 jit_solution(3691572763191146010)
XLA Ops:
  0.0 3.2 %prep.1 = (bf16[48,256,128]{2,1,0:T(8,128)(2,1)S(1)}, bf16[8,256,128]{2,1,0:T(8,128)(2,1)}, bf16[8,256,128]{2,1,0:T(8,128)(2,1)}, f32[256,128]{1,0:T(8,128)S(1)}...) custom-call(bf16[256,32,128]{2,1,0:T(8,128)(2,1)} %density.1, s32[1,256]{1,0:T(1,128)} %bitcast.9, ...), custom_call_target="tpu_custom_call" | custom-call | tf_op jit(solution)/shard_map/prep/pallas_call | solution.py:158
  3.2 11.4 %all-to-all-start = ((f32[32,1,128]{2,1,0:T(1,128)}), f32[32,1,128]{2,1,0:T(1,128)S(1)}, u32[]{:S(2)}, u32[]{:S(2)}) async-start(f32[32,1,128]{2,1,0:T(1,128)} %get-tuple-element.27), calls=%async_computation | async-start | bytes 32768 | tf_op jit(solution)/shard_map/all_to_all | solution.py:559
  14.6 0.1 collective-permute-start
  14.7 1.5 %collective-permute-start.1 = (bf16[8,256,128]{2,1,0:T(8,128)(2,1)}, bf16[8,256,128]{2,1,0:T(8,128)(2,1)}, u32[]{:S(2)}, u32[]{:S(2)}) collective-permute-start(bf16[8,256,128]{2,1,0:T(8,128)(2,1)} %get-tuple-element.26), channel_id=1, source_target_pairs={{1,2},{2,1},{3,4},{4,3},{5,6},{6,5},{9,10},{10,9},{11,12},{12,11},... | collective-permute-start | bytes 1572872 | tf_op jit(solution)/shard_map/ppermute | solution.py:567
  16.2 5.0 %inner.1 = (f32[8,256,128]{2,1,0:T(8,128)}, f32[16,1,128]{2,1,0:T(1,128)}, bf16[16,128,256]{2,1,0:T(8,128)(2,1)}) custom-call(s32[8,32]{1,0:T(8,128)} %bitcast.6, bf16[48,256,128]{2,1,0:T(8,128)(2,1)S(1)} %get-tuple-element.24.window.window_in, bf16[2,32,8,128,128]{4,3,2,1,0:T(8,128)(2,1)} %blocks.5, bf16[64,32,128]{2,1,0:T(8,128)(2,1)} %from_moments.1), custom_call_target="tpu_custom_call" | custom-call | tf_op jit(solution)/shard_map/inner/pallas_call | solution.py:354
  21.2 2.0 %all-to-all-done.ends = f32[32,1,128]{2,1,0:T(1,128)S(1)} async-done(((f32[32,1,128]{2,1,0:T(1,128)}), f32[32,1,128]{2,1,0:T(1,128)S(1)}, u32[]{:S(2)}, u32[]{:S(2)}) %all-to-all-start) | async-done | bytes 16416 | tf_op jit(solution)/shard_map/all_to_all | solution.py:559
  23.2 0.0 slice-start
  23.2 0.0 slice-start.1
  23.2 0.0 slice-start.2
  23.2 0.0 slice-start.3
  23.2 0.2 arrive.1.a
  23.4 0.2 collective-permute-start.2
  23.6 1.1 %collective-permute-done.2.b = f32[128,128]{1,0:T(8,128)S(1)} collective-permute-done((f32[128,128]{1,0:T(8,128)S(1)}, f32[128,128]{1,0:T(8,128)S(1)}, u32[]{:S(2)}, u32[]{:S(2)}) %collective-permute-start.2) | collective-permute-done | bytes 65568 | tf_op jit(solution)/shard_map/ppermute | solution.py:567
  24.7 1.6 %collective-permute-start.4 = (bf16[128,128]{1,0:T(8,128)(2,1)S(1)}, bf16[128,128]{1,0:T(8,128)(2,1)S(1)}, u32[]{:S(2)}, u32[]{:S(2)}) collective-permute-start(bf16[128,128]{1,0:T(8,128)(2,1)S(1)} %pair_sum.1.refs_0_), channel_id=1, source_target_pairs={{0,2},{1,3},{2,4},{3,5},{4,6},{5,7},{6,0},{7,1},{8,10},{9,11},{10,... | collective-permute-start | bytes 98312 | tf_op jit(solution)/shard_map/ppermute | solution.py:572
  26.3 2.7 %collective-permute-start.5 = (bf16[128,128]{1,0:T(8,128)(2,1)S(1)}, bf16[128,128]{1,0:T(8,128)(2,1)S(1)}, u32[]{:S(2)}, u32[]{:S(2)}) collective-permute-start(bf16[128,128]{1,0:T(8,128)(2,1)S(1)} %pair_sum.1.refs_0_), channel_id=1, source_target_pairs={{0,4},{1,5},{2,6},{3,7},{4,0},{5,1},{6,2},{7,3},{8,12},{9,13},{10,... | collective-permute-start | bytes 98312 | tf_op jit(solution)/shard_map/ppermute | solution.py:572
  29.0 1.4 %collective-permute-start.6 = (bf16[128,128]{1,0:T(8,128)(2,1)S(1)}, bf16[128,128]{1,0:T(8,128)(2,1)S(1)}, u32[]{:S(2)}, u32[]{:S(2)}) collective-permute-start(bf16[128,128]{1,0:T(8,128)(2,1)S(1)} %pair_sum.1.refs_0_), channel_id=1, source_target_pairs={{0,6},{1,7},{2,0},{3,1},{4,2},{5,3},{6,4},{7,5},{8,14},{9,15},{10,... | collective-permute-start | bytes 98312 | tf_op jit(solution)/shard_map/ppermute | solution.py:572
  30.4 0.0 collective-permute-done.from_pair
  30.5 0.0 collective-permute-done.1.from_other
  30.5 0.0 slice-done
  30.5 0.0 slice-done.1
  30.5 0.0 slice-done.2
  30.5 0.0 slice-done.3
  30.5 2.8 %edge.1 = (f32[8,256,128]{2,1,0:T(8,128)S(1)}, f32[32,1,128]{2,1,0:T(1,128)S(1)}, bf16[48,256,128]{2,1,0:T(8,128)(2,1)S(1)}) custom-call(s32[8,32]{1,0:T(8,128)} %bitcast.7, bf16[48,256,128]{2,1,0:T(8,128)(2,1)S(1)} %get-tuple-element.24.window.window_in, bf16[8,256,128]{2,1,0:T(8,128)(2,1)} %collective-permute-done.from_pair, ...), custom_call_target="tpu_custom_call", output_to_operand_aliasing={{2}: (1, {})} | custom-call | tf_op jit(solution)/shard_map/edge/pallas_call | solution.py:436
  33.3 2.9 %collective-permute-start.3 = (f32[32,1,128]{2,1,0:T(1,128)S(1)}, f32[32,1,128]{2,1,0:T(1,128)S(1)}, u32[]{:S(2)}, u32[]{:S(2)}) collective-permute-start(f32[32,1,128]{2,1,0:T(1,128)S(1)} %get-tuple-element.40), channel_id=1, source_target_pairs={{0,8},{8,16},{16,24},{24,32},{32,40},{40,48},{48,56},{56,64},{64,7... | collective-permute-start | bytes 49160 | tf_op jit(solution)/shard_map/ppermute | solution.py:577
  36.1 3.1 %rest.1 = (f32[24,256,128]{2,1,0:T(8,128)S(1)}, bf16[16,128,256]{2,1,0:T(8,128)(2,1)S(1)}) custom-call(s32[8,32]{1,0:T(8,128)} %bitcast.8, bf16[48,256,128]{2,1,0:T(8,128)(2,1)S(1)} %get-tuple-element.36.window, bf16[2,32,8,128,128]{4,3,2,1,0:T(8,128)(2,1)S(1)} %bitcast.5, f32[8,256,128]{2,1,0:T(8,128)} %get-tuple-element.37.inner, ...), custom_call_target="tpu_custom_call" | custom-call | tf_op jit(solution)/shard_map/rest/pallas_call | solution.py:481
  39.2 0.0 collective-permute-done.4.refs_1_
  39.3 0.0 collective-permute-done.5.refs_2_
  39.3 0.0 collective-permute-done.6.refs_3_
  39.3 1.7 %collective-permute-done.3.carry = f32[32,1,128]{2,1,0:T(1,128)S(1)} collective-permute-done((f32[32,1,128]{2,1,0:T(1,128)S(1)}, f32[32,1,128]{2,1,0:T(1,128)S(1)}, u32[]{:S(2)}, u32[]{:S(2)}) %collective-permute-start.3) | collective-permute-done | bytes 16416 | tf_op jit(solution)/shard_map/ppermute | solution.py:577
  41.0 2.6 %final.1 = bf16[256,32,128]{2,1,0:T(8,128)(2,1)} custom-call(f32[8,256,128]{2,1,0:T(8,128)S(1)} %get-tuple-element.35.edge, f32[24,256,128]{2,1,0:T(8,128)S(1)} %get-tuple-element.39.rest, f32[32,1,128]{2,1,0:T(1,128)S(1)} %collective-permute-done.3.carry, bf16[128,128]{1,0:T(8,128)(2,1)S(1)} %pair_sum.1.refs_0_, ...), custom_call_target="tpu_custom_call" | custom-call | tf_op jit(solution)/shard_map/final/pallas_call | solution.py:543
  (2 shorter events, 0.0 us)
Async XLA Ops:
  3.2 19.9 %all-to-all-start = ((f32[32,1,128]{2,1,0:T(1,128)}), f32[32,1,128]{2,1,0:T(1,128)S(1)}, u32[]{:S(2)}, u32[]{:S(2)}) async-start(f32[32,1,128]{2,1,0:T(1,128)} %get-tuple-element.27), calls=%async_computation | async-start | bytes 32768 | tf_op jit(solution)/shard_map/all_to_all | solution.py:559
  14.6 15.8 %collective-permute-start = (bf16[8,256,128]{2,1,0:T(8,128)(2,1)}, bf16[8,256,128]{2,1,0:T(8,128)(2,1)}, u32[]{:S(2)}, u32[]{:S(2)}) collective-permute-start(bf16[8,256,128]{2,1,0:T(8,128)(2,1)} %get-tuple-element.25), channel_id=1, source_target_pairs={{0,1},{1,0},{2,3},{3,2},{4,5},{5,4},{6,7},{7,6},{8,9},{9,8},{10,11... | collective-permute-start | bytes 1572872 | tf_op jit(solution)/shard_map/ppermute | solution.py:567
  14.7 15.7 %collective-permute-start.1 = (bf16[8,256,128]{2,1,0:T(8,128)(2,1)}, bf16[8,256,128]{2,1,0:T(8,128)(2,1)}, u32[]{:S(2)}, u32[]{:S(2)}) collective-permute-start(bf16[8,256,128]{2,1,0:T(8,128)(2,1)} %get-tuple-element.26), channel_id=1, source_target_pairs={{1,2},{2,1},{3,4},{4,3},{5,6},{6,5},{9,10},{10,9},{11,12},{12,11},... | collective-permute-start | bytes 1572872 | tf_op jit(solution)/shard_map/ppermute | solution.py:567
  23.2 7.3 %slice-start = ((s8[16777216]{0:T(1024)(128)(4,1)}), s8[4194304]{0:T(1024)(128)(4,1)S(1)}, s32[]{:S(2)}) async-start(s8[16777216]{0:T(1024)(128)(4,1)} %bitcast.4), calls=%async_computation.1 | async-start | bytes 8388608
  23.2 7.3 %slice-start.1 = ((s8[16777216]{0:T(1024)(128)(4,1)}), s8[4194304]{0:T(1024)(128)(4,1)S(1)}, s32[]{:S(2)}) async-start(s8[16777216]{0:T(1024)(128)(4,1)} %bitcast.4), calls=%async_computation.2 | async-start | bytes 8388608
  23.2 7.3 %slice-start.2 = ((s8[16777216]{0:T(1024)(128)(4,1)}), s8[4194304]{0:T(1024)(128)(4,1)S(1)}, s32[]{:S(2)}) async-start(s8[16777216]{0:T(1024)(128)(4,1)} %bitcast.4), calls=%async_computation.3 | async-start | bytes 8388608
  23.2 7.3 %slice-start.3 = ((s8[16777216]{0:T(1024)(128)(4,1)}), s8[4194304]{0:T(1024)(128)(4,1)S(1)}, s32[]{:S(2)}) async-start(s8[16777216]{0:T(1024)(128)(4,1)} %bitcast.4), calls=%async_computation.4 | async-start | bytes 8388608
  23.4 1.3 %collective-permute-start.2 = (f32[128,128]{1,0:T(8,128)S(1)}, f32[128,128]{1,0:T(8,128)S(1)}, u32[]{:S(2)}, u32[]{:S(2)}) collective-permute-start(f32[128,128]{1,0:T(8,128)S(1)} %arrive.1.a), channel_id=1, source_target_pairs={{0,1},{1,0},{2,3},{3,2},{4,5},{5,4},{6,7},{7,6},{8,9},{9,8},{10,11... | collective-permute-start | bytes 196616 | tf_op jit(solution)/shard_map/ppermute | solution.py:567
  24.7 14.5 %collective-permute-start.4 = (bf16[128,128]{1,0:T(8,128)(2,1)S(1)}, bf16[128,128]{1,0:T(8,128)(2,1)S(1)}, u32[]{:S(2)}, u32[]{:S(2)}) collective-permute-start(bf16[128,128]{1,0:T(8,128)(2,1)S(1)} %pair_sum.1.refs_0_), channel_id=1, source_target_pairs={{0,2},{1,3},{2,4},{3,5},{4,6},{5,7},{6,0},{7,1},{8,10},{9,11},{10,... | collective-permute-start | bytes 98312 | tf_op jit(solution)/shard_map/ppermute | solution.py:572
  26.3 13.0 %collective-permute-start.5 = (bf16[128,128]{1,0:T(8,128)(2,1)S(1)}, bf16[128,128]{1,0:T(8,128)(2,1)S(1)}, u32[]{:S(2)}, u32[]{:S(2)}) collective-permute-start(bf16[128,128]{1,0:T(8,128)(2,1)S(1)} %pair_sum.1.refs_0_), channel_id=1, source_target_pairs={{0,4},{1,5},{2,6},{3,7},{4,0},{5,1},{6,2},{7,3},{8,12},{9,13},{10,... | collective-permute-start | bytes 98312 | tf_op jit(solution)/shard_map/ppermute | solution.py:572
  29.0 10.3 %collective-permute-start.6 = (bf16[128,128]{1,0:T(8,128)(2,1)S(1)}, bf16[128,128]{1,0:T(8,128)(2,1)S(1)}, u32[]{:S(2)}, u32[]{:S(2)}) collective-permute-start(bf16[128,128]{1,0:T(8,128)(2,1)S(1)} %pair_sum.1.refs_0_), channel_id=1, source_target_pairs={{0,6},{1,7},{2,0},{3,1},{4,2},{5,3},{6,4},{7,5},{8,14},{9,15},{10,... | collective-permute-start | bytes 98312 | tf_op jit(solution)/shard_map/ppermute | solution.py:572
  33.3 7.7 %collective-permute-start.3 = (f32[32,1,128]{2,1,0:T(1,128)S(1)}, f32[32,1,128]{2,1,0:T(1,128)S(1)}, u32[]{:S(2)}, u32[]{:S(2)}) collective-permute-start(f32[32,1,128]{2,1,0:T(1,128)S(1)} %get-tuple-element.40), channel_id=1, source_target_pairs={{0,8},{8,16},{16,24},{24,32},{32,40},{40,48},{48,56},{56,64},{64,7... | collective-permute-start | bytes 49160 | tf_op jit(solution)/shard_map/ppermute | solution.py:577
